TPU v7x, 128 devices: a whole 4x4x4 slice. The times are simulated.
128 devices in a mesh: band: 64 (over y, x, z), mp: 2 (over core).
Axes of the slice: x: 4, y: 4, z: 4, core: 2. Of those that a mesh axis runs over, the one named last changes fastest.
Arguments:
- grid_nodes: bfloat16 [262144, 512], P('band', 'mp'), may hold values from -6 to 6
- mesh_nodes: bfloat16 [32768, 512], P('band', 'mp'), may hold values from -6 to 6
- send_weight: bfloat16 [512, 512], P(None, 'mp'), may hold values from -0.25 to 0.25
- self_weight: bfloat16 [512, 512], P(None, 'mp'), may hold values from -0.25 to 0.25
- pooled_weight: bfloat16 [512, 512], P(None, 'mp'), may hold values from -0.25 to 0.25
- out_weight: bfloat16 [512, 2, 512], P('mp'), may hold values from -0.25 to 0.25
- encode_source: int32 [12288], P('band'), may hold values from 0 to 31
- encode_slot: int32 [12288], P('band'), may hold values from 0 to 63
- encode_tiles: bfloat16 [12288, 128, 128], P('band'), may hold values from -0.078125 to 0.078125
- slot_block: int32 [64, 64], P('band'), may hold values from 0 to 3
- decode_slot: int32 [12288], P('band'), may hold values from 0 to 63
- decode_target: int32 [12288], P('band'), may hold values from 0 to 31
- decode_tiles: bfloat16 [12288, 128, 128], P('band'), may hold values from -0.21875 to 0.21875
Outputs:
- grid_state: bfloat16 [262144, 512], P('band', 'mp')
- mesh_state: bfloat16 [32768, 512], P('band', 'mp')
All inputs are finite; a program needn't handle non-finite values.
Results may differ from a plain program's by a relative error of at most 0.005.
Values may be sent and summed in bfloat16 or wider, within the bound.
No kernel may reach another device: no remote copies, remote signals or barrier semaphores. Data moves between devices by JAX's collectives and lax.ppermute only.
A program may use at most 192 MiB of HBM per device.

v0:
```python
import jax
import jax.numpy as jnp
from jax import lax
from jax.sharding import PartitionSpec as P


def cut_along(shard, dim, count):
    before, after = (shard.shape[:dim], shard.shape[dim + 1 :])
    return jnp.moveaxis(shard.reshape(*before, count, -1, *after), dim, 0)


def cut_rows(length, count):
    step = length // count
    if step >= 8:
        step -= step % 8
    return [step * k for k in range(1, count)]


def in_order(tiles, dim):
    tiles = jnp.moveaxis(tiles, 0, dim)
    dims = tiles.shape
    return tiles.reshape(*dims[:dim], dims[dim] * dims[dim + 1], *dims[dim + 2 :])


def several_exchanges(shard, axis, pieces, split_dim, concat_dim):
    tiles = cut_along(shard, split_dim, lax.axis_size(axis))
    widest = max(range(1, max(2, tiles.ndim - 1)), key=lambda d: tiles.shape[d])
    gathered = []
    for slab in jnp.split(tiles, cut_rows(tiles.shape[widest], pieces), axis=widest):
        if slab.size:
            gathered.append(lax.all_to_all(slab, axis, split_axis=0, concat_axis=0, tiled=True))
    return in_order(jnp.concatenate(gathered, axis=widest), concat_dim)


def sent_to_all(shard, axis):
    count = lax.axis_size(axis)
    return lax.all_to_all(
        jnp.broadcast_to(shard[None], (count, *shard.shape)), axis, 0, 0, tiled=True
    )


def collect(shard, axis, dim):
    return in_order(sent_to_all(shard, axis), dim)


def in_one_piece(arrays, axis, dim, along):
    widths = [a.shape[along] for a in arrays]
    both = jnp.concatenate(arrays, axis=along)
    out = collect(both, axis, dim)
    return tuple(jnp.split(out, [sum(widths[:k]) for k in range(1, len(widths))], axis=along))


def per_device(
    grid_nodes,
    mesh_nodes,
    send_weight,
    self_weight,
    pooled_weight,
    out_weight,
    encode_source,
    encode_slot,
    encode_tiles,
    slot_block,
    decode_slot,
    decode_target,
    decode_tiles,
):
    band_count = lax.axis_size("band")
    tile_edge = encode_tiles.shape[1]
    feature_width = grid_nodes.shape[1]
    grid_blocks = grid_nodes.shape[0] // tile_edge
    mesh_blocks = mesh_nodes.shape[0] // tile_edge
    full_grid = lax.all_gather(grid_nodes, "mp", axis=1, tiled=True)
    message = jax.nn.silu(
        jnp.dot(full_grid, send_weight, preferred_element_type=jnp.float32)
    ).astype(jnp.bfloat16)
    message_blocks = message.reshape(grid_blocks, tile_edge, feature_width)
    sources = jnp.take(message_blocks, encode_source, axis=0)
    partials = jnp.einsum("eij,ejc->eic", encode_tiles, sources, preferred_element_type=jnp.float32)
    slot_sums = jax.ops.segment_sum(partials, encode_slot, num_segments=band_count)
    arrived, owner_block = (
        several_exchanges(slot_sums, "band", 2, 0, 0),
        several_exchanges(slot_block[0], "band", 2, 0, 0),
    )
    selector = (owner_block[None, :] == jnp.arange(mesh_blocks, dtype=jnp.int32)[:, None]).astype(
        jnp.float32
    )
    aggregate = jnp.einsum("bs,sic->bic", selector, arrived, precision=lax.Precision.HIGHEST)
    pooled = aggregate.reshape(-1, feature_width).astype(jnp.bfloat16)
    mesh_full, pooled_full = in_one_piece((mesh_nodes, pooled), "mp", 1, 0)
    inner_sum = jnp.dot(mesh_full, self_weight, preferred_element_type=jnp.float32) + jnp.dot(
        pooled_full, pooled_weight, preferred_element_type=jnp.float32
    )
    hidden = jax.nn.silu(inner_sum).astype(jnp.bfloat16)
    partial_out = jnp.dot(
        hidden, out_weight.reshape(hidden.shape[1], -1), preferred_element_type=jnp.float32
    )
    partial_out = partial_out.reshape(hidden.shape[0], 2, -1)
    reduced = lax.psum_scatter(partial_out, "mp", scatter_dimension=2, tiled=True)
    mesh_state = (mesh_nodes.astype(jnp.float32) + reduced[:, 0, :]).astype(jnp.bfloat16)
    decode_source = (
        reduced[:, 1, :].astype(jnp.bfloat16).reshape(mesh_blocks, tile_edge, feature_width)
    )
    outgoing = jnp.take(decode_source, owner_block, axis=0)
    returned = lax.all_to_all(outgoing, "band", split_axis=0, concat_axis=0, tiled=True)
    picked = jnp.take(returned, decode_slot, axis=0)
    contribution = jnp.einsum(
        "eij,ejc->eic", decode_tiles, picked, preferred_element_type=jnp.float32
    )
    grid_sum = jax.ops.segment_sum(contribution, decode_target, num_segments=grid_blocks)
    grid_state = (grid_nodes.astype(jnp.float32) + grid_sum.reshape(-1, feature_width)).astype(
        jnp.bfloat16
    )
    return (grid_state, mesh_state)


def solution(mesh):
    return jax.shard_map(
        per_device,
        mesh=mesh,
        in_specs=(
            P("band", "mp"),
            P("band", "mp"),
            P(None, "mp"),
            P(None, "mp"),
            P(None, "mp"),
            P("mp", None, None),
            P("band"),
            P("band"),
            P("band", None, None),
            P("band", None),
            P("band"),
            P("band"),
            P("band", None, None),
        ),
        out_specs=(P("band", "mp"), P("band", "mp")),
        check_vma=False,
    )
```

profile of v0, /device:TPU:0, one launch (start us, length us, event | category | flops | bytes accessed | tf_op | source)
XLA Modules:
  0.0 490.1 jit_solution(7685467857731626918)
XLA Ops:
  9.3 11.5 %all-to-all-start = ((s32[64,1,1]{2,1,0:T(1,128)}), s32[64,1,1]{2,1,0:T(1,128)S(1)}, u32[]{:S(2)}, u32[]{:S(2)}) async-start(s32[64,1,1]{2,1,0:T(1,128)} %copy.39), calls=%async_computation | async-start | bytes 65536 | tf_op jit(solution)/shard_map/all_to_all | solution.py:31
  22.2 5.4 %all-gather.2.cloned.1.call-done = bf16[4096,512]{1,0:T(8,128)(2,1)} async-done(((bf16[4096,256]{1,0:T(8,128)(2,1)}), bf16[4096,512]{1,0:T(8,128)(2,1)}) %all-gather.2.cloned.1.call-update) | async-done | bytes 4194320 | tf_op jit(solution)/shard_map/all_gather | solution.py:73
  27.6 3.4 multiply_convert_fusion
  31.1 8.2 %gather_fusion = bf16[192,128,256]{2,1,0:T(8,128)(2,1)} fusion(bf16[32,128,256]{2,1,0:T(8,128)(2,1)S(1)} %bitcast.58, s32[1024]{0:T(1024)S(1)} %pad_clamp_fusion.2), kind=kCustom, calls=%fused_computation | custom fusion | bytes 25166592 | tf_op jit(solution)/shard_map/jit(_take)/gather | solution.py:78
  39.3 16.4 %fusion.6 = f32[192,128,256]{1,2,0:T(8,128)} fusion(bf16[192,128,128]{2,1,0:T(8,128)(2,1)} %param.21, bf16[192,128,256]{2,1,0:T(8,128)(2,1)} %gather_fusion, pred[192]{0:T(512)(128)(4,1)S(1)} %compare_and_fusion), kind=kOutput, calls=%fused_computation.11 | convolution fusion | flops 1616904192 | bytes 44040384 | tf_op jit(solution)/shard_map/eij,ejc->eic/dot_general | solution.py:79
  55.7 24.7 %copy.41 = f32[192,128,256]{2,1,0:T(8,128)} copy(f32[192,128,256]{1,2,0:T(8,128)} %fusion.6) | data formatting | bytes 50331648 | tf_op jit(solution)/shard_map/eij,ejc->eic/dot_general | solution.py:79
  80.4 4.3 broadcast_in_dim.55
  84.6 55.8 %scatter_fusion = f32[64,128,256]{2,1,0:T(8,128)} fusion(f32[64,128,256]{2,1,0:T(8,128)} %broadcast_in_dim.55, s32[192]{0:T(256)S(1)} %copy-done.8, f32[192,128,256]{2,1,0:T(8,128)} %copy.41), kind=kCustom, calls=%fused_computation.3 | custom fusion | flops 6291456 | bytes 75498240 | tf_op jit(solution)/shard_map/scatter-add | solution.py:80
  140.4 7.8 %slice_bitcast_fusion.1 = (f32[64,1,64,256]{3,2,1,0:T(8,128)}, f32[64,1,64,256]{3,2,1,0:T(8,128)}) fusion(f32[64,1,128,256]{3,2,0,1:T(8,128)} %bitcast.56), kind=kLoop, calls=%fused_computation.20 | loop fusion | bytes 16777216 | tf_op jit(solution)/shard_map/split | solution.py:29
  148.2 63.2 %all_to_all.35 = f32[64,1,64,256]{3,2,1,0:T(8,128)} all-to-all(f32[64,1,64,256]{3,2,1,0:T(8,128)} %get-tuple-element.2), channel_id=1, replica_groups=mesh['band'=64,'mp'=2] {'band'}, dimensions={0} | all-to-all | bytes 8388608 | tf_op jit(solution)/shard_map/all_to_all | solution.py:31
  211.5 6.2 %all-to-all-start.2 = ((f32[64,1,64,256]{3,2,1,0:T(8,128)}), f32[64,1,64,256]{3,2,1,0:T(8,128)}, u32[]{:S(2)}, u32[]{:S(2)}) async-start(f32[64,1,64,256]{3,2,1,0:T(8,128)} %get-tuple-element.3), calls=%async_computation.2 | async-start | bytes 8388608 | tf_op jit(solution)/shard_map/all_to_all | solution.py:31
  219.4 6.6 %copy.44 = f32[64,1,64,256]{3,0,2,1:T(8,128)} copy(f32[64,1,64,256]{3,2,1,0:T(8,128)} %all_to_all.35) | data formatting | bytes 8388608 | tf_op jit(solution)/shard_map/all_to_all | solution.py:31
  226.0 42.3 %all-to-all-done.2 = f32[64,1,64,256]{3,2,1,0:T(8,128)} async-done(((f32[64,1,64,256]{3,2,1,0:T(8,128)}), f32[64,1,64,256]{3,2,1,0:T(8,128)}, u32[]{:S(2)}, u32[]{:S(2)}) %all-to-all-start.2) | async-done | bytes 4194336 | tf_op jit(solution)/shard_map/all_to_all | solution.py:31
  268.2 4.8 copy.45
  276.3 4.6 all_to_all.36
  283.6 14.2 %reduce-scatter.2.cloned.1.call-done = f32[512,2,256]{2,0,1:T(8,128)} async-done(((f32[512,2,512]{2,0,1:T(8,128)}), f32[512,2,256]{2,0,1:T(8,128)}) %reduce-scatter.2.cloned.1.call-update) | async-done | bytes 1048592 | tf_op jit(solution)/shard_map/reduce_scatter | solution.py:99
  301.6 4.6 broadcast_select_fusion
  306.2 10.8 %all-to-all-start.4 = ((bf16[64,128,256]{2,1,0:T(8,128)(2,1)}), bf16[64,128,256]{2,1,0:T(8,128)(2,1)}, u32[]{:S(2)}, u32[]{:S(2)}) async-start(bf16[64,128,256]{2,1,0:T(8,128)(2,1)} %broadcast_select_fusion), calls=%async_computation.5 | async-start | bytes 8388608 | tf_op jit(solution)/shard_map/all_to_all | solution.py:105
  317.8 50.8 %all-to-all-done.4 = bf16[64,128,256]{2,1,0:T(8,128)(2,1)} async-done(((bf16[64,128,256]{2,1,0:T(8,128)(2,1)}), bf16[64,128,256]{2,1,0:T(8,128)(2,1)}, u32[]{:S(2)}, u32[]{:S(2)}) %all-to-all-start.4) | async-done | bytes 4194336 | tf_op jit(solution)/shard_map/all_to_all | solution.py:105
  368.6 10.4 %gather_fusion.2 = bf16[192,128,256]{2,1,0:T(8,128)(2,1)} fusion(bf16[64,128,256]{2,1,0:T(8,128)(2,1)} %all-to-all-done.4, s32[1024]{0:T(1024)S(1)} %pad_clamp_fusion), kind=kCustom, calls=%fused_computation.2 | custom fusion | bytes 25166592 | tf_op jit(solution)/shard_map/jit(_take)/gather | solution.py:106
  379.0 16.4 %fusion.9 = f32[192,128,256]{1,2,0:T(8,128)} fusion(bf16[192,128,128]{2,1,0:T(8,128)(2,1)} %param.25, bf16[192,128,256]{2,1,0:T(8,128)(2,1)} %gather_fusion.2, pred[192]{0:T(512)(128)(4,1)S(1)} %compare_and_fusion.2), kind=kOutput, calls=%fused_computation.12 | convolution fusion | flops 1616904192 | bytes 44040384 | tf_op jit(solution)/shard_map/eij,ejc->eic/dot_general | solution.py:107
  395.4 24.7 %copy.50 = f32[192,128,256]{2,1,0:T(8,128)} copy(f32[192,128,256]{1,2,0:T(8,128)} %fusion.9) | data formatting | bytes 50331648 | tf_op jit(solution)/shard_map/eij,ejc->eic/dot_general | solution.py:107
  422.5 56.7 %scatter_fusion.1 = f32[32,128,256]{2,1,0:T(8,128)} fusion(f32[32,128,256]{2,1,0:T(8,128)} %broadcast_in_dim.51, s32[192]{0:T(256)S(1)} %copy-done.9, f32[192,128,256]{2,1,0:T(8,128)} %copy.50), kind=kCustom, calls=%fused_computation.4 | custom fusion | flops 6291456 | bytes 75498240 | tf_op jit(solution)/shard_map/scatter-add | solution.py:110
  479.3 4.0 fusion.17
  (54 shorter events, 18.1 us)
Async XLA Ops:
  7.2 20.5 %copy-start = (bf16[512,256]{1,0:T(8,128)(2,1)S(1)}, bf16[512,256]{1,0:T(8,128)(2,1)}, u32[]{:S(2)}) copy-start(bf16[512,256]{1,0:T(8,128)(2,1)} %param.15) | copy-start | bytes 786436
  7.2 20.4 %all-gather.2.cloned.1.call-start = ((), (), s32[]{:S(2)}) async-start(), calls=%async_computation.6 | async-start | bytes 6291456 | tf_op jit(solution)/shard_map/all_gather | solution.py:73
  9.3 139.0 %all-to-all-start = ((s32[64,1,1]{2,1,0:T(1,128)}), s32[64,1,1]{2,1,0:T(1,128)S(1)}, u32[]{:S(2)}, u32[]{:S(2)}) async-start(s32[64,1,1]{2,1,0:T(1,128)} %copy.39), calls=%async_computation | async-start | bytes 65536 | tf_op jit(solution)/shard_map/all_to_all | solution.py:31
  80.4 4.3 copy-start.8
  211.5 6.4 %copy-start.6 = (bf16[256,2,512]{2,1,0:T(2,128)(2,1)S(1)}, bf16[256,2,512]{2,1,0:T(2,128)(2,1)}, u32[]{:S(2)}) copy-start(bf16[256,2,512]{2,1,0:T(2,128)(2,1)} %param.18) | copy-start | bytes 1572868
  211.5 56.8 %all-to-all-start.2 = ((f32[64,1,64,256]{3,2,1,0:T(8,128)}), f32[64,1,64,256]{3,2,1,0:T(8,128)}, u32[]{:S(2)}, u32[]{:S(2)}) async-start(f32[64,1,64,256]{3,2,1,0:T(8,128)} %get-tuple-element.3), calls=%async_computation.2 | async-start | bytes 8388608 | tf_op jit(solution)/shard_map/all_to_all | solution.py:31
  217.7 80.2 %reduce-scatter.2.cloned.1.call-start = ((), (), s32[]{:S(2)}) async-start(), calls=%async_computation.7 | async-start | bytes 3145728 | tf_op jit(solution)/shard_map/reduce_scatter | solution.py:99
  268.2 4.8 copy-start.2
  273.0 2.9 copy-start.4
  275.8 5.1 %copy-start.7 = (bf16[512,256]{1,0:T(8,128)(2,1)S(1)}, bf16[512,256]{1,0:T(8,128)(2,1)}, u32[]{:S(2)}) copy-start(bf16[512,256]{1,0:T(8,128)(2,1)} %param.16) | copy-start | bytes 786436
  275.9 5.4 %copy-start.11 = (bf16[512,256]{1,0:T(8,128)(2,1)S(1)}, bf16[512,256]{1,0:T(8,128)(2,1)}, u32[]{:S(2)}) copy-start(bf16[512,256]{1,0:T(8,128)(2,1)} %param.17) | copy-start | bytes 786436
  306.2 10.8 %copy-start.10 = (s32[192]{0:T(256)S(1)}, s32[192]{0:T(256)}, u32[]{:S(2)}) copy-start(s32[192]{0:T(256)} %param.23) | copy-start | bytes 2308
  306.2 10.9 %copy-start.5 = (f32[512,2,256]{2,0,1:T(8,128)S(1)}, f32[512,2,256]{2,0,1:T(8,128)}, u32[]{:S(2)}) copy-start(f32[512,2,256]{2,0,1:T(8,128)} %reduce-scatter.2.cloned.1.call-done) | copy-start | bytes 3145732
  306.2 62.4 %all-to-all-start.4 = ((bf16[64,128,256]{2,1,0:T(8,128)(2,1)}), bf16[64,128,256]{2,1,0:T(8,128)(2,1)}, u32[]{:S(2)}, u32[]{:S(2)}) async-start(bf16[64,128,256]{2,1,0:T(8,128)(2,1)} %broadcast_select_fusion), calls=%async_computation.5 | async-start | bytes 8388608 | tf_op jit(solution)/shard_map/all_to_all | solution.py:105
  420.1 2.5 copy-start.9
  422.5 56.8 %copy-start.3 = (bf16[4096,256]{1,0:T(8,128)(2,1)S(1)}, bf16[4096,256]{1,0:T(8,128)(2,1)}, u32[]{:S(2)}) copy-start(bf16[4096,256]{1,0:T(8,128)(2,1)} %param.13) | copy-start | bytes 6291460
  422.5 60.7 %copy-start.1 = (bf16[512,256]{1,0:T(8,128)(2,1)S(1)}, bf16[512,256]{1,0:T(8,128)(2,1)}, u32[]{:S(2)}) copy-start(bf16[512,256]{1,0:T(8,128)(2,1)} %param.15) | copy-start | bytes 786436
Sparse Core Ops, SparseCore 0:
  9.6 17.9 all-gather.1
  283.7 14.1 reduce-scatter.1
where the time goes:
time: 495 us; the launch traced here: 490 us
  other arithmetic  125 us (25%)
  waiting for transfers between devices  113 us (23%)
  local copies, waits for them, and re-layouts  99.8 us (20%)
  blocking collectives  67.8 us (14%)
  matrix products  41.5 us (8%)
  starting transfers between devices  28.8 us (6%)
  between operations  14.3 us (3%)
    all_to_all x1, blocking collectives, several_exchanges(): lax.all_to_all(slab, axis, split_axis=0, concat_axis=0, tiled=True)  63.2 us
    scatter-add x1, other arithmetic, per_device(): jax.ops.segment_sum(contribution, decode_target, num_segments=grid_blocks)  56.7 us
    scatter-add x1, other arithmetic, per_device(): jax.ops.segment_sum(partials, encode_slot, num_segments=band_count)  55.8 us
    all_to_all x1, waiting for transfers between devices, per_device(): lax.all_to_all(outgoing, 'band', split_axis=0, concat_axis=0, tiled=True)  50.8 us
    all_to_all x2, waiting for transfers between devices, several_exchanges(): lax.all_to_all(slab, axis, split_axis=0, concat_axis=0, tiled=True)  42.3 us
    dot_general x1, local copies, waits for them, and re-layouts, per_device(): jnp.einsum('eij,ejc->eic', encode_tiles, sources, preferred_element_type=...  24.7 us
    dot_general x1, local copies, waits for them, and re-layouts, per_device(): jnp.einsum('eij,ejc->eic', decode_tiles, picked, preferred_element_type=j...  24.7 us
    all_to_all x2, starting transfers between devices, several_exchanges(): lax.all_to_all(slab, axis, split_axis=0, concat_axis=0, tiled=True)  17.7 us
  transfers between devices with their start and end apart: 5, of which 4 were waited for; matrix products, arithmetic and copies ran while one was open for 27% of the time, Pallas kernels for 0%

commit v1 on v0

v1 whole, which is shorter than its diff:
```python
import functools

import jax
import jax.numpy as jnp
from jax import lax
from jax.experimental import pallas as pl
from jax.experimental.pallas import tpu as pltpu
from jax.sharding import PartitionSpec as P

MB = 1 << 20
F32 = jnp.float32
BF16 = jnp.bfloat16
SWAP = [(0, 1), (1, 0)]


def silu(v):
    return v / (1.0 + jnp.exp(-v))


def dot(a, b):
    return jnp.dot(a, b, preferred_element_type=F32)


def half(i, width):
    return pl.ds(pl.multiple_of(i * width, width), width)


def encode_body(nm, nt, slot_ref, source_ref, core_ref, own, other, weight, tiles, out, message, acc):
    step = pl.program_id(0)
    rows = own.shape[0]
    per = tiles.shape[0]
    edge = tiles.shape[1]
    per_out = out.shape[0]
    zero_step = acc.shape[0] // nm

    @pl.when(step < nm)
    def _():
        core = core_ref[0]
        k = own.shape[1]
        z = dot(own[...], weight[half(core, k), :]) + dot(other[...], weight[half(1 - core, k), :])
        value = silu(z).astype(BF16)
        blocks = rows // edge
        message[pl.ds(step * blocks, blocks)] = value.reshape(blocks, edge, value.shape[1])
        acc[pl.ds(step * zero_step, zero_step)] = jnp.zeros((zero_step, *acc.shape[1:]), F32)

    @pl.when((step >= nm) & (step < nm + nt))
    def _():
        base = (step - nm) * per
        for i in range(per):
            slot = slot_ref[base + i]
            source = source_ref[base + i]
            acc[slot] += dot(tiles[i], message[source])

    @pl.when(step >= nm + nt)
    def _():
        first = (step - nm - nt) * per_out
        out[...] = acc[pl.ds(first, per_out)].astype(BF16)


def encode(own, other, weight, tiles, source, slot, core, slots):
    rows, k = own.shape
    count, edge, _ = tiles.shape
    width = weight.shape[1]
    nm, nt, no = 8, 8, 8
    return pl.pallas_call(
        functools.partial(encode_body, nm, nt),
        out_shape=jax.ShapeDtypeStruct((slots, edge, width), BF16),
        grid_spec=pltpu.PrefetchScalarGridSpec(
            num_scalar_prefetch=3,
            grid=(nm + nt + no,),
            in_specs=[
                pl.BlockSpec((rows // nm, k), lambda i, *_: (jnp.minimum(i, nm - 1), 0)),
                pl.BlockSpec((rows // nm, k), lambda i, *_: (jnp.minimum(i, nm - 1), 0)),
                pl.BlockSpec(weight.shape, lambda i, *_: (0, 0)),
                pl.BlockSpec((count // nt, edge, edge), lambda i, *_: (jnp.clip(i - nm, 0, nt - 1), 0, 0)),
            ],
            out_specs=pl.BlockSpec((slots // no, edge, width), lambda i, *_: (jnp.clip(i - nm - nt, 0, no - 1), 0, 0)),
            scratch_shapes=[
                pltpu.VMEM((rows // edge, edge, width), BF16),
                pltpu.VMEM((slots, edge, width), F32),
            ],
        ),
        compiler_params=pltpu.CompilerParams(vmem_limit_bytes=60 * MB),
        cost_estimate=pl.CostEstimate(
            flops=2 * count * edge * edge * width, bytes_accessed=16 * MB, transcendentals=rows * width
        ),
        name="encode",
    )(slot, source, core, own, other, weight, tiles)


def mesh_body(
    nr, block_ref, link_ref, core_ref, arrived, mesh, mesh_other, self_w, self_o, pool_w, pool_o, out_w, out_o,
    keep, send, outgoing, acc, state, source,
):
    step = pl.program_id(0)
    core = core_ref[0]
    bands = arrived.shape[0] // 2
    rows, width = arrived.shape[1:]

    @pl.when(step == 0)
    def _():
        acc[...] = jnp.zeros(acc.shape, F32)

    @pl.when(step < nr)
    def _():
        for i in range(bands):
            block = block_ref[step * bands + i]
            for part in range(2):
                acc[block, :, part * width : (part + 1) * width] += arrived[2 * i + part].astype(F32)

    @pl.when(step == nr - 1)
    def _():
        pooled = acc[...].reshape(-1, 2 * width).astype(BF16)
        mine, theirs = mesh[...], mesh_other[...]
        hidden = []
        for sw, pw in ((self_w, pool_w), (self_o, pool_o)):
            inner = (
                dot(mine, sw[half(core, width), :])
                + dot(theirs, sw[half(1 - core, width), :])
                + dot(pooled, pw[...])
            )
            hidden.append(silu(inner).astype(BF16))
        full = 2 * width
        state[...] = dot(hidden[0], out_w[:, :full]) + dot(hidden[1], out_o[:, :full])
        sent = dot(hidden[0], out_w[:, full:]) + dot(hidden[1], out_o[:, full:])
        source[...] = sent.astype(BF16).reshape(source.shape)
        keep[...] = (mine.astype(F32) + state[:, half(core, width)]).astype(BF16)
        send[...] = (theirs.astype(F32) + state[:, half(1 - core, width)]).astype(BF16)

    @pl.when(step >= nr)
    def _():
        count = outgoing.shape[0] // 2
        for i in range(count):
            block = link_ref[(step - nr) * count + i]
            for part in range(2):
                outgoing[2 * i + part] = source[block, :, part * width : (part + 1) * width]


def mesh_update(arrived, owner_block, core, mesh, mesh_other, weights, blocks):
    pieces, rows, width = arrived.shape
    nr, no = 8, 8
    whole = lambda a: pl.BlockSpec(a.shape, lambda i, *_: (0,) * a.ndim)
    flat = jax.ShapeDtypeStruct(mesh.shape, BF16)
    return pl.pallas_call(
        functools.partial(mesh_body, nr),
        out_shape=(flat, flat, jax.ShapeDtypeStruct(arrived.shape, BF16)),
        grid_spec=pltpu.PrefetchScalarGridSpec(
            num_scalar_prefetch=3,
            grid=(nr + no,),
            in_specs=[
                pl.BlockSpec((pieces // nr, rows, width), lambda i, *_: (jnp.minimum(i, nr - 1), 0, 0)),
                whole(mesh),
                whole(mesh_other),
                *[whole(w) for w in weights],
            ],
            out_specs=[
                whole(flat),
                whole(flat),
                pl.BlockSpec((pieces // no, rows, width), lambda i, *_: (jnp.maximum(i - nr, 0), 0, 0)),
            ],
            scratch_shapes=[
                pltpu.VMEM((blocks, rows, 2 * width), F32),
                pltpu.VMEM((blocks * rows, 2 * width), F32),
                pltpu.VMEM((blocks, rows, 2 * width), BF16),
            ],
        ),
        compiler_params=pltpu.CompilerParams(vmem_limit_bytes=60 * MB),
        cost_estimate=pl.CostEstimate(flops=10**9, bytes_accessed=12 * MB, transcendentals=1 << 17),
        name="mesh_update",
    )(owner_block, owner_block, core, arrived, mesh, mesh_other, *weights)


def decode_body(ni, nt, slot_ref, target_ref, picked, grid_in, tiles, out, acc):
    step = pl.program_id(0)
    per = tiles.shape[0]
    per_in = grid_in.shape[0]
    per_out = out.shape[0]

    @pl.when(step < ni)
    def _():
        acc[pl.ds(step * per_in, per_in)] = grid_in[...].astype(F32)

    @pl.when((step >= ni) & (step < ni + nt))
    def _():
        base = (step - ni) * per
        for i in range(per):
            acc[target_ref[base + i]] += dot(tiles[i], picked[slot_ref[base + i]])

    @pl.when(step >= ni + nt)
    def _():
        out[...] = acc[pl.ds((step - ni - nt) * per_out, per_out)].astype(BF16)


def decode(picked, grid_blocks, tiles, slot, target):
    count, edge, _ = tiles.shape
    blocks, _, width = grid_blocks.shape
    ni, nt, no = 4, 8, 8
    return pl.pallas_call(
        functools.partial(decode_body, ni, nt),
        out_shape=jax.ShapeDtypeStruct(grid_blocks.shape, BF16),
        grid_spec=pltpu.PrefetchScalarGridSpec(
            num_scalar_prefetch=2,
            grid=(ni + nt + no,),
            in_specs=[
                pl.BlockSpec(picked.shape, lambda i, *_: (0, 0, 0)),
                pl.BlockSpec((blocks // ni, edge, width), lambda i, *_: (jnp.minimum(i, ni - 1), 0, 0)),
                pl.BlockSpec((count // nt, edge, edge), lambda i, *_: (jnp.clip(i - ni, 0, nt - 1), 0, 0)),
            ],
            out_specs=pl.BlockSpec((blocks // no, edge, width), lambda i, *_: (jnp.clip(i - ni - nt, 0, no - 1), 0, 0)),
            scratch_shapes=[pltpu.VMEM((blocks, edge, width), F32)],
        ),
        compiler_params=pltpu.CompilerParams(vmem_limit_bytes=60 * MB),
        cost_estimate=pl.CostEstimate(
            flops=2 * count * edge * edge * width, bytes_accessed=16 * MB, transcendentals=0
        ),
        name="decode",
    )(slot, target, picked, grid_blocks, tiles)


def swap(x):
    return lax.ppermute(x, "mp", SWAP)


def per_device(
    grid_nodes,
    mesh_nodes,
    send_weight,
    self_weight,
    pooled_weight,
    out_weight,
    encode_source,
    encode_slot,
    encode_tiles,
    slot_block,
    decode_slot,
    decode_target,
    decode_tiles,
):
    bands = lax.axis_size("band")
    core = lax.axis_index("mp").astype(jnp.int32)
    core_1 = core.reshape(1)
    edge = encode_tiles.shape[1]
    width = grid_nodes.shape[1]
    mesh_blocks = mesh_nodes.shape[0] // edge
    rows = edge // 2

    grid_other = swap(grid_nodes)
    owner_block = lax.all_to_all(slot_block[0], "band", split_axis=0, concat_axis=0, tiled=True)
    halves = mesh_nodes.reshape(mesh_blocks, 2, rows, width)
    mesh_keep = lax.dynamic_index_in_dim(halves, core, 1, keepdims=False).reshape(-1, width)
    mesh_send = lax.dynamic_index_in_dim(halves, 1 - core, 1, keepdims=False).reshape(-1, width)
    out_flat = out_weight.reshape(out_weight.shape[0], -1)
    mesh_other = swap(mesh_send)
    self_other, pooled_other, out_other = swap(self_weight), swap(pooled_weight), swap(out_flat)

    slot_sums = encode(
        grid_nodes, grid_other, send_weight, encode_tiles, encode_source, encode_slot, core_1, bands
    )
    arrived = lax.all_to_all(
        slot_sums.reshape(2 * bands, rows, width), ("band", "mp"), split_axis=0, concat_axis=0, tiled=True
    )
    keep, send, outgoing = mesh_update(
        arrived,
        owner_block,
        core_1,
        mesh_keep,
        mesh_other,
        (self_weight, self_other, pooled_weight, pooled_other, out_flat, out_other),
        mesh_blocks,
    )
    returned = lax.all_to_all(outgoing, ("band", "mp"), split_axis=0, concat_axis=0, tiled=True)
    came = swap(send).reshape(mesh_blocks, 1, rows, width)
    kept = keep.reshape(mesh_blocks, 1, rows, width)
    mesh_state = jnp.concatenate(
        [jnp.where(core == 0, kept, came), jnp.where(core == 0, came, kept)], axis=1
    ).reshape(mesh_nodes.shape)
    grid_state = decode(
        returned.reshape(bands, edge, width),
        grid_nodes.reshape(-1, edge, width),
        decode_tiles,
        decode_slot,
        decode_target,
    )
    return grid_state.reshape(grid_nodes.shape), mesh_state


def solution(mesh):
    return jax.shard_map(
        per_device,
        mesh=mesh,
        in_specs=(
            P("band", "mp"),
            P("band", "mp"),
            P(None, "mp"),
            P(None, "mp"),
            P(None, "mp"),
            P("mp", None, None),
            P("band"),
            P("band"),
            P("band", None, None),
            P("band", None),
            P("band"),
            P("band"),
            P("band", None, None),
        ),
        out_specs=(P("band", "mp"), P("band", "mp")),
        check_vma=False,
    )
```

time: 495 us -> 182 us (0.37)
  other arithmetic: 125 us -> 1.81 us
  local copies, waits for them, and re-layouts: 99.8 us -> 4.18 us
  blocking collectives: 67.8 us -> 0 us
  Pallas kernels: 0 us -> 44.1 us
  matrix products: 41.5 us -> 0 us
  between operations: 14.3 us -> 0.85 us
  waiting for transfers between devices: 113 us -> 100 us
    scatter-add x2 -> x0, other arithmetic: 113 us -> none  [the longest x1 56.7 us: per_device(): jax.ops.segment_sum(contribution, decode_target, num_segments=grid_blocks)]
    all_to_all x2 -> x0, blocking collectives: 67.8 us -> none  [the longest x1 63.2 us: several_exchanges(): lax.all_to_all(slab, axis, split_axis=0, concat_axis=0, tiled=True)]
    dot_general x3 -> x0, local copies, waits for them, and re-layouts: 49.6 us -> none  [the longest x1 24.7 us: per_device(): jnp.einsum('eij,ejc->eic', encode_tiles, sources, preferred_element_type=...]
    pallas_call x0 -> x3, Pallas kernels: none -> 44.1 us  [the longest x1 18.1 us: encode(): pl.pallas_call(functools.partial(encode_body, nm, nt), out_shape=jax.Shap...]
    dot_general x6 -> x0, matrix products: 41.5 us -> none  [the longest x1 16.4 us: per_device(): jnp.einsum('eij,ejc->eic', encode_tiles, sources, preferred_element_type=...]
    gather x3 -> x0, local copies, waits for them, and re-layouts: 21.4 us -> none  [the longest x1 10.4 us: per_device(): picked = jnp.take(returned, decode_slot, axis=0)]
    reduce_scatter x1 -> x0, waiting for transfers between devices: 14.2 us -> none  [per_device(): lax.psum_scatter(partial_out, 'mp', scatter_dimension=2, tiled=True)]
    all_to_all x3 -> x1, local copies, waits for them, and re-layouts: 12.7 us -> 1.36 us  [per_device(): lax.all_to_all(slot_block[0], 'band', split_axis=0, concat_axis=0, tiled=...]
  transfers between devices with their start and end apart: 5 -> 9, of which waited for: 4 -> 3; matrix products, arithmetic and copies ran while one was open for 27% -> 3% of each run, Pallas kernels for 0% -> 10%
where the time goes in v1:
time: 182 us; the launch traced here: 181 us
  waiting for transfers between devices  100 us (55%)
  Pallas kernels  44.1 us (24%)
  starting transfers between devices  29.3 us (16%)
  local copies, waits for them, and re-layouts  4.18 us (2%)
    all_to_all x1, waiting for transfers between devices, per_device(): lax.all_to_all(outgoing, ('band', 'mp'), split_axis=0, concat_axis=0, til...  50.3 us
    all_to_all x1, waiting for transfers between devices, per_device(): lax.all_to_all(slot_sums.reshape(2 * bands, rows, width), ('band', 'mp'),...  48.8 us
    pallas_call x1, Pallas kernels, encode(): pl.pallas_call(functools.partial(encode_body, nm, nt), out_shape=jax.Shap...  18.1 us
    pallas_call x1, Pallas kernels, decode(): pl.pallas_call(functools.partial(decode_body, ni, nt), out_shape=jax.Shap...  14.9 us
    all_to_all x1, starting transfers between devices, per_device(): lax.all_to_all(slot_block[0], 'band', split_axis=0, concat_axis=0, tiled=...  11.5 us
    pallas_call x1, Pallas kernels, mesh_update(): pl.pallas_call(functools.partial(mesh_body, nr), out_shape=(flat, flat, j...  11.1 us
    all_to_all x1, starting transfers between devices, per_device(): lax.all_to_all(slot_sums.reshape(2 * bands, rows, width), ('band', 'mp'),...  10.5 us
    all_to_all x1, starting transfers between devices, per_device(): lax.all_to_all(outgoing, ('band', 'mp'), split_axis=0, concat_axis=0, til...  5.99 us
  transfers between devices with their start and end apart: 9, of which 3 were waited for; matrix products, arithmetic and copies ran while one was open for 3% of the time, Pallas kernels for 10%

profile of v1, /device:TPU:0, one launch (start us, length us, event | category | flops | bytes accessed | tf_op | source)
XLA Modules:
  0.0 180.7 jit_solution(5236818186069284897)
XLA Ops:
  0.6 0.1 collective-permute-start
  0.7 1.4 copy.22
  2.1 11.5 %all-to-all-start = ((s32[64,1,1]{2,1,0:T(1,128)}), s32[64,1,1]{2,1,0:T(1,128)S(1)}, u32[]{:S(2)}, u32[]{:S(2)}) async-start(s32[64,1,1]{2,1,0:T(1,128)} %copy.22), calls=%async_computation | async-start | bytes 65536 | tf_op jit(solution)/shard_map/all_to_all | solution.py:248
  13.6 0.0 copy-start
  13.6 1.3 copy-done
  15.0 18.1 %encode.1 = bf16[64,128,256]{2,1,0:T(8,128)(2,1)} custom-call(s32[192]{0:T(256)} %slot_ref.2, s32[192]{0:T(256)} %source_ref.1, s32[1]{0:T(128)} %bitcast.1.core_ref, bf16[4096,256]{1,0:T(8,128)(2,1)} %own.1, bf16[4096,256]{1,0:T(8,128)(2,1)} %copy-done, bf16[512,256]{1,0:T(8,128)(2,1)} %weight.1, bf16[192,128,128]{2,1,0:T(8,128)(2,1)} %tiles.2), custom_call_target="tpu_custom_call" | custom-call | flops 1610612736 | bytes 16777216 | tf_op jit(solution)/shard_map/encode/pallas_call | solution.py:65
  33.1 0.0 copy-start.5
  33.1 0.0 copy-start.8
  33.1 10.5 %all-to-all-start.1 = ((bf16[128,64,256]{2,1,0:T(8,128)(2,1)}), bf16[128,64,256]{2,1,0:T(8,128)(2,1)}, u32[]{:S(2)}, u32[]{:S(2)}) async-start(bf16[128,64,256]{2,1,0:T(8,128)(2,1)} %bitcast.18), calls=%async_computation.1 | async-start | bytes 8388608 | tf_op jit(solution)/shard_map/all_to_all | solution.py:259
  43.7 0.1 copy.28
  43.8 0.1 collective-permute-start.4
  43.9 0.5 collective-permute-start.2
  44.4 0.1 collective-permute-start.3
  44.5 0.7 constant_dynamic-slice_fusion
  45.1 0.4 collective-permute-start.1
  45.5 1.8 reduce.block_ref.link_ref
  47.4 48.8 %all-to-all-done.1.arrived = bf16[128,64,256]{2,1,0:T(8,128)(2,1)} async-done(((bf16[128,64,256]{2,1,0:T(8,128)(2,1)}), bf16[128,64,256]{2,1,0:T(8,128)(2,1)}, u32[]{:S(2)}, u32[]{:S(2)}) %all-to-all-start.1) | async-done | bytes 4194336 | tf_op jit(solution)/shard_map/all_to_all | solution.py:259
  96.2 11.1 %mesh_update.1 = (bf16[256,256]{1,0:T(8,128)(2,1)}, bf16[256,256]{1,0:T(8,128)(2,1)}, bf16[128,64,256]{2,1,0:T(8,128)(2,1)}) custom-call(s32[64]{0:T(128)} %reduce.block_ref.link_ref, s32[64]{0:T(128)} %reduce.block_ref.link_ref, s32[1]{0:T(128)} %bitcast.1.core_ref, bf16[128,64,256]{2,1,0:T(8,128)(2,1)} %all-to-all-done.1.arrived, ...), custom_call_target="tpu_custom_call" | custom-call | flops 1000000000 | bytes 12582912 | tf_op jit(solution)/shard_map/mesh_update/pallas_call | solution.py:144
  107.3 6.0 %all-to-all-start.2 = ((bf16[128,64,256]{2,1,0:T(8,128)(2,1)}), bf16[128,64,256]{2,1,0:T(8,128)(2,1)}, u32[]{:S(2)}, u32[]{:S(2)}) async-start(bf16[128,64,256]{2,1,0:T(8,128)(2,1)} %get-tuple-element.5), calls=%async_computation.2 | async-start | bytes 8388608 | tf_op jit(solution)/shard_map/all_to_all | solution.py:271
  113.3 0.1 collective-permute-start.5
  113.4 1.3 collective-permute-done.5
  114.8 0.7 copy.25
  115.5 50.3 %all-to-all-done.2 = bf16[128,64,256]{2,1,0:T(8,128)(2,1)} async-done(((bf16[128,64,256]{2,1,0:T(8,128)(2,1)}), bf16[128,64,256]{2,1,0:T(8,128)(2,1)}, u32[]{:S(2)}, u32[]{:S(2)}) %all-to-all-start.2) | async-done | bytes 4194336 | tf_op jit(solution)/shard_map/all_to_all | solution.py:271
  165.8 14.9 %decode.1 = bf16[32,128,256]{2,1,0:T(8,128)(2,1)} custom-call(s32[192]{0:T(256)} %slot_ref.3, s32[192]{0:T(256)} %target_ref.1, bf16[64,128,256]{2,1,0:T(8,128)(2,1)} %bitcast.6.picked, bf16[32,128,256]{2,1,0:T(8,128)(2,1)} %bitcast.19, bf16[192,128,128]{2,1,0:T(8,128)(2,1)} %tiles.3), custom_call_target="tpu_custom_call" | custom-call | flops 1610612736 | bytes 16777216 | tf_op jit(solution)/shard_map/decode/pallas_call | solution.py:198
  (28 shorter events, 0.1 us)
Async XLA Ops:
  0.6 13.0 %collective-permute-start = (bf16[4096,256]{1,0:T(8,128)(2,1)}, bf16[4096,256]{1,0:T(8,128)(2,1)S(1)}, u32[]{:S(2)}, u32[]{:S(2)}) collective-permute-start(bf16[4096,256]{1,0:T(8,128)(2,1)} %own.1), channel_id=1, source_target_pairs={{0,1},{1,0},{2,3},{3,2},{4,5},{5,4},{6,7},{7,6},{8,9},{9,8},{10,11... | collective-permute-start | bytes 6291464 | tf_op jit(solution)/shard_map/ppermute | solution.py:221
  2.1 31.0 %all-to-all-start = ((s32[64,1,1]{2,1,0:T(1,128)}), s32[64,1,1]{2,1,0:T(1,128)S(1)}, u32[]{:S(2)}, u32[]{:S(2)}) async-start(s32[64,1,1]{2,1,0:T(1,128)} %copy.22), calls=%async_computation | async-start | bytes 65536 | tf_op jit(solution)/shard_map/all_to_all | solution.py:248
  13.6 1.3 copy-start
  33.1 10.6 %copy-start.3 = (bf16[256,2,512]{2,1,0:T(2,128)(2,1)S(1)}, bf16[256,2,512]{2,1,0:T(2,128)(2,1)}, u32[]{:S(2)}) copy-start(bf16[256,2,512]{2,1,0:T(2,128)(2,1)} %param.18) | copy-start | bytes 1572868
  33.1 10.8 %copy-start.4 = (bf16[512,256]{1,0:T(8,128)(2,1)S(1)}, bf16[512,256]{1,0:T(8,128)(2,1)}, u32[]{:S(2)}) copy-start(bf16[512,256]{1,0:T(8,128)(2,1)} %self_w.1) | copy-start | bytes 786436
  33.1 11.2 %copy-start.5 = (bf16[512,256]{1,0:T(8,128)(2,1)S(1)}, bf16[512,256]{1,0:T(8,128)(2,1)}, u32[]{:S(2)}) copy-start(bf16[512,256]{1,0:T(8,128)(2,1)} %pool_w.1) | copy-start | bytes 786436
  33.1 11.3 %copy-start.8 = (bf16[512,256]{1,0:T(8,128)(2,1)S(1)}, bf16[512,256]{1,0:T(8,128)(2,1)}, u32[]{:S(2)}) copy-start(bf16[512,256]{1,0:T(8,128)(2,1)} %param.14) | copy-start | bytes 786436
  33.1 63.0 %all-to-all-start.1 = ((bf16[128,64,256]{2,1,0:T(8,128)(2,1)}), bf16[128,64,256]{2,1,0:T(8,128)(2,1)}, u32[]{:S(2)}, u32[]{:S(2)}) async-start(bf16[128,64,256]{2,1,0:T(8,128)(2,1)} %bitcast.18), calls=%async_computation.1 | async-start | bytes 8388608 | tf_op jit(solution)/shard_map/all_to_all | solution.py:259
  43.7 52.4 %copy-start.1 = (bf16[32,8,2,512]{3,1,2,0:T(8,128)(2,1)}, bf16[32,8,2,512]{3,1,2,0:T(8,128)(2,1)S(1)}, u32[]{:S(2)}) copy-start(bf16[32,8,2,512]{3,1,2,0:T(8,128)(2,1)S(1)} %copy.28) | copy-start | bytes 1572868
  43.8 3.6 %collective-permute-start.4 = (bf16[256,1024]{1,0:T(8,128)(2,1)S(1)}, bf16[256,1024]{1,0:T(8,128)(2,1)S(1)}, u32[]{:S(2)}, u32[]{:S(2)}) collective-permute-start(bf16[256,1024]{1,0:T(8,128)(2,1)S(1)} %bitcast.20), channel_id=1, source_target_pairs={{0,1},{1,0},{2,3},{3,2},{4,5},{5,4},{6,7},{7,6},{8,9},{9,8},{10,11... | collective-permute-start | bytes 1572872 | tf_op jit(solution)/shard_map/ppermute | solution.py:221
  43.9 3.5 %collective-permute-start.2 = (bf16[512,256]{1,0:T(8,128)(2,1)S(1)}, bf16[512,256]{1,0:T(8,128)(2,1)S(1)}, u32[]{:S(2)}, u32[]{:S(2)}) collective-permute-start(bf16[512,256]{1,0:T(8,128)(2,1)S(1)} %copy-done.4), channel_id=1, source_target_pairs={{0,1},{1,0},{2,3},{3,2},{4,5},{5,4},{6,7},{7,6},{8,9},{9,8},{10,11... | collective-permute-start | bytes 786440 | tf_op jit(solution)/shard_map/ppermute | solution.py:221
  44.4 3.0 %collective-permute-start.3 = (bf16[512,256]{1,0:T(8,128)(2,1)S(1)}, bf16[512,256]{1,0:T(8,128)(2,1)S(1)}, u32[]{:S(2)}, u32[]{:S(2)}) collective-permute-start(bf16[512,256]{1,0:T(8,128)(2,1)S(1)} %copy-done.5), channel_id=1, source_target_pairs={{0,1},{1,0},{2,3},{3,2},{4,5},{5,4},{6,7},{7,6},{8,9},{9,8},{10,11... | collective-permute-start | bytes 786440 | tf_op jit(solution)/shard_map/ppermute | solution.py:221
  45.1 2.2 %collective-permute-start.1 = (bf16[256,256]{1,0:T(8,128)(2,1)S(1)}, bf16[256,256]{1,0:T(8,128)(2,1)S(1)}, u32[]{:S(2)}, u32[]{:S(2)}) collective-permute-start(bf16[256,256]{1,0:T(8,128)(2,1)S(1)} %bitcast.29), channel_id=1, source_target_pairs={{0,1},{1,0},{2,3},{3,2},{4,5},{5,4},{6,7},{7,6},{8,9},{9,8},{10,11... | collective-permute-start | bytes 393224 | tf_op jit(solution)/shard_map/ppermute | solution.py:221
  47.3 48.9 %copy-start.9 = (bf16[256,256]{1,0:T(8,128)(2,1)}, bf16[256,256]{1,0:T(8,128)(2,1)S(1)}, u32[]{:S(2)}) copy-start(bf16[256,256]{1,0:T(8,128)(2,1)S(1)} %collective-permute-done.1.mesh_other) | copy-start | bytes 393220
  47.3 48.9 %copy-start.6 = (bf16[512,256]{1,0:T(8,128)(2,1)}, bf16[512,256]{1,0:T(8,128)(2,1)S(1)}, u32[]{:S(2)}) copy-start(bf16[512,256]{1,0:T(8,128)(2,1)S(1)} %collective-permute-done.2.self_o) | copy-start | bytes 786436
  47.3 48.8 %copy-start.7 = (bf16[512,256]{1,0:T(8,128)(2,1)}, bf16[512,256]{1,0:T(8,128)(2,1)S(1)}, u32[]{:S(2)}) copy-start(bf16[512,256]{1,0:T(8,128)(2,1)S(1)} %collective-permute-done.3.pool_o) | copy-start | bytes 786436
  47.4 48.8 %copy-start.2 = (bf16[256,1024]{1,0:T(8,128)(2,1)}, bf16[256,1024]{1,0:T(8,128)(2,1)S(1)}, u32[]{:S(2)}) copy-start(bf16[256,1024]{1,0:T(8,128)(2,1)S(1)} %collective-permute-done.4.out_o) | copy-start | bytes 1572868
  107.3 6.0 %copy-start.11 = (bf16[256,256]{1,0:T(8,128)(2,1)S(1)}, bf16[256,256]{1,0:T(8,128)(2,1)}, u32[]{:S(2)}) copy-start(bf16[256,256]{1,0:T(8,128)(2,1)} %get-tuple-element.7) | copy-start | bytes 393220
  107.3 7.4 %copy-start.10 = (bf16[256,256]{1,0:T(8,128)(2,1)S(1)}, bf16[256,256]{1,0:T(8,128)(2,1)}, u32[]{:S(2)}) copy-start(bf16[256,256]{1,0:T(8,128)(2,1)} %get-tuple-element.6) | copy-start | bytes 393220
  107.3 58.5 %all-to-all-start.2 = ((bf16[128,64,256]{2,1,0:T(8,128)(2,1)}), bf16[128,64,256]{2,1,0:T(8,128)(2,1)}, u32[]{:S(2)}, u32[]{:S(2)}) async-start(bf16[128,64,256]{2,1,0:T(8,128)(2,1)} %get-tuple-element.5), calls=%async_computation.2 | async-start | bytes 8388608 | tf_op jit(solution)/shard_map/all_to_all | solution.py:271
  113.3 1.4 collective-permute-start.5

commit v2 on v1

v2 whole, which is shorter than its diff:
```python
import functools

import jax
import jax.numpy as jnp
from jax import lax
from jax.experimental import pallas as pl
from jax.experimental.pallas import tpu as pltpu
from jax.sharding import PartitionSpec as P

MB = 1 << 20
F32 = jnp.float32
BF16 = jnp.bfloat16
SWAP = [(0, 1), (1, 0)]


def silu(v):
    return v / (1.0 + jnp.exp(-v))


def dot(a, b):
    return jnp.dot(a, b, preferred_element_type=F32)


def half(i, width):
    return pl.ds(pl.multiple_of(i * width, width), width)


def fetch(source, target, semaphores, count):
    size = source.shape[0] // count

    def piece(k):
        rows = pl.ds(k * size, size)
        return pltpu.make_async_copy(source.at[rows], target.at[rows], semaphores.at[k])

    for k in range(count):
        piece(k).start()
    return lambda k: piece(k).wait()


def hbm():
    return pl.BlockSpec(memory_space=pl.ANY)


PARAMS = pltpu.CompilerParams(vmem_limit_bytes=60 * MB)


PIECES = 4
UNROLL = 16
TAG = 8


def encode_body(
    slot_ref, source_ref, link_ref, core_ref, own_hbm, other_hbm, weight_hbm, tiles_hbm, out_hbm,
    own, other, weight, tiles, message, acc, out, own_sem, other_sem, weight_sem, tiles_sem, out_sem,
):
    core = core_ref[0]
    blocks, edge, width = message.shape
    slots = acc.shape[0]
    count = tiles.shape[0]
    rows = edge // 2
    lanes = out.shape[2]
    weight_ready = fetch(weight_hbm, weight, weight_sem, 1)
    own_ready = fetch(own_hbm, own, own_sem, PIECES)
    other_ready = fetch(other_hbm, other, other_sem, PIECES)
    tiles_ready = fetch(tiles_hbm, tiles, tiles_sem, PIECES)
    weight_ready(0)

    inner = 2 * edge
    per = blocks * edge // inner // PIECES
    cleared = slots // (per * PIECES)

    @pl.loop(0, PIECES)
    def _(piece):
        own_ready(piece)
        other_ready(piece)

        @pl.loop(0, per)
        def _(j):
            step = piece * per + j
            at = pl.ds(pl.multiple_of(step * inner, inner), inner)
            z = dot(own[at, :], weight[half(core, width), :]) + dot(other[at, :], weight[half(1 - core, width), :])
            message[pl.ds(step * 2, 2)] = silu(z).astype(BF16).reshape(2, edge, width)
            acc[pl.ds(step * cleared, cleared)] = jnp.zeros((cleared, edge, width), F32)

    @pl.loop(0, PIECES)
    def _(piece):
        tiles_ready(piece)

        @pl.loop(0, count // PIECES // UNROLL)
        def _(j):
            base = piece * (count // PIECES) + j * UNROLL
            for i in range(UNROLL):
                acc[slot_ref[base + i]] += dot(tiles[base + i], message[source_ref[base + i]])

    size = 2 * slots // PIECES

    def leave(k):
        at = pl.ds(k * size, size)
        return pltpu.make_async_copy(out.at[at], out_hbm.at[at], out_sem.at[k])

    @pl.loop(0, PIECES)
    def _(piece):
        @pl.loop(0, slots // PIECES, unroll=4)
        def _(j):
            slot = piece * (slots // PIECES) + j
            tag = jnp.full((TAG, lanes), link_ref[slot].astype(F32), F32).astype(BF16)
            for part in range(2):
                value = acc[slot, part * rows : (part + 1) * rows, :].astype(BF16)
                for column in range(2):
                    out[2 * slot + part, column * rows : (column + 1) * rows, :] = value[
                        :, column * lanes : (column + 1) * lanes
                    ]
                out[2 * slot + part, 2 * rows :, :] = tag

        leave(piece).start()

    for piece in range(PIECES):
        leave(piece).wait()


def encode(own, other, weight, tiles, source, slot, link, core, slots):
    count, edge, _ = tiles.shape
    width = weight.shape[1]
    sent = (2 * slots, edge + TAG, width // 2)
    dma = pltpu.SemaphoreType.DMA
    return pl.pallas_call(
        encode_body,
        out_shape=jax.ShapeDtypeStruct(sent, BF16),
        grid_spec=pltpu.PrefetchScalarGridSpec(
            num_scalar_prefetch=4,
            in_specs=[hbm()] * 4,
            out_specs=hbm(),
            scratch_shapes=[
                pltpu.VMEM(own.shape, BF16),
                pltpu.VMEM(other.shape, BF16),
                pltpu.VMEM(weight.shape, BF16),
                pltpu.VMEM(tiles.shape, BF16),
                pltpu.VMEM((own.shape[0] // edge, edge, width), BF16),
                pltpu.VMEM((slots, edge, width), F32),
                pltpu.VMEM(sent, BF16),
                dma((PIECES,)),
                dma((PIECES,)),
                dma((1,)),
                dma((PIECES,)),
                dma((PIECES,)),
            ],
        ),
        compiler_params=PARAMS,
        cost_estimate=pl.CostEstimate(
            flops=2 * count * edge * edge * width, bytes_accessed=16 * MB, transcendentals=own.shape[0] * width
        ),
        name="encode",
    )(slot, source, link, core, own, other, weight, tiles)


def mesh_body(core_ref, arrived_hbm, mesh_hbm, other_hbm, *refs):
    weights_hbm, refs = refs[:6], refs[6:]
    keep, send, outgoing_hbm, arrived, mine_ref, theirs_ref = refs[:6]
    weights, refs = refs[6:12], refs[12:]
    acc, state, source, outgoing, block_ref, arrived_sem, small_sem, out_sem = refs
    core = core_ref[0]
    bands = arrived.shape[0] // 2
    lanes = arrived.shape[2]
    rows = acc.shape[1]
    width = 2 * lanes
    ready = fetch(arrived_hbm, arrived, arrived_sem, PIECES)
    small = [
        pltpu.make_async_copy(x, y, small_sem.at[k])
        for k, (x, y) in enumerate(zip((mesh_hbm, other_hbm, *weights_hbm), (mine_ref, theirs_ref, *weights)))
    ]
    for copy in small:
        copy.start()
    acc[...] = jnp.zeros(acc.shape, F32)

    @pl.loop(0, PIECES)
    def _(piece):
        ready(piece)

        @pl.loop(0, bands // PIECES, unroll=4)
        def _(j):
            band = piece * (bands // PIECES) + j
            tag = arrived[2 * band, 2 * rows :, :].astype(F32)
            block = jnp.max(tag).astype(jnp.int32)
            block_ref[band] = block

        @pl.loop(0, bands // PIECES, unroll=2)
        def _(j):
            band = piece * (bands // PIECES) + j
            block = block_ref[band]
            for part in range(2):
                for column in range(2):
                    at = (2 * part + column) * lanes
                    acc[block, :, at : at + lanes] += arrived[
                        2 * band + part, column * rows : (column + 1) * rows, :
                    ].astype(F32)

    for copy in small:
        copy.wait()
    self_w, self_o, pool_w, pool_o, out_w, out_o = weights
    pooled = acc[...].reshape(-1, 2 * width).astype(BF16)
    mine, theirs = mine_ref[...], theirs_ref[...]
    hidden = []
    for sw, pw in ((self_w, pool_w), (self_o, pool_o)):
        inner = (
            dot(mine, sw[half(core, width), :]) + dot(theirs, sw[half(1 - core, width), :]) + dot(pooled, pw[...])
        )
        hidden.append(silu(inner).astype(BF16))
    full = 2 * width
    sent = dot(hidden[0], out_w[:, full:]) + dot(hidden[1], out_o[:, full:])
    source[...] = sent.astype(BF16).reshape(source.shape)

    size = 2 * bands // PIECES

    def leave(k):
        at = pl.ds(k * size, size)
        return pltpu.make_async_copy(outgoing.at[at], outgoing_hbm.at[at], out_sem.at[k])

    @pl.loop(0, PIECES)
    def _(piece):
        @pl.loop(0, bands // PIECES, unroll=4)
        def _(j):
            band = piece * (bands // PIECES) + j
            block = block_ref[band]
            for part in range(2):
                outgoing[2 * band + part] = source[block, :, part * width : (part + 1) * width]

        leave(piece).start()

    state[...] = dot(hidden[0], out_w[:, :full]) + dot(hidden[1], out_o[:, :full])
    keep[...] = (mine.astype(F32) + state[:, half(core, width)]).astype(BF16)
    send[...] = (theirs.astype(F32) + state[:, half(1 - core, width)]).astype(BF16)
    for piece in range(PIECES):
        leave(piece).wait()


def mesh_update(arrived, core, mesh, mesh_other, weights, blocks):
    pieces, height, lanes = arrived.shape
    rows, width = (height - TAG) // 2, 2 * lanes
    flat = jax.ShapeDtypeStruct(mesh.shape, BF16)
    leaving = (pieces, rows, width)
    dma = pltpu.SemaphoreType.DMA
    vmem = pl.BlockSpec(memory_space=pltpu.VMEM)
    return pl.pallas_call(
        mesh_body,
        out_shape=(flat, flat, jax.ShapeDtypeStruct(leaving, BF16)),
        grid_spec=pltpu.PrefetchScalarGridSpec(
            num_scalar_prefetch=1,
            in_specs=[hbm()] * 9,
            out_specs=[vmem, vmem, hbm()],
            scratch_shapes=[
                pltpu.VMEM(arrived.shape, BF16),
                pltpu.VMEM(mesh.shape, BF16),
                pltpu.VMEM(mesh.shape, BF16),
                *[pltpu.VMEM(w.shape, BF16) for w in weights],
                pltpu.VMEM((blocks, rows, 2 * width), F32),
                pltpu.VMEM((blocks * rows, 2 * width), F32),
                pltpu.VMEM((blocks, rows, 2 * width), BF16),
                pltpu.VMEM(leaving, BF16),
                pltpu.SMEM((pieces // 2,), jnp.int32),
                dma((PIECES,)),
                dma((8,)),
                dma((PIECES,)),
            ],
        ),
        compiler_params=PARAMS,
        cost_estimate=pl.CostEstimate(flops=10**9, bytes_accessed=12 * MB, transcendentals=1 << 17),
        name="mesh_update",
    )(core, arrived, mesh, mesh_other, *weights)


def decode_body(
    slot_ref, target_ref, picked_hbm, grid_hbm, tiles_hbm, out_hbm,
    picked, start, tiles, acc, out, picked_sem, start_sem, tiles_sem, out_sem,
):
    count = tiles.shape[0]
    blocks = acc.shape[0]
    start_ready = fetch(grid_hbm, start, start_sem, PIECES)
    picked_ready = fetch(picked_hbm, picked, picked_sem, PIECES)
    tiles_ready = fetch(tiles_hbm, tiles, tiles_sem, PIECES)
    per = blocks // PIECES

    @pl.loop(0, PIECES)
    def _(piece):
        start_ready(piece)

        @pl.loop(0, per, unroll=4)
        def _(j):
            acc[piece * per + j] = start[piece * per + j].astype(F32)

    for piece in range(PIECES):
        picked_ready(piece)

    @pl.loop(0, PIECES)
    def _(piece):
        tiles_ready(piece)

        @pl.loop(0, count // PIECES // UNROLL)
        def _(j):
            base = piece * (count // PIECES) + j * UNROLL
            for i in range(UNROLL):
                acc[target_ref[base + i]] += dot(tiles[base + i], picked[slot_ref[base + i]])

    def leave(k):
        at = pl.ds(k * per, per)
        return pltpu.make_async_copy(out.at[at], out_hbm.at[at], out_sem.at[k])

    @pl.loop(0, PIECES)
    def _(piece):
        @pl.loop(0, per, unroll=4)
        def _(j):
            out[piece * per + j] = acc[piece * per + j].astype(BF16)

        leave(piece).start()

    for piece in range(PIECES):
        leave(piece).wait()


def decode(picked, grid_blocks, tiles, slot, target):
    count, edge, _ = tiles.shape
    width = grid_blocks.shape[2]
    dma = pltpu.SemaphoreType.DMA
    return pl.pallas_call(
        decode_body,
        out_shape=jax.ShapeDtypeStruct(grid_blocks.shape, BF16),
        grid_spec=pltpu.PrefetchScalarGridSpec(
            num_scalar_prefetch=2,
            in_specs=[hbm()] * 3,
            out_specs=hbm(),
            scratch_shapes=[
                pltpu.VMEM(picked.shape, BF16),
                pltpu.VMEM(grid_blocks.shape, BF16),
                pltpu.VMEM(tiles.shape, BF16),
                pltpu.VMEM(grid_blocks.shape, F32),
                pltpu.VMEM(grid_blocks.shape, BF16),
                *[dma((PIECES,))] * 4,
            ],
        ),
        compiler_params=PARAMS,
        cost_estimate=pl.CostEstimate(
            flops=2 * count * edge * edge * width, bytes_accessed=16 * MB, transcendentals=0
        ),
        name="decode",
    )(slot, target, picked, grid_blocks, tiles)


def swap(x):
    return lax.ppermute(x, "mp", SWAP)


def per_device(
    grid_nodes,
    mesh_nodes,
    send_weight,
    self_weight,
    pooled_weight,
    out_weight,
    encode_source,
    encode_slot,
    encode_tiles,
    slot_block,
    decode_slot,
    decode_target,
    decode_tiles,
):
    bands = lax.axis_size("band")
    core = lax.axis_index("mp").astype(jnp.int32)
    core_1 = core.reshape(1)
    edge = encode_tiles.shape[1]
    width = grid_nodes.shape[1]
    mesh_blocks = mesh_nodes.shape[0] // edge
    rows = edge // 2

    grid_other = swap(grid_nodes)
    halves = mesh_nodes.reshape(mesh_blocks, 2, rows, width)
    mesh_keep = lax.dynamic_index_in_dim(halves, core, 1, keepdims=False).reshape(-1, width)
    mesh_send = lax.dynamic_index_in_dim(halves, 1 - core, 1, keepdims=False).reshape(-1, width)
    out_flat = out_weight.reshape(out_weight.shape[0], -1)
    mesh_other = swap(mesh_send)
    self_other, pooled_other, out_other = swap(self_weight), swap(pooled_weight), swap(out_flat)

    slot_sums = encode(
        grid_nodes, grid_other, send_weight, encode_tiles, encode_source, encode_slot, slot_block[0], core_1, bands
    )
    arrived = lax.all_to_all(slot_sums, ("band", "mp"), split_axis=0, concat_axis=0, tiled=True)
    keep, send, outgoing = mesh_update(
        arrived,
        core_1,
        mesh_keep,
        mesh_other,
        (self_weight, self_other, pooled_weight, pooled_other, out_flat, out_other),
        mesh_blocks,
    )
    returned = lax.all_to_all(outgoing, ("band", "mp"), split_axis=0, concat_axis=0, tiled=True)
    came = swap(send).reshape(mesh_blocks, 1, rows, width)
    kept = keep.reshape(mesh_blocks, 1, rows, width)
    mesh_state = jnp.concatenate(
        [jnp.where(core == 0, kept, came), jnp.where(core == 0, came, kept)], axis=1
    ).reshape(mesh_nodes.shape)
    grid_state = decode(
        returned.reshape(bands, edge, width),
        grid_nodes.reshape(-1, edge, width),
        decode_tiles,
        decode_slot,
        decode_target,
    )
    return grid_state.reshape(grid_nodes.shape), mesh_state


def solution(mesh):
    return jax.shard_map(
        per_device,
        mesh=mesh,
        in_specs=(
            P("band", "mp"),
            P("band", "mp"),
            P(None, "mp"),
            P(None, "mp"),
            P(None, "mp"),
            P("mp", None, None),
            P("band"),
            P("band"),
            P("band", None, None),
            P("band", None),
            P("band"),
            P("band"),
            P("band", None, None),
        ),
        out_specs=(P("band", "mp"), P("band", "mp")),
        check_vma=False,
    )
```

time: 182 us -> 170 us (0.934)
  waiting for transfers between devices: 100 us -> 109 us
  Pallas kernels: 44.1 us -> 35.5 us
  starting transfers between devices: 29.3 us -> 20.8 us
    all_to_all x2 -> x1, starting transfers between devices: 22 us -> 11.6 us  [per_device(): lax.all_to_all(slot_sums, ('band', 'mp'), split_axis=0, concat_axis=0, ti...]
    pallas_call x3, Pallas kernels: 44.1 us -> 35.5 us  [the longest x1 15.6 us: encode(): pl.pallas_call(encode_body, out_shape=jax.ShapeDtypeStruct(sent, BF16), g...]
    ppermute x6, waiting for transfers between devices: 1.34 us -> 6.84 us  [swap(): return lax.ppermute(x, 'mp', SWAP)]
    all_to_all x2 -> x1, waiting for transfers between devices: 48.8 us -> 52.3 us  [per_device(): lax.all_to_all(slot_sums, ('band', 'mp'), split_axis=0, concat_axis=0, ti...]
    all_to_all x1, starting transfers between devices: 5.99 us -> 7.92 us  [per_device(): lax.all_to_all(outgoing, ('band', 'mp'), split_axis=0, concat_axis=0, til...]
  transfers between devices with their start and end apart: 9 -> 8, of which waited for: 3 -> 5; matrix products, arithmetic and copies ran while one was open for 3% -> 1% of each run, Pallas kernels for 10% -> 0%
where the time goes in v2:
time: 170 us; the launch traced here: 169 us
  waiting for transfers between devices  109 us (64%)
  Pallas kernels  35.5 us (21%)
  starting transfers between devices  20.8 us (12%)
  local copies, waits for them, and re-layouts  2.83 us (2%)
    all_to_all x1, waiting for transfers between devices, per_device(): lax.all_to_all(slot_sums, ('band', 'mp'), split_axis=0, concat_axis=0, ti...  52.3 us
    all_to_all x1, waiting for transfers between devices, per_device(): lax.all_to_all(outgoing, ('band', 'mp'), split_axis=0, concat_axis=0, til...  50.3 us
    pallas_call x1, Pallas kernels, encode(): pl.pallas_call(encode_body, out_shape=jax.ShapeDtypeStruct(sent, BF16), g...  15.6 us
    all_to_all x1, starting transfers between devices, per_device(): lax.all_to_all(slot_sums, ('band', 'mp'), split_axis=0, concat_axis=0, ti...  11.6 us
    pallas_call x1, Pallas kernels, decode(): pl.pallas_call(decode_body, out_shape=jax.ShapeDtypeStruct(grid_blocks.sh...  11.6 us
    pallas_call x1, Pallas kernels, mesh_update(): pl.pallas_call(mesh_body, out_shape=(flat, flat, jax.ShapeDtypeStruct(lea...  8.27 us
    all_to_all x1, starting transfers between devices, per_device(): lax.all_to_all(outgoing, ('band', 'mp'), split_axis=0, concat_axis=0, til...  7.92 us
    ppermute x6, waiting for transfers between devices, swap(): return lax.ppermute(x, 'mp', SWAP)  6.84 us
  transfers between devices with their start and end apart: 8, of which 5 were waited for; matrix products, arithmetic and copies ran while one was open for 1% of the time, Pallas kernels for 0%

profile of v2, /device:TPU:0, one launch (start us, length us, event | category | flops | bytes accessed | tf_op | source)
XLA Modules:
  0.0 169.5 jit_solution(853106740439378148)
XLA Ops:
  0.6 0.1 collective-permute-start
  0.7 4.4 %collective-permute-done.other_hbm = bf16[4096,256]{1,0:T(8,128)(2,1)S(1)} collective-permute-done((bf16[4096,256]{1,0:T(8,128)(2,1)}, bf16[4096,256]{1,0:T(8,128)(2,1)S(1)}, u32[]{:S(2)}, u32[]{:S(2)}) %collective-permute-start) | collective-permute-done | bytes 2097184 | tf_op jit(solution)/shard_map/ppermute | solution.py:348
  5.1 1.3 copy-done
  6.4 15.6 %encode.1 = bf16[128,136,128]{2,1,0:T(8,128)(2,1)} custom-call(s32[192]{0:T(256)} %slot_ref.2, s32[192]{0:T(256)} %source_ref.1, s32[64]{0:T(128)} %bitcast.28, s32[1]{0:T(128)} %bitcast.core_ref, bf16[4096,256]{1,0:T(8,128)(2,1)} %own_hbm.1, bf16[4096,256]{1,0:T(8,128)(2,1)} %copy-done, bf16[512,256]{1,0:T(8,128)(2,1)} %weight_hbm.1, ...), custom_call_target="tpu_custom_call" | custom-call | flops 1610612736 | bytes 16777216 | tf_op jit(solution)/shard_map/encode/pallas_call | solution.py:126
  22.0 0.0 copy-start.2
  22.0 0.0 copy-start.4
  22.1 0.0 copy-start.5
  22.1 0.0 copy-start.8
  22.1 11.6 %all-to-all-start = ((bf16[128,136,128]{2,1,0:T(8,128)(2,1)}), bf16[128,136,128]{2,1,0:T(8,128)(2,1)}, u32[]{:S(2)}, u32[]{:S(2)}) async-start(bf16[128,136,128]{2,1,0:T(8,128)(2,1)} %encode.1), calls=%async_computation | async-start | bytes 8912896 | tf_op jit(solution)/shard_map/all_to_all | solution.py:385
  33.7 0.1 copy.20
  33.8 0.1 collective-permute-start.4
  33.9 0.5 collective-permute-start.2
  34.4 0.1 collective-permute-start.3
  34.5 0.7 constant_dynamic-slice_fusion
  35.2 0.4 collective-permute-start.1
  35.6 1.2 collective-permute-done.1.other_hbm
  36.8 52.3 %all-to-all-done.arrived_hbm = bf16[128,136,128]{2,1,0:T(8,128)(2,1)} async-done(((bf16[128,136,128]{2,1,0:T(8,128)(2,1)}), bf16[128,136,128]{2,1,0:T(8,128)(2,1)}, u32[]{:S(2)}, u32[]{:S(2)}) %all-to-all-start) | async-done | bytes 4456480 | tf_op jit(solution)/shard_map/all_to_all | solution.py:385
  89.1 8.3 %mesh_update.1 = (bf16[256,256]{1,0:T(8,128)(2,1)}, bf16[256,256]{1,0:T(8,128)(2,1)}, bf16[128,64,256]{2,1,0:T(8,128)(2,1)}) custom-call(s32[1]{0:T(128)} %bitcast.core_ref, bf16[128,136,128]{2,1,0:T(8,128)(2,1)} %all-to-all-done.arrived_hbm, bf16[256,256]{1,0:T(8,128)(2,1)} %bitcast.22, bf16[256,256]{1,0:T(8,128)(2,1)} %copy-done.9, ...), custom_call_target="tpu_custom_call" | custom-call | flops 1000000000 | bytes 12582912 | tf_op jit(solution)/shard_map/mesh_update/pallas_call | solution.py:243
  97.4 7.9 %all-to-all-start.1 = ((bf16[128,64,256]{2,1,0:T(8,128)(2,1)}), bf16[128,64,256]{2,1,0:T(8,128)(2,1)}, u32[]{:S(2)}, u32[]{:S(2)}) async-start(bf16[128,64,256]{2,1,0:T(8,128)(2,1)} %get-tuple-element.5), calls=%async_computation.1 | async-start | bytes 8388608 | tf_op jit(solution)/shard_map/all_to_all | solution.py:394
  105.4 0.1 collective-permute-start.5
  105.5 1.3 collective-permute-done.5
  106.8 0.7 copy.17
  107.6 50.3 %all-to-all-done.1 = bf16[128,64,256]{2,1,0:T(8,128)(2,1)} async-done(((bf16[128,64,256]{2,1,0:T(8,128)(2,1)}), bf16[128,64,256]{2,1,0:T(8,128)(2,1)}, u32[]{:S(2)}, u32[]{:S(2)}) %all-to-all-start.1) | async-done | bytes 4194336 | tf_op jit(solution)/shard_map/all_to_all | solution.py:394
  157.8 11.6 %decode.1 = bf16[32,128,256]{2,1,0:T(8,128)(2,1)} custom-call(s32[192]{0:T(256)} %slot_ref.3, s32[192]{0:T(256)} %target_ref.1, bf16[64,128,256]{2,1,0:T(8,128)(2,1)} %bitcast.5.picked_hbm, bf16[32,128,256]{2,1,0:T(8,128)(2,1)} %bitcast.17, bf16[192,128,128]{2,1,0:T(8,128)(2,1)} %tiles_hbm.3), custom_call_target="tpu_custom_call" | custom-call | flops 1610612736 | bytes 16777216 | tf_op jit(solution)/shard_map/decode/pallas_call | solution.py:323
  (24 shorter events, 0.1 us)
Async XLA Ops:
  0.6 4.5 %collective-permute-start = (bf16[4096,256]{1,0:T(8,128)(2,1)}, bf16[4096,256]{1,0:T(8,128)(2,1)S(1)}, u32[]{:S(2)}, u32[]{:S(2)}) collective-permute-start(bf16[4096,256]{1,0:T(8,128)(2,1)} %own_hbm.1), channel_id=1, source_target_pairs={{0,1},{1,0},{2,3},{3,2},{4,5},{5,4},{6,7},{7,6},{8,9},{9,8},{10,11... | collective-permute-start | bytes 6291464 | tf_op jit(solution)/shard_map/ppermute | solution.py:348
  5.1 1.3 copy-start
  22.0 11.7 %copy-start.2 = (bf16[256,2,512]{2,1,0:T(2,128)(2,1)S(1)}, bf16[256,2,512]{2,1,0:T(2,128)(2,1)}, u32[]{:S(2)}) copy-start(bf16[256,2,512]{2,1,0:T(2,128)(2,1)} %param.18) | copy-start | bytes 1572868
  22.0 11.9 %copy-start.4 = (bf16[512,256]{1,0:T(8,128)(2,1)S(1)}, bf16[512,256]{1,0:T(8,128)(2,1)}, u32[]{:S(2)}) copy-start(bf16[512,256]{1,0:T(8,128)(2,1)} %refs_0_.1) | copy-start | bytes 786436
  22.1 12.4 %copy-start.5 = (bf16[512,256]{1,0:T(8,128)(2,1)S(1)}, bf16[512,256]{1,0:T(8,128)(2,1)}, u32[]{:S(2)}) copy-start(bf16[512,256]{1,0:T(8,128)(2,1)} %refs_2_.1) | copy-start | bytes 786436
  22.1 12.5 %copy-start.8 = (bf16[512,256]{1,0:T(8,128)(2,1)S(1)}, bf16[512,256]{1,0:T(8,128)(2,1)}, u32[]{:S(2)}) copy-start(bf16[512,256]{1,0:T(8,128)(2,1)} %param.14) | copy-start | bytes 786436
  22.1 67.0 %all-to-all-start = ((bf16[128,136,128]{2,1,0:T(8,128)(2,1)}), bf16[128,136,128]{2,1,0:T(8,128)(2,1)}, u32[]{:S(2)}, u32[]{:S(2)}) async-start(bf16[128,136,128]{2,1,0:T(8,128)(2,1)} %encode.1), calls=%async_computation | async-start | bytes 8912896 | tf_op jit(solution)/shard_map/all_to_all | solution.py:385
  33.8 55.3 %copy-start.1 = (bf16[32,8,2,512]{3,1,2,0:T(8,128)(2,1)}, bf16[32,8,2,512]{3,1,2,0:T(8,128)(2,1)S(1)}, u32[]{:S(2)}) copy-start(bf16[32,8,2,512]{3,1,2,0:T(8,128)(2,1)S(1)} %copy.20) | copy-start | bytes 1572868
  33.8 3.0 %collective-permute-start.4 = (bf16[256,1024]{1,0:T(8,128)(2,1)S(1)}, bf16[256,1024]{1,0:T(8,128)(2,1)S(1)}, u32[]{:S(2)}, u32[]{:S(2)}) collective-permute-start(bf16[256,1024]{1,0:T(8,128)(2,1)S(1)} %bitcast.19), channel_id=1, source_target_pairs={{0,1},{1,0},{2,3},{3,2},{4,5},{5,4},{6,7},{7,6},{8,9},{9,8},{10,11... | collective-permute-start | bytes 1572872 | tf_op jit(solution)/shard_map/ppermute | solution.py:348
  33.9 2.8 %collective-permute-start.2 = (bf16[512,256]{1,0:T(8,128)(2,1)S(1)}, bf16[512,256]{1,0:T(8,128)(2,1)S(1)}, u32[]{:S(2)}, u32[]{:S(2)}) collective-permute-start(bf16[512,256]{1,0:T(8,128)(2,1)S(1)} %copy-done.4), channel_id=1, source_target_pairs={{0,1},{1,0},{2,3},{3,2},{4,5},{5,4},{6,7},{7,6},{8,9},{9,8},{10,11... | collective-permute-start | bytes 786440 | tf_op jit(solution)/shard_map/ppermute | solution.py:348
  34.4 2.3 %collective-permute-start.3 = (bf16[512,256]{1,0:T(8,128)(2,1)S(1)}, bf16[512,256]{1,0:T(8,128)(2,1)S(1)}, u32[]{:S(2)}, u32[]{:S(2)}) collective-permute-start(bf16[512,256]{1,0:T(8,128)(2,1)S(1)} %copy-done.5), channel_id=1, source_target_pairs={{0,1},{1,0},{2,3},{3,2},{4,5},{5,4},{6,7},{7,6},{8,9},{9,8},{10,11... | collective-permute-start | bytes 786440 | tf_op jit(solution)/shard_map/ppermute | solution.py:348
  35.2 1.6 collective-permute-start.1
  36.8 52.3 %copy-start.9 = (bf16[256,256]{1,0:T(8,128)(2,1)}, bf16[256,256]{1,0:T(8,128)(2,1)S(1)}, u32[]{:S(2)}) copy-start(bf16[256,256]{1,0:T(8,128)(2,1)S(1)} %collective-permute-done.1.other_hbm) | copy-start | bytes 393220
  36.8 52.3 %copy-start.6 = (bf16[512,256]{1,0:T(8,128)(2,1)}, bf16[512,256]{1,0:T(8,128)(2,1)S(1)}, u32[]{:S(2)}) copy-start(bf16[512,256]{1,0:T(8,128)(2,1)S(1)} %collective-permute-done.2.refs_1_) | copy-start | bytes 786436
  36.8 52.3 %copy-start.7 = (bf16[512,256]{1,0:T(8,128)(2,1)}, bf16[512,256]{1,0:T(8,128)(2,1)S(1)}, u32[]{:S(2)}) copy-start(bf16[512,256]{1,0:T(8,128)(2,1)S(1)} %collective-permute-done.3.refs_3_) | copy-start | bytes 786436
  36.8 52.3 %copy-start.3 = (bf16[256,1024]{1,0:T(8,128)(2,1)}, bf16[256,1024]{1,0:T(8,128)(2,1)S(1)}, u32[]{:S(2)}) copy-start(bf16[256,1024]{1,0:T(8,128)(2,1)S(1)} %collective-permute-done.4.refs_5_) | copy-start | bytes 1572868
  97.4 7.9 %copy-start.11 = (bf16[256,256]{1,0:T(8,128)(2,1)S(1)}, bf16[256,256]{1,0:T(8,128)(2,1)}, u32[]{:S(2)}) copy-start(bf16[256,256]{1,0:T(8,128)(2,1)} %get-tuple-element.7) | copy-start | bytes 393220
  97.4 9.4 %copy-start.10 = (bf16[256,256]{1,0:T(8,128)(2,1)S(1)}, bf16[256,256]{1,0:T(8,128)(2,1)}, u32[]{:S(2)}) copy-start(bf16[256,256]{1,0:T(8,128)(2,1)} %get-tuple-element.6) | copy-start | bytes 393220
  97.4 60.4 %all-to-all-start.1 = ((bf16[128,64,256]{2,1,0:T(8,128)(2,1)}), bf16[128,64,256]{2,1,0:T(8,128)(2,1)}, u32[]{:S(2)}, u32[]{:S(2)}) async-start(bf16[128,64,256]{2,1,0:T(8,128)(2,1)} %get-tuple-element.5), calls=%async_computation.1 | async-start | bytes 8388608 | tf_op jit(solution)/shard_map/all_to_all | solution.py:394
  105.4 1.4 collective-permute-start.5

commit v3 on v2

--- a/solution.py
+++ b/solution.py
@@ -32,26 +32,33 @@
         rows = pl.ds(k * size, size)
         return pltpu.make_async_copy(source.at[rows], target.at[rows], semaphores.at[k])
 
-    for k in range(count):
-        piece(k).start()
-    return lambda k: piece(k).wait()
+    return lambda k: piece(k).start(), lambda k: piece(k).wait()
 
 
 def hbm():
-    return pl.BlockSpec(memory_space=pl.ANY)
-
-
-PARAMS = pltpu.CompilerParams(vmem_limit_bytes=60 * MB)
+    return pl.BlockSpec(memory_space=pltpu.HBM)
+
+
+def stay(*arrays):
+    return tuple(pltpu.with_memory_space_constraint(a, pltpu.HBM) for a in arrays)
+
+
+def vmem():
+    return pl.BlockSpec(memory_space=pltpu.VMEM)
+
+
+WIDE = pltpu.CompilerParams(vmem_limit_bytes=56 * MB)
+NARROW = pltpu.CompilerParams(vmem_limit_bytes=44 * MB)
 
 
 PIECES = 4
-UNROLL = 16
+UNROLL = 48
 TAG = 8
 
 
 def encode_body(
-    slot_ref, source_ref, link_ref, core_ref, own_hbm, other_hbm, weight_hbm, tiles_hbm, out_hbm,
-    own, other, weight, tiles, message, acc, out, own_sem, other_sem, weight_sem, tiles_sem, out_sem,
+    slot_ref, source_ref, link_ref, core_ref, own_hbm, other, weight, tiles_hbm, out_hbm,
+    own, tiles, message, acc, out, own_sem, tiles_sem, out_sem,
 ):
     core = core_ref[0]
     blocks, edge, width = message.shape
@@ -59,27 +66,26 @@
     count = tiles.shape[0]
     rows = edge // 2
     lanes = out.shape[2]
-    weight_ready = fetch(weight_hbm, weight, weight_sem, 1)
-    own_ready = fetch(own_hbm, own, own_sem, PIECES)
-    other_ready = fetch(other_hbm, other, other_sem, PIECES)
-    tiles_ready = fetch(tiles_hbm, tiles, tiles_sem, PIECES)
-    weight_ready(0)
-
-    inner = 2 * edge
+    own_start, own_ready = fetch(own_hbm, own, own_sem, PIECES)
+    tiles_start, tiles_ready = fetch(tiles_hbm, tiles, tiles_sem, PIECES)
+    for piece in range(PIECES):
+        own_start(piece)
+
+    inner = 8 * edge
     per = blocks * edge // inner // PIECES
     cleared = slots // (per * PIECES)
 
     @pl.loop(0, PIECES)
     def _(piece):
         own_ready(piece)
-        other_ready(piece)
+        tiles_start(piece)
 
         @pl.loop(0, per)
         def _(j):
             step = piece * per + j
             at = pl.ds(pl.multiple_of(step * inner, inner), inner)
             z = dot(own[at, :], weight[half(core, width), :]) + dot(other[at, :], weight[half(1 - core, width), :])
-            message[pl.ds(step * 2, 2)] = silu(z).astype(BF16).reshape(2, edge, width)
+            message[pl.ds(step * 8, 8)] = silu(z).astype(BF16).reshape(8, edge, width)
             acc[pl.ds(step * cleared, cleared)] = jnp.zeros((cleared, edge, width), F32)
 
     @pl.loop(0, PIECES)
@@ -125,58 +131,47 @@
     dma = pltpu.SemaphoreType.DMA
     return pl.pallas_call(
         encode_body,
-        out_shape=jax.ShapeDtypeStruct(sent, BF16),
+        out_shape=pltpu.HBM(sent, BF16),
         grid_spec=pltpu.PrefetchScalarGridSpec(
             num_scalar_prefetch=4,
-            in_specs=[hbm()] * 4,
+            in_specs=[hbm(), vmem(), vmem(), hbm()],
             out_specs=hbm(),
             scratch_shapes=[
                 pltpu.VMEM(own.shape, BF16),
-                pltpu.VMEM(other.shape, BF16),
-                pltpu.VMEM(weight.shape, BF16),
                 pltpu.VMEM(tiles.shape, BF16),
                 pltpu.VMEM((own.shape[0] // edge, edge, width), BF16),
                 pltpu.VMEM((slots, edge, width), F32),
                 pltpu.VMEM(sent, BF16),
-                dma((PIECES,)),
-                dma((PIECES,)),
-                dma((1,)),
-                dma((PIECES,)),
-                dma((PIECES,)),
+                *[dma((PIECES,))] * 3,
             ],
         ),
-        compiler_params=PARAMS,
+        compiler_params=WIDE,
         cost_estimate=pl.CostEstimate(
             flops=2 * count * edge * edge * width, bytes_accessed=16 * MB, transcendentals=own.shape[0] * width
         ),
         name="encode",
-    )(slot, source, link, core, own, other, weight, tiles)
-
-
-def mesh_body(core_ref, arrived_hbm, mesh_hbm, other_hbm, *refs):
-    weights_hbm, refs = refs[:6], refs[6:]
-    keep, send, outgoing_hbm, arrived, mine_ref, theirs_ref = refs[:6]
-    weights, refs = refs[6:12], refs[12:]
-    acc, state, source, outgoing, block_ref, arrived_sem, small_sem, out_sem = refs
+    )(slot, source, link, core, *stay(own), other, weight, *stay(tiles))
+
+
+def mesh_body(
+    core_ref, arrived_hbm, mine_ref, theirs_ref, self_w, self_o, pool_w, pool_o, out_w, out_o, keep, send,
+    outgoing_hbm, arrived, acc, state, source, outgoing, block_ref, arrived_sem, out_sem,
+):
     core = core_ref[0]
     bands = arrived.shape[0] // 2
     lanes = arrived.shape[2]
     rows = acc.shape[1]
     width = 2 * lanes
-    ready = fetch(arrived_hbm, arrived, arrived_sem, PIECES)
-    small = [
-        pltpu.make_async_copy(x, y, small_sem.at[k])
-        for k, (x, y) in enumerate(zip((mesh_hbm, other_hbm, *weights_hbm), (mine_ref, theirs_ref, *weights)))
-    ]
-    for copy in small:
-        copy.start()
+    arrived_start, ready = fetch(arrived_hbm, arrived, arrived_sem, PIECES)
+    for piece in range(PIECES):
+        arrived_start(piece)
     acc[...] = jnp.zeros(acc.shape, F32)
 
     @pl.loop(0, PIECES)
     def _(piece):
         ready(piece)
 
-        @pl.loop(0, bands // PIECES, unroll=4)
+        @pl.loop(0, bands // PIECES, unroll=16)
         def _(j):
             band = piece * (bands // PIECES) + j
             tag = arrived[2 * band, 2 * rows :, :].astype(F32)
@@ -194,9 +189,6 @@
                         2 * band + part, column * rows : (column + 1) * rows, :
                     ].astype(F32)
 
-    for copy in small:
-        copy.wait()
-    self_w, self_o, pool_w, pool_o, out_w, out_o = weights
     pooled = acc[...].reshape(-1, 2 * width).astype(BF16)
     mine, theirs = mine_ref[...], theirs_ref[...]
     hidden = []
@@ -239,33 +231,28 @@
     flat = jax.ShapeDtypeStruct(mesh.shape, BF16)
     leaving = (pieces, rows, width)
     dma = pltpu.SemaphoreType.DMA
-    vmem = pl.BlockSpec(memory_space=pltpu.VMEM)
     return pl.pallas_call(
         mesh_body,
-        out_shape=(flat, flat, jax.ShapeDtypeStruct(leaving, BF16)),
+        out_shape=(flat, flat, pltpu.HBM(leaving, BF16)),
         grid_spec=pltpu.PrefetchScalarGridSpec(
             num_scalar_prefetch=1,
-            in_specs=[hbm()] * 9,
-            out_specs=[vmem, vmem, hbm()],
+            in_specs=[hbm()] + [vmem()] * 8,
+            out_specs=[vmem(), vmem(), hbm()],
             scratch_shapes=[
                 pltpu.VMEM(arrived.shape, BF16),
-                pltpu.VMEM(mesh.shape, BF16),
-                pltpu.VMEM(mesh.shape, BF16),
-                *[pltpu.VMEM(w.shape, BF16) for w in weights],
                 pltpu.VMEM((blocks, rows, 2 * width), F32),
                 pltpu.VMEM((blocks * rows, 2 * width), F32),
                 pltpu.VMEM((blocks, rows, 2 * width), BF16),
                 pltpu.VMEM(leaving, BF16),
                 pltpu.SMEM((pieces // 2,), jnp.int32),
                 dma((PIECES,)),
-                dma((8,)),
                 dma((PIECES,)),
             ],
         ),
-        compiler_params=PARAMS,
+        compiler_params=NARROW,
         cost_estimate=pl.CostEstimate(flops=10**9, bytes_accessed=12 * MB, transcendentals=1 << 17),
         name="mesh_update",
-    )(core, arrived, mesh, mesh_other, *weights)
+    )(core, *stay(arrived), mesh, mesh_other, *weights)
 
 
 def decode_body(
@@ -274,10 +261,14 @@
 ):
     count = tiles.shape[0]
     blocks = acc.shape[0]
-    start_ready = fetch(grid_hbm, start, start_sem, PIECES)
-    picked_ready = fetch(picked_hbm, picked, picked_sem, PIECES)
-    tiles_ready = fetch(tiles_hbm, tiles, tiles_sem, PIECES)
+    start_start, start_ready = fetch(grid_hbm, start, start_sem, PIECES)
+    picked_start, picked_ready = fetch(picked_hbm, picked, picked_sem, PIECES)
+    tiles_start, tiles_ready = fetch(tiles_hbm, tiles, tiles_sem, PIECES)
     per = blocks // PIECES
+    for begin in (start_start, picked_start):
+        for piece in range(PIECES):
+            begin(piece)
+    tiles_start(0)
 
     @pl.loop(0, PIECES)
     def _(piece):
@@ -289,6 +280,8 @@
 
     for piece in range(PIECES):
         picked_ready(piece)
+    for piece in range(1, PIECES):
+        tiles_start(piece)
 
     @pl.loop(0, PIECES)
     def _(piece):
@@ -336,12 +329,12 @@
                 *[dma((PIECES,))] * 4,
             ],
         ),
-        compiler_params=PARAMS,
+        compiler_params=WIDE,
         cost_estimate=pl.CostEstimate(
             flops=2 * count * edge * edge * width, bytes_accessed=16 * MB, transcendentals=0
         ),
         name="decode",
-    )(slot, target, picked, grid_blocks, tiles)
+    )(slot, target, *stay(picked, grid_blocks, tiles))
 
 
 def swap(x):

time: 170 us -> 161 us (0.947)
  Pallas kernels: 35.5 us -> 27 us
    pallas_call x2, Pallas kernels: 23.9 us -> 17.5 us  [the longest x1 11.8 us: encode(): pl.pallas_call(encode_body, out_shape=pltpu.HBM(sent, BF16), grid_spec=pl...]
    pallas_call x1, Pallas kernels: 11.6 us -> 9.49 us  [decode(): pl.pallas_call(decode_body, out_shape=jax.ShapeDtypeStruct(grid_blocks.sh...]
where the time goes in v3:
time: 161 us
  waiting for transfers between devices  110 us (68%)
  Pallas kernels  27 us (17%)
  starting transfers between devices  20.9 us (13%)
  local copies, waits for them, and re-layouts  2.15 us (1%)
    all_to_all x1, waiting for transfers between devices, per_device(): lax.all_to_all(slot_sums, ('band', 'mp'), split_axis=0, concat_axis=0, ti...  52.3 us
    all_to_all x1, waiting for transfers between devices, per_device(): lax.all_to_all(outgoing, ('band', 'mp'), split_axis=0, concat_axis=0, til...  50.3 us
    pallas_call x1, Pallas kernels, encode(): pl.pallas_call(encode_body, out_shape=pltpu.HBM(sent, BF16), grid_spec=pl...  11.8 us
    all_to_all x1, starting transfers between devices, per_device(): lax.all_to_all(slot_sums, ('band', 'mp'), split_axis=0, concat_axis=0, ti...  11.6 us
    pallas_call x1, Pallas kernels, decode(): pl.pallas_call(decode_body, out_shape=jax.ShapeDtypeStruct(grid_blocks.sh...  9.49 us
    all_to_all x1, starting transfers between devices, per_device(): lax.all_to_all(outgoing, ('band', 'mp'), split_axis=0, concat_axis=0, til...  7.92 us
    ppermute x6, waiting for transfers between devices, swap(): return lax.ppermute(x, 'mp', SWAP)  7.41 us
    pallas_call x1, Pallas kernels, mesh_update(): pl.pallas_call(mesh_body, out_shape=(flat, flat, pltpu.HBM(leaving, BF16)...  5.68 us
  transfers between devices with their start and end apart: 8, of which 5 were waited for; matrix products, arithmetic and copies ran while one was open for 1% of the time, Pallas kernels for 0%

profile of v3, /device:TPU:0, one launch (start us, length us, event | category | flops | bytes accessed | tf_op | source)
XLA Modules:
  0.0 160.9 jit_solution(7579141522716117141)
XLA Ops:
  0.6 0.1 collective-permute-start
  0.7 4.4 %collective-permute-done.other = bf16[4096,256]{1,0:T(8,128)(2,1)S(1)} collective-permute-done((bf16[4096,256]{1,0:T(8,128)(2,1)}, bf16[4096,256]{1,0:T(8,128)(2,1)S(1)}, u32[]{:S(2)}, u32[]{:S(2)}) %collective-permute-start) | collective-permute-done | bytes 2097184 | tf_op jit(solution)/shard_map/ppermute | solution.py:341
  5.1 1.3 copy-done.2
  6.4 11.8 %encode.1 = bf16[128,136,128]{2,1,0:T(8,128)(2,1)} custom-call(s32[192]{0:T(256)} %slot_ref.2, s32[192]{0:T(256)} %source_ref.1, s32[64]{0:T(128)} %bitcast.28, s32[1]{0:T(128)} %bitcast.core_ref, bf16[4096,256]{1,0:T(8,128)(2,1)} %own_hbm.1, bf16[4096,256]{1,0:T(8,128)(2,1)} %copy-done.2, bf16[512,256]{1,0:T(8,128)(2,1)} %weight.1, ...), custom_call_target="tpu_custom_call" | custom-call | flops 1610612736 | bytes 16777216 | tf_op jit(solution)/shard_map/encode/pallas_call | solution.py:132
  18.2 0.0 copy-start.3
  18.2 0.0 copy-start
  18.2 0.0 copy-start.1
  18.2 0.0 copy-start.4
  18.2 11.6 %all-to-all-start = ((bf16[128,136,128]{2,1,0:T(8,128)(2,1)}), bf16[128,136,128]{2,1,0:T(8,128)(2,1)}, u32[]{:S(2)}, u32[]{:S(2)}) async-start(bf16[128,136,128]{2,1,0:T(8,128)(2,1)} %encode.1), calls=%async_computation | async-start | bytes 8912896 | tf_op jit(solution)/shard_map/all_to_all | solution.py:378
  29.9 0.1 copy.20
  30.0 0.1 collective-permute-start.4
  30.1 0.5 collective-permute-start.2
  30.6 0.1 collective-permute-start.3
  30.7 0.5 collective-permute-start.1
  31.2 1.7 %collective-permute-done.1.theirs_ref = bf16[256,256]{1,0:T(8,128)(2,1)S(1)} collective-permute-done((bf16[256,256]{1,0:T(8,128)(2,1)S(1)}, bf16[256,256]{1,0:T(8,128)(2,1)S(1)}, u32[]{:S(2)}, u32[]{:S(2)}) %collective-permute-start.1) | collective-permute-done | bytes 131104 | tf_op jit(solution)/shard_map/ppermute | solution.py:341
  32.9 0.0 collective-permute-done.3.pool_o
  32.9 52.3 %all-to-all-done.arrived_hbm = bf16[128,136,128]{2,1,0:T(8,128)(2,1)} async-done(((bf16[128,136,128]{2,1,0:T(8,128)(2,1)}), bf16[128,136,128]{2,1,0:T(8,128)(2,1)}, u32[]{:S(2)}, u32[]{:S(2)}) %all-to-all-start) | async-done | bytes 4456480 | tf_op jit(solution)/shard_map/all_to_all | solution.py:378
  85.3 5.7 %mesh_update.1 = (bf16[256,256]{1,0:T(8,128)(2,1)S(1)}, bf16[256,256]{1,0:T(8,128)(2,1)S(1)}, bf16[128,64,256]{2,1,0:T(8,128)(2,1)}) custom-call(s32[1]{0:T(128)} %bitcast.core_ref, bf16[128,136,128]{2,1,0:T(8,128)(2,1)} %all-to-all-done.arrived_hbm, bf16[256,256]{1,0:T(8,128)(2,1)S(1)} %bitcast.19, bf16[256,256]{1,0:T(8,128)(2,1)S(1)} %collective-permute-done.1.theirs_ref, ...), custom_call_target="tpu_custom_call" | custom-call | flops 1000000000 | bytes 12582912 | tf_op jit(solution)/shard_map/mesh_update/pallas_call | solution.py:234
  91.0 7.9 %all-to-all-start.1 = ((bf16[128,64,256]{2,1,0:T(8,128)(2,1)}), bf16[128,64,256]{2,1,0:T(8,128)(2,1)}, u32[]{:S(2)}, u32[]{:S(2)}) async-start(bf16[128,64,256]{2,1,0:T(8,128)(2,1)} %get-tuple-element.5), calls=%async_computation.1 | async-start | bytes 8388608 | tf_op jit(solution)/shard_map/all_to_all | solution.py:387
  98.9 0.1 collective-permute-start.5
  99.0 1.3 collective-permute-done.5
  100.4 0.7 copy.17
  101.1 50.3 %all-to-all-done.1 = bf16[128,64,256]{2,1,0:T(8,128)(2,1)} async-done(((bf16[128,64,256]{2,1,0:T(8,128)(2,1)}), bf16[128,64,256]{2,1,0:T(8,128)(2,1)}, u32[]{:S(2)}, u32[]{:S(2)}) %all-to-all-start.1) | async-done | bytes 4194336 | tf_op jit(solution)/shard_map/all_to_all | solution.py:387
  151.4 9.5 %decode.1 = bf16[32,128,256]{2,1,0:T(8,128)(2,1)} custom-call(s32[192]{0:T(256)} %slot_ref.3, s32[192]{0:T(256)} %target_ref.1, bf16[64,128,256]{2,1,0:T(8,128)(2,1)} %bitcast.5.picked_hbm, bf16[32,128,256]{2,1,0:T(8,128)(2,1)} %bitcast.20, bf16[192,128,128]{2,1,0:T(8,128)(2,1)} %tiles_hbm.3), custom_call_target="tpu_custom_call" | custom-call | flops 1610612736 | bytes 16777216 | tf_op jit(solution)/shard_map/decode/pallas_call | solution.py:316
  (10 shorter events, 0.1 us)
Async XLA Ops:
  0.6 4.5 %collective-permute-start = (bf16[4096,256]{1,0:T(8,128)(2,1)}, bf16[4096,256]{1,0:T(8,128)(2,1)S(1)}, u32[]{:S(2)}, u32[]{:S(2)}) collective-permute-start(bf16[4096,256]{1,0:T(8,128)(2,1)} %own_hbm.1), channel_id=1, source_target_pairs={{0,1},{1,0},{2,3},{3,2},{4,5},{5,4},{6,7},{7,6},{8,9},{9,8},{10,11... | collective-permute-start | bytes 6291464 | tf_op jit(solution)/shard_map/ppermute | solution.py:341
  5.1 1.3 copy-start.2
  18.2 11.7 %copy-start.3 = (bf16[256,2,512]{2,1,0:T(2,128)(2,1)S(1)}, bf16[256,2,512]{2,1,0:T(2,128)(2,1)}, u32[]{:S(2)}) copy-start(bf16[256,2,512]{2,1,0:T(2,128)(2,1)} %param.18) | copy-start | bytes 1572868
  18.2 11.9 %copy-start = (bf16[512,256]{1,0:T(8,128)(2,1)S(1)}, bf16[512,256]{1,0:T(8,128)(2,1)}, u32[]{:S(2)}) copy-start(bf16[512,256]{1,0:T(8,128)(2,1)} %self_w.1) | copy-start | bytes 786436
  18.2 12.4 %copy-start.1 = (bf16[512,256]{1,0:T(8,128)(2,1)S(1)}, bf16[512,256]{1,0:T(8,128)(2,1)}, u32[]{:S(2)}) copy-start(bf16[512,256]{1,0:T(8,128)(2,1)} %pool_w.1) | copy-start | bytes 786436
  18.2 12.4 %copy-start.4 = (bf16[512,256]{1,0:T(8,128)(2,1)S(1)}, bf16[512,256]{1,0:T(8,128)(2,1)}, u32[]{:S(2)}) copy-start(bf16[512,256]{1,0:T(8,128)(2,1)} %param.14) | copy-start | bytes 786436
  18.2 67.0 %all-to-all-start = ((bf16[128,136,128]{2,1,0:T(8,128)(2,1)}), bf16[128,136,128]{2,1,0:T(8,128)(2,1)}, u32[]{:S(2)}, u32[]{:S(2)}) async-start(bf16[128,136,128]{2,1,0:T(8,128)(2,1)} %encode.1), calls=%async_computation | async-start | bytes 8912896 | tf_op jit(solution)/shard_map/all_to_all | solution.py:378
  30.0 2.9 %collective-permute-start.4 = (bf16[256,1024]{1,0:T(8,128)(2,1)S(1)}, bf16[256,1024]{1,0:T(8,128)(2,1)S(1)}, u32[]{:S(2)}, u32[]{:S(2)}) collective-permute-start(bf16[256,1024]{1,0:T(8,128)(2,1)S(1)} %bitcast.17), channel_id=1, source_target_pairs={{0,1},{1,0},{2,3},{3,2},{4,5},{5,4},{6,7},{7,6},{8,9},{9,8},{10,11... | collective-permute-start | bytes 1572872 | tf_op jit(solution)/shard_map/ppermute | solution.py:341
  30.1 2.8 %collective-permute-start.2 = (bf16[512,256]{1,0:T(8,128)(2,1)S(1)}, bf16[512,256]{1,0:T(8,128)(2,1)S(1)}, u32[]{:S(2)}, u32[]{:S(2)}) collective-permute-start(bf16[512,256]{1,0:T(8,128)(2,1)S(1)} %copy-done), channel_id=1, source_target_pairs={{0,1},{1,0},{2,3},{3,2},{4,5},{5,4},{6,7},{7,6},{8,9},{9,8},{10,11... | collective-permute-start | bytes 786440 | tf_op jit(solution)/shard_map/ppermute | solution.py:341
  30.6 2.3 %collective-permute-start.3 = (bf16[512,256]{1,0:T(8,128)(2,1)S(1)}, bf16[512,256]{1,0:T(8,128)(2,1)S(1)}, u32[]{:S(2)}, u32[]{:S(2)}) collective-permute-start(bf16[512,256]{1,0:T(8,128)(2,1)S(1)} %copy-done.1), channel_id=1, source_target_pairs={{0,1},{1,0},{2,3},{3,2},{4,5},{5,4},{6,7},{7,6},{8,9},{9,8},{10,11... | collective-permute-start | bytes 786440 | tf_op jit(solution)/shard_map/ppermute | solution.py:341
  30.7 2.2 %collective-permute-start.1 = (bf16[256,256]{1,0:T(8,128)(2,1)S(1)}, bf16[256,256]{1,0:T(8,128)(2,1)S(1)}, u32[]{:S(2)}, u32[]{:S(2)}) collective-permute-start(bf16[256,256]{1,0:T(8,128)(2,1)S(1)} %bitcast.27), channel_id=1, source_target_pairs={{0,1},{1,0},{2,3},{3,2},{4,5},{5,4},{6,7},{7,6},{8,9},{9,8},{10,11... | collective-permute-start | bytes 393224 | tf_op jit(solution)/shard_map/ppermute | solution.py:341
  91.0 60.4 %all-to-all-start.1 = ((bf16[128,64,256]{2,1,0:T(8,128)(2,1)}), bf16[128,64,256]{2,1,0:T(8,128)(2,1)}, u32[]{:S(2)}, u32[]{:S(2)}) async-start(bf16[128,64,256]{2,1,0:T(8,128)(2,1)} %get-tuple-element.5), calls=%async_computation.1 | async-start | bytes 8388608 | tf_op jit(solution)/shard_map/all_to_all | solution.py:387
  98.9 1.4 collective-permute-start.5

commit v4 on v3

--- a/solution.py
+++ b/solution.py
@@ -47,8 +47,30 @@
     return pl.BlockSpec(memory_space=pltpu.VMEM)
 
 
-WIDE = pltpu.CompilerParams(vmem_limit_bytes=56 * MB)
 NARROW = pltpu.CompilerParams(vmem_limit_bytes=44 * MB)
+
+
+def load_body(count, *refs):
+    sources, targets, semaphores = refs[:count], refs[-count - 1 : -1], refs[-1]
+    copies = [pltpu.make_async_copy(x, y, semaphores.at[k]) for k, (x, y) in enumerate(zip(sources, targets))]
+    for copy in copies:
+        copy.start()
+    for copy in copies:
+        copy.wait()
+
+
+def load(name, arrays, after=()):
+    count = len(arrays)
+    return pl.pallas_call(
+        functools.partial(load_body, count),
+        out_shape=tuple(pltpu.VMEM(a.shape, a.dtype) for a in arrays),
+        in_specs=[hbm()] * (count + len(after)),
+        out_specs=tuple(vmem() for _ in arrays),
+        scratch_shapes=[pltpu.SemaphoreType.DMA((count,))],
+        compiler_params=pltpu.CompilerParams(vmem_limit_bytes=24 * MB),
+        cost_estimate=pl.CostEstimate(flops=0, bytes_accessed=16 * MB, transcendentals=0),
+        name=name,
+    )(*stay(*arrays), *stay(*after))
 
 
 PIECES = 4
@@ -57,8 +79,7 @@
 
 
 def encode_body(
-    slot_ref, source_ref, link_ref, core_ref, own_hbm, other, weight, tiles_hbm, out_hbm,
-    own, tiles, message, acc, out, own_sem, tiles_sem, out_sem,
+    slot_ref, source_ref, link_ref, core_ref, own, other, weight, tiles, out_hbm, message, acc, out, out_sem,
 ):
     core = core_ref[0]
     blocks, edge, width = message.shape
@@ -66,20 +87,12 @@
     count = tiles.shape[0]
     rows = edge // 2
     lanes = out.shape[2]
-    own_start, own_ready = fetch(own_hbm, own, own_sem, PIECES)
-    tiles_start, tiles_ready = fetch(tiles_hbm, tiles, tiles_sem, PIECES)
-    for piece in range(PIECES):
-        own_start(piece)
-
     inner = 8 * edge
     per = blocks * edge // inner // PIECES
     cleared = slots // (per * PIECES)
 
     @pl.loop(0, PIECES)
     def _(piece):
-        own_ready(piece)
-        tiles_start(piece)
-
         @pl.loop(0, per)
         def _(j):
             step = piece * per + j
@@ -90,8 +103,6 @@
 
     @pl.loop(0, PIECES)
     def _(piece):
-        tiles_ready(piece)
-
         @pl.loop(0, count // PIECES // UNROLL)
         def _(j):
             base = piece * (count // PIECES) + j * UNROLL
@@ -134,23 +145,21 @@
         out_shape=pltpu.HBM(sent, BF16),
         grid_spec=pltpu.PrefetchScalarGridSpec(
             num_scalar_prefetch=4,
-            in_specs=[hbm(), vmem(), vmem(), hbm()],
+            in_specs=[vmem()] * 4,
             out_specs=hbm(),
             scratch_shapes=[
-                pltpu.VMEM(own.shape, BF16),
-                pltpu.VMEM(tiles.shape, BF16),
                 pltpu.VMEM((own.shape[0] // edge, edge, width), BF16),
                 pltpu.VMEM((slots, edge, width), F32),
                 pltpu.VMEM(sent, BF16),
-                *[dma((PIECES,))] * 3,
+                dma((PIECES,)),
             ],
         ),
-        compiler_params=WIDE,
+        compiler_params=pltpu.CompilerParams(vmem_limit_bytes=32 * MB),
         cost_estimate=pl.CostEstimate(
             flops=2 * count * edge * edge * width, bytes_accessed=16 * MB, transcendentals=own.shape[0] * width
         ),
         name="encode",
-    )(slot, source, link, core, *stay(own), other, weight, *stay(tiles))
+    )(slot, source, link, core, own, other, weight, tiles)
 
 
 def mesh_body(
@@ -256,32 +265,27 @@
 
 
 def decode_body(
-    slot_ref, target_ref, picked_hbm, grid_hbm, tiles_hbm, out_hbm,
-    picked, start, tiles, acc, out, picked_sem, start_sem, tiles_sem, out_sem,
+    slot_ref, target_ref, picked_hbm, start, tiles_hbm, out_hbm,
+    picked, tiles, acc, out, picked_sem, tiles_sem, out_sem,
 ):
     count = tiles.shape[0]
     blocks = acc.shape[0]
-    start_start, start_ready = fetch(grid_hbm, start, start_sem, PIECES)
     picked_start, picked_ready = fetch(picked_hbm, picked, picked_sem, PIECES)
     tiles_start, tiles_ready = fetch(tiles_hbm, tiles, tiles_sem, PIECES)
     per = blocks // PIECES
-    for begin in (start_start, picked_start):
-        for piece in range(PIECES):
-            begin(piece)
-    tiles_start(0)
-
-    @pl.loop(0, PIECES)
-    def _(piece):
-        start_ready(piece)
-
+    for piece in range(PIECES):
+        picked_start(piece)
+    for piece in range(PIECES):
+        tiles_start(piece)
+
+    @pl.loop(0, PIECES)
+    def _(piece):
         @pl.loop(0, per, unroll=4)
         def _(j):
             acc[piece * per + j] = start[piece * per + j].astype(F32)
 
     for piece in range(PIECES):
         picked_ready(piece)
-    for piece in range(1, PIECES):
-        tiles_start(piece)
 
     @pl.loop(0, PIECES)
     def _(piece):
@@ -318,23 +322,22 @@
         out_shape=jax.ShapeDtypeStruct(grid_blocks.shape, BF16),
         grid_spec=pltpu.PrefetchScalarGridSpec(
             num_scalar_prefetch=2,
-            in_specs=[hbm()] * 3,
+            in_specs=[hbm(), vmem(), hbm()],
             out_specs=hbm(),
             scratch_shapes=[
                 pltpu.VMEM(picked.shape, BF16),
-                pltpu.VMEM(grid_blocks.shape, BF16),
                 pltpu.VMEM(tiles.shape, BF16),
                 pltpu.VMEM(grid_blocks.shape, F32),
                 pltpu.VMEM(grid_blocks.shape, BF16),
-                *[dma((PIECES,))] * 4,
+                *[dma((PIECES,))] * 3,
             ],
         ),
-        compiler_params=WIDE,
+        compiler_params=pltpu.CompilerParams(vmem_limit_bytes=40 * MB),
         cost_estimate=pl.CostEstimate(
             flops=2 * count * edge * edge * width, bytes_accessed=16 * MB, transcendentals=0
         ),
         name="decode",
-    )(slot, target, *stay(picked, grid_blocks, tiles))
+    )(slot, target, *stay(picked), grid_blocks, *stay(tiles))
 
 
 def swap(x):
@@ -372,8 +375,9 @@
     mesh_other = swap(mesh_send)
     self_other, pooled_other, out_other = swap(self_weight), swap(pooled_weight), swap(out_flat)
 
+    own, near_weight, near_tiles = load("load_encode", (grid_nodes, send_weight, encode_tiles))
     slot_sums = encode(
-        grid_nodes, grid_other, send_weight, encode_tiles, encode_source, encode_slot, slot_block[0], core_1, bands
+        own, grid_other, near_weight, near_tiles, encode_source, encode_slot, slot_block[0], core_1, bands
     )
     arrived = lax.all_to_all(slot_sums, ("band", "mp"), split_axis=0, concat_axis=0, tiled=True)
     keep, send, outgoing = mesh_update(
@@ -385,7 +389,8 @@
         mesh_blocks,
     )
     returned = lax.all_to_all(outgoing, ("band", "mp"), split_axis=0, concat_axis=0, tiled=True)
-    came = swap(send).reshape(mesh_blocks, 1, rows, width)
+    came = swap(send)
+    came = came.reshape(mesh_blocks, 1, rows, width)
     kept = keep.reshape(mesh_blocks, 1, rows, width)
     mesh_state = jnp.concatenate(
         [jnp.where(core == 0, kept, came), jnp.where(core == 0, came, kept)], axis=1

time: 161 us -> 157 us (0.975)
  waiting for transfers between devices: 110 us -> 106 us
    ppermute x6, waiting for transfers between devices: 7.41 us -> 3.82 us  [swap(): return lax.ppermute(x, 'mp', SWAP)]
    pallas_call x0 -> x1, Pallas kernels: none -> 3.54 us  [load(): pl.pallas_call(functools.partial(load_body, count), out_shape=tuple((pltp...]
    pallas_call x1, Pallas kernels: 11.8 us -> 8.93 us  [encode(): pl.pallas_call(encode_body, out_shape=pltpu.HBM(sent, BF16), grid_spec=pl...]
  transfers between devices with their start and end apart: 8 -> 8, of which waited for: 5 -> 5; matrix products, arithmetic and copies ran while one was open for 1% -> 1% of each run, Pallas kernels for 0% -> 2%
where the time goes in v4:
time: 157 us
  waiting for transfers between devices  106 us (68%)
  Pallas kernels  27.7 us (18%)
  starting transfers between devices  20.9 us (13%)
    all_to_all x1, waiting for transfers between devices, per_device(): lax.all_to_all(slot_sums, ('band', 'mp'), split_axis=0, concat_axis=0, ti...  52.3 us
    all_to_all x1, waiting for transfers between devices, per_device(): lax.all_to_all(outgoing, ('band', 'mp'), split_axis=0, concat_axis=0, til...  50.3 us
    all_to_all x1, starting transfers between devices, per_device(): lax.all_to_all(slot_sums, ('band', 'mp'), split_axis=0, concat_axis=0, ti...  11.6 us
    pallas_call x1, Pallas kernels, decode(): pl.pallas_call(decode_body, out_shape=jax.ShapeDtypeStruct(grid_blocks.sh...  9.51 us
    pallas_call x1, Pallas kernels, encode(): pl.pallas_call(encode_body, out_shape=pltpu.HBM(sent, BF16), grid_spec=pl...  8.93 us
    all_to_all x1, starting transfers between devices, per_device(): lax.all_to_all(outgoing, ('band', 'mp'), split_axis=0, concat_axis=0, til...  7.92 us
    pallas_call x1, Pallas kernels, mesh_update(): pl.pallas_call(mesh_body, out_shape=(flat, flat, pltpu.HBM(leaving, BF16)...  5.69 us
    ppermute x6, waiting for transfers between devices, swap(): return lax.ppermute(x, 'mp', SWAP)  3.82 us
  transfers between devices with their start and end apart: 8, of which 5 were waited for; matrix products, arithmetic and copies ran while one was open for 1% of the time, Pallas kernels for 2%

profile of v4, /device:TPU:0, one launch (start us, length us, event | category | flops | bytes accessed | tf_op | source)
XLA Modules:
  0.0 156.8 jit_solution(15105893563243436942)
XLA Ops:
  0.6 0.1 collective-permute-start
  0.8 3.5 %load_encode.1 = (bf16[4096,256]{1,0:T(8,128)(2,1)S(1)}, bf16[512,256]{1,0:T(8,128)(2,1)S(1)}, bf16[192,128,128]{2,1,0:T(8,128)(2,1)S(1)}) custom-call(bf16[4096,256]{1,0:T(8,128)(2,1)} %refs_0_.1, bf16[512,256]{1,0:T(8,128)(2,1)} %refs_1_.1, bf16[192,128,128]{2,1,0:T(8,128)(2,1)} %refs_2_.1), custom_call_target="tpu_custom_call" | custom-call | bytes 16777216 | tf_op jit(solution)/shard_map/load_encode/pallas_call | solution.py:64
  4.3 0.8 collective-permute-done.other
  5.1 8.9 %encode.1 = bf16[128,136,128]{2,1,0:T(8,128)(2,1)} custom-call(s32[192]{0:T(256)S(1)} %copy-done.3, s32[192]{0:T(256)S(1)} %copy-done.4, s32[64]{0:T(128)S(1)} %bitcast.21, s32[1]{0:T(128)} %bitcast.core_ref, bf16[4096,256]{1,0:T(8,128)(2,1)S(1)} %get-tuple-element.8.own, bf16[4096,256]{1,0:T(8,128)(2,1)S(1)} %collective-permute-done.other, ...), custom_call_target="tpu_custom_call" | custom-call | flops 1610612736 | bytes 16777216 | tf_op jit(solution)/shard_map/encode/pallas_call | solution.py:143
  14.0 0.0 copy-start.8
  14.0 0.0 copy-start.1
  14.1 0.0 copy-start.2
  14.1 0.0 copy-start.9
  14.1 11.6 %all-to-all-start = ((bf16[128,136,128]{2,1,0:T(8,128)(2,1)}), bf16[128,136,128]{2,1,0:T(8,128)(2,1)}, u32[]{:S(2)}, u32[]{:S(2)}) async-start(bf16[128,136,128]{2,1,0:T(8,128)(2,1)} %encode.1), calls=%async_computation | async-start | bytes 8912896 | tf_op jit(solution)/shard_map/all_to_all | solution.py:382
  25.7 0.1 copy.20
  25.8 0.1 collective-permute-start.4
  25.9 0.5 collective-permute-start.2
  26.4 0.1 collective-permute-start.3
  26.5 0.5 collective-permute-start.1
  27.0 1.7 %collective-permute-done.1.theirs_ref = bf16[256,256]{1,0:T(8,128)(2,1)S(1)} collective-permute-done((bf16[256,256]{1,0:T(8,128)(2,1)S(1)}, bf16[256,256]{1,0:T(8,128)(2,1)S(1)}, u32[]{:S(2)}, u32[]{:S(2)}) %collective-permute-start.1) | collective-permute-done | bytes 131104 | tf_op jit(solution)/shard_map/ppermute | solution.py:344
  28.8 52.3 %all-to-all-done.arrived_hbm = bf16[128,136,128]{2,1,0:T(8,128)(2,1)} async-done(((bf16[128,136,128]{2,1,0:T(8,128)(2,1)}), bf16[128,136,128]{2,1,0:T(8,128)(2,1)}, u32[]{:S(2)}, u32[]{:S(2)}) %all-to-all-start) | async-done | bytes 4456480 | tf_op jit(solution)/shard_map/all_to_all | solution.py:382
  81.1 5.7 %mesh_update.1 = (bf16[256,256]{1,0:T(8,128)(2,1)S(1)}, bf16[256,256]{1,0:T(8,128)(2,1)S(1)}, bf16[128,64,256]{2,1,0:T(8,128)(2,1)}) custom-call(s32[1]{0:T(128)} %bitcast.core_ref, bf16[128,136,128]{2,1,0:T(8,128)(2,1)} %all-to-all-done.arrived_hbm, bf16[256,256]{1,0:T(8,128)(2,1)S(1)} %bitcast.20, bf16[256,256]{1,0:T(8,128)(2,1)S(1)} %collective-permute-done.1.theirs_ref, ...), custom_call_target="tpu_custom_call" | custom-call | flops 1000000000 | bytes 12582912 | tf_op jit(solution)/shard_map/mesh_update/pallas_call | solution.py:243
  86.8 0.0 copy-start
  86.8 7.9 %all-to-all-start.1 = ((bf16[128,64,256]{2,1,0:T(8,128)(2,1)}), bf16[128,64,256]{2,1,0:T(8,128)(2,1)}, u32[]{:S(2)}, u32[]{:S(2)}) async-start(bf16[128,64,256]{2,1,0:T(8,128)(2,1)} %get-tuple-element.11), calls=%async_computation.1 | async-start | bytes 8388608 | tf_op jit(solution)/shard_map/all_to_all | solution.py:391
  94.8 0.1 collective-permute-start.5
  94.9 1.3 collective-permute-done.5
  96.2 0.7 copy.17
  97.0 50.3 %all-to-all-done.1 = bf16[128,64,256]{2,1,0:T(8,128)(2,1)} async-done(((bf16[128,64,256]{2,1,0:T(8,128)(2,1)}), bf16[128,64,256]{2,1,0:T(8,128)(2,1)}, u32[]{:S(2)}, u32[]{:S(2)}) %all-to-all-start.1) | async-done | bytes 4194336 | tf_op jit(solution)/shard_map/all_to_all | solution.py:391
  147.3 9.5 %decode.1 = bf16[32,128,256]{2,1,0:T(8,128)(2,1)} custom-call(s32[192]{0:T(256)S(1)} %copy-done.5, s32[192]{0:T(256)S(1)} %copy-done.6, bf16[64,128,256]{2,1,0:T(8,128)(2,1)} %bitcast.5.picked_hbm, bf16[32,128,256]{2,1,0:T(8,128)(2,1)S(1)} %bitcast.17, bf16[192,128,128]{2,1,0:T(8,128)(2,1)} %tiles_hbm.1), custom_call_target="tpu_custom_call" | custom-call | flops 1610612736 | bytes 16777216 | tf_op jit(solution)/shard_map/decode/pallas_call | solution.py:320
  (21 shorter events, 0.1 us)
Async XLA Ops:
  0.6 4.5 %collective-permute-start = (bf16[4096,256]{1,0:T(8,128)(2,1)}, bf16[4096,256]{1,0:T(8,128)(2,1)S(1)}, u32[]{:S(2)}, u32[]{:S(2)}) collective-permute-start(bf16[4096,256]{1,0:T(8,128)(2,1)} %refs_0_.1), channel_id=1, source_target_pairs={{0,1},{1,0},{2,3},{3,2},{4,5},{5,4},{6,7},{7,6},{8,9},{9,8},{10,11... | collective-permute-start | bytes 6291464 | tf_op jit(solution)/shard_map/ppermute | solution.py:344
  0.7 4.4 %copy-start.3 = (s32[192]{0:T(256)S(1)}, s32[192]{0:T(256)}, u32[]{:S(2)}) copy-start(s32[192]{0:T(256)} %slot_ref.2) | copy-start | bytes 2308
  0.7 4.3 %copy-start.4 = (s32[192]{0:T(256)S(1)}, s32[192]{0:T(256)}, u32[]{:S(2)}) copy-start(s32[192]{0:T(256)} %source_ref.1) | copy-start | bytes 2308
  0.8 4.3 %copy-start.7 = (s32[1,64]{1,0:T(1,128)S(1)}, s32[1,64]{1,0:T(1,128)}, u32[]{:S(2)}) copy-start(s32[1,64]{1,0:T(1,128)} %param.22) | copy-start | bytes 772
  14.0 11.7 %copy-start.8 = (bf16[256,2,512]{2,1,0:T(2,128)(2,1)S(1)}, bf16[256,2,512]{2,1,0:T(2,128)(2,1)}, u32[]{:S(2)}) copy-start(bf16[256,2,512]{2,1,0:T(2,128)(2,1)} %param.18) | copy-start | bytes 1572868
  14.0 11.9 %copy-start.1 = (bf16[512,256]{1,0:T(8,128)(2,1)S(1)}, bf16[512,256]{1,0:T(8,128)(2,1)}, u32[]{:S(2)}) copy-start(bf16[512,256]{1,0:T(8,128)(2,1)} %self_w.1) | copy-start | bytes 786436
  14.1 12.4 %copy-start.2 = (bf16[512,256]{1,0:T(8,128)(2,1)S(1)}, bf16[512,256]{1,0:T(8,128)(2,1)}, u32[]{:S(2)}) copy-start(bf16[512,256]{1,0:T(8,128)(2,1)} %pool_w.1) | copy-start | bytes 786436
  14.1 12.4 %copy-start.9 = (bf16[512,256]{1,0:T(8,128)(2,1)S(1)}, bf16[512,256]{1,0:T(8,128)(2,1)}, u32[]{:S(2)}) copy-start(bf16[512,256]{1,0:T(8,128)(2,1)} %param.14) | copy-start | bytes 786436
  14.1 67.0 %all-to-all-start = ((bf16[128,136,128]{2,1,0:T(8,128)(2,1)}), bf16[128,136,128]{2,1,0:T(8,128)(2,1)}, u32[]{:S(2)}, u32[]{:S(2)}) async-start(bf16[128,136,128]{2,1,0:T(8,128)(2,1)} %encode.1), calls=%async_computation | async-start | bytes 8912896 | tf_op jit(solution)/shard_map/all_to_all | solution.py:382
  25.8 2.9 %collective-permute-start.4 = (bf16[256,1024]{1,0:T(8,128)(2,1)S(1)}, bf16[256,1024]{1,0:T(8,128)(2,1)S(1)}, u32[]{:S(2)}, u32[]{:S(2)}) collective-permute-start(bf16[256,1024]{1,0:T(8,128)(2,1)S(1)} %bitcast.18), channel_id=1, source_target_pairs={{0,1},{1,0},{2,3},{3,2},{4,5},{5,4},{6,7},{7,6},{8,9},{9,8},{10,11... | collective-permute-start | bytes 1572872 | tf_op jit(solution)/shard_map/ppermute | solution.py:344
  25.9 2.8 %collective-permute-start.2 = (bf16[512,256]{1,0:T(8,128)(2,1)S(1)}, bf16[512,256]{1,0:T(8,128)(2,1)S(1)}, u32[]{:S(2)}, u32[]{:S(2)}) collective-permute-start(bf16[512,256]{1,0:T(8,128)(2,1)S(1)} %copy-done.1), channel_id=1, source_target_pairs={{0,1},{1,0},{2,3},{3,2},{4,5},{5,4},{6,7},{7,6},{8,9},{9,8},{10,11... | collective-permute-start | bytes 786440 | tf_op jit(solution)/shard_map/ppermute | solution.py:344
  26.4 2.3 %collective-permute-start.3 = (bf16[512,256]{1,0:T(8,128)(2,1)S(1)}, bf16[512,256]{1,0:T(8,128)(2,1)S(1)}, u32[]{:S(2)}, u32[]{:S(2)}) collective-permute-start(bf16[512,256]{1,0:T(8,128)(2,1)S(1)} %copy-done.2), channel_id=1, source_target_pairs={{0,1},{1,0},{2,3},{3,2},{4,5},{5,4},{6,7},{7,6},{8,9},{9,8},{10,11... | collective-permute-start | bytes 786440 | tf_op jit(solution)/shard_map/ppermute | solution.py:344
  26.5 2.2 %collective-permute-start.1 = (bf16[256,256]{1,0:T(8,128)(2,1)S(1)}, bf16[256,256]{1,0:T(8,128)(2,1)S(1)}, u32[]{:S(2)}, u32[]{:S(2)}) collective-permute-start(bf16[256,256]{1,0:T(8,128)(2,1)S(1)} %bitcast.28), channel_id=1, source_target_pairs={{0,1},{1,0},{2,3},{3,2},{4,5},{5,4},{6,7},{7,6},{8,9},{9,8},{10,11... | collective-permute-start | bytes 393224 | tf_op jit(solution)/shard_map/ppermute | solution.py:344
  86.8 60.5 %copy-start = (bf16[4096,256]{1,0:T(8,128)(2,1)S(1)}, bf16[4096,256]{1,0:T(8,128)(2,1)}, u32[]{:S(2)}) copy-start(bf16[4096,256]{1,0:T(8,128)(2,1)} %refs_0_.1) | copy-start | bytes 6291460
  86.8 60.5 %copy-start.5 = (s32[192]{0:T(256)S(1)}, s32[192]{0:T(256)}, u32[]{:S(2)}) copy-start(s32[192]{0:T(256)} %slot_ref.3) | copy-start | bytes 2308
  86.8 60.4 %copy-start.6 = (s32[192]{0:T(256)S(1)}, s32[192]{0:T(256)}, u32[]{:S(2)}) copy-start(s32[192]{0:T(256)} %target_ref.1) | copy-start | bytes 2308
  86.8 60.4 %all-to-all-start.1 = ((bf16[128,64,256]{2,1,0:T(8,128)(2,1)}), bf16[128,64,256]{2,1,0:T(8,128)(2,1)}, u32[]{:S(2)}, u32[]{:S(2)}) async-start(bf16[128,64,256]{2,1,0:T(8,128)(2,1)} %get-tuple-element.11), calls=%async_computation.1 | async-start | bytes 8388608 | tf_op jit(solution)/shard_map/all_to_all | solution.py:391
  94.8 1.4 collective-permute-start.5

commit v5 on v4

--- a/solution.py
+++ b/solution.py
@@ -50,41 +50,111 @@
 NARROW = pltpu.CompilerParams(vmem_limit_bytes=44 * MB)
 
 
-def load_body(count, *refs):
-    sources, targets, semaphores = refs[:count], refs[-count - 1 : -1], refs[-1]
-    copies = [pltpu.make_async_copy(x, y, semaphores.at[k]) for k, (x, y) in enumerate(zip(sources, targets))]
+def pair_up(key_ref, begin, count, table, row, pending, missing):
+    keys = pending.shape[0]
+
+    @pl.loop(0, keys, unroll=16)
+    def _(k):
+        pending[k] = -1
+
+    def visit(t, n):
+        key = key_ref[begin + t]
+        waiting = pending[key]
+        both = waiting >= 0
+        table[row, n] = waiting
+        table[row + 1, n] = begin + t
+        pending[key] = jnp.where(both, -1, begin + t)
+        return n + both.astype(jnp.int32)
+
+    def leave(k, n):
+        waiting = pending[k]
+        table[row, n] = waiting
+        table[row + 1, n] = missing
+        return n + (waiting >= 0).astype(jnp.int32)
+
+    n = lax.fori_loop(0, count, visit, jnp.int32(0), unroll=8)
+    n = lax.fori_loop(0, keys, leave, n, unroll=8)
+
+    @pl.loop(0, GROUP, unroll=8)
+    def _(k):
+        table[row, n + k] = missing
+        table[row + 1, n + k] = missing
+
+    table[row + 2, 0] = (n + GROUP - 1) // GROUP
+
+
+def products(table, row, first, tiles, sums, sum_ref, rows, row_ref):
+    last = row_ref.shape[0] - 1
+    for i in range(GROUP):
+        one, two = table[row, first + i], table[row + 1, first + i]
+        near, far = jnp.minimum(one, last), jnp.minimum(two, last)
+        both = jnp.concatenate([tiles[one], tiles[two]], axis=1)
+        under = jnp.concatenate([rows[row_ref[near]], rows[row_ref[far]]], axis=0)
+        sums[sum_ref[near]] += dot(both, under)
+
+
+def load_body(key_ref, own_hbm, weight_hbm, tiles_hbm, own, weight, tiles, table, pending, semaphores):
+    count = tiles_hbm.shape[0]
+    moves = ((own_hbm, own), (weight_hbm, weight), (tiles_hbm, tiles.at[pl.ds(0, count)]))
+    copies = [pltpu.make_async_copy(x, y, semaphores.at[k]) for k, (x, y) in enumerate(moves)]
     for copy in copies:
         copy.start()
+    tiles[count:] = jnp.zeros((tiles.shape[0] - count, *tiles.shape[1:]), BF16)
+    pair_up(key_ref, 0, count, table, 0, pending, count)
     for copy in copies:
         copy.wait()
 
 
-def load(name, arrays, after=()):
-    count = len(arrays)
+def pair_body(parts, key_ref, after, table, pending):
+    count = key_ref.shape[0]
+    for k in range(parts):
+        pair_up(key_ref, k * (count // parts), count // parts, table, 3 * k, pending, count)
+
+
+def pairs(key, keys, parts, after):
     return pl.pallas_call(
-        functools.partial(load_body, count),
-        out_shape=tuple(pltpu.VMEM(a.shape, a.dtype) for a in arrays),
-        in_specs=[hbm()] * (count + len(after)),
-        out_specs=tuple(vmem() for _ in arrays),
-        scratch_shapes=[pltpu.SemaphoreType.DMA((count,))],
+        functools.partial(pair_body, parts),
+        out_shape=jax.ShapeDtypeStruct((8, TABLE), jnp.int32),
+        in_specs=[pl.BlockSpec(memory_space=pltpu.SMEM), hbm()],
+        out_specs=pl.BlockSpec(memory_space=pltpu.SMEM),
+        scratch_shapes=[pltpu.SMEM((keys,), jnp.int32)],
+        cost_estimate=pl.CostEstimate(flops=0, bytes_accessed=8 * MB, transcendentals=0),
+        name="pair_decode",
+    )(key, *stay(after))
+
+
+def load(key, keys, own, weight, tiles):
+    padded = (tiles.shape[0] + 8, *tiles.shape[1:])
+    return pl.pallas_call(
+        load_body,
+        out_shape=(
+            pltpu.VMEM(own.shape, BF16),
+            pltpu.VMEM(weight.shape, BF16),
+            pltpu.VMEM(padded, BF16),
+            jax.ShapeDtypeStruct((8, TABLE), jnp.int32),
+        ),
+        in_specs=[pl.BlockSpec(memory_space=pltpu.SMEM), hbm(), hbm(), hbm()],
+        out_specs=(vmem(), vmem(), vmem(), pl.BlockSpec(memory_space=pltpu.SMEM)),
+        scratch_shapes=[pltpu.SMEM((keys,), jnp.int32), pltpu.SemaphoreType.DMA((3,))],
         compiler_params=pltpu.CompilerParams(vmem_limit_bytes=24 * MB),
         cost_estimate=pl.CostEstimate(flops=0, bytes_accessed=16 * MB, transcendentals=0),
-        name=name,
-    )(*stay(*arrays), *stay(*after))
+        name="load_encode",
+    )(key, *stay(own, weight, tiles))
 
 
 PIECES = 4
-UNROLL = 48
+GROUP = 32
+TABLE = 256
+PARTS = 2
 TAG = 8
 
 
 def encode_body(
-    slot_ref, source_ref, link_ref, core_ref, own, other, weight, tiles, out_hbm, message, acc, out, out_sem,
+    table, slot_ref, source_ref, link_ref, core_ref, own, other, weight, tiles, out_hbm, message, acc, out, out_sem,
 ):
     core = core_ref[0]
     blocks, edge, width = message.shape
     slots = acc.shape[0]
-    count = tiles.shape[0]
     rows = edge // 2
     lanes = out.shape[2]
     inner = 8 * edge
@@ -101,13 +171,9 @@
             message[pl.ds(step * 8, 8)] = silu(z).astype(BF16).reshape(8, edge, width)
             acc[pl.ds(step * cleared, cleared)] = jnp.zeros((cleared, edge, width), F32)
 
-    @pl.loop(0, PIECES)
-    def _(piece):
-        @pl.loop(0, count // PIECES // UNROLL)
-        def _(j):
-            base = piece * (count // PIECES) + j * UNROLL
-            for i in range(UNROLL):
-                acc[slot_ref[base + i]] += dot(tiles[base + i], message[source_ref[base + i]])
+    @pl.loop(0, table[2, 0])
+    def _(j):
+        products(table, 0, j * GROUP, tiles, acc, slot_ref, message, source_ref)
 
     size = 2 * slots // PIECES
 
@@ -135,7 +201,7 @@
         leave(piece).wait()
 
 
-def encode(own, other, weight, tiles, source, slot, link, core, slots):
+def encode(own, other, weight, tiles, table, source, slot, link, core, slots):
     count, edge, _ = tiles.shape
     width = weight.shape[1]
     sent = (2 * slots, edge + TAG, width // 2)
@@ -144,7 +210,7 @@
         encode_body,
         out_shape=pltpu.HBM(sent, BF16),
         grid_spec=pltpu.PrefetchScalarGridSpec(
-            num_scalar_prefetch=4,
+            num_scalar_prefetch=5,
             in_specs=[vmem()] * 4,
             out_specs=hbm(),
             scratch_shapes=[
@@ -159,7 +225,7 @@
             flops=2 * count * edge * edge * width, bytes_accessed=16 * MB, transcendentals=own.shape[0] * width
         ),
         name="encode",
-    )(slot, source, link, core, own, other, weight, tiles)
+    )(table, slot, source, link, core, own, other, weight, tiles)
 
 
 def mesh_body(
@@ -265,18 +331,18 @@
 
 
 def decode_body(
-    slot_ref, target_ref, picked_hbm, start, tiles_hbm, out_hbm,
+    table, slot_ref, target_ref, picked_hbm, start, tiles_hbm, out_hbm,
     picked, tiles, acc, out, picked_sem, tiles_sem, out_sem,
 ):
-    count = tiles.shape[0]
+    count = tiles_hbm.shape[0]
     blocks = acc.shape[0]
     picked_start, picked_ready = fetch(picked_hbm, picked, picked_sem, PIECES)
-    tiles_start, tiles_ready = fetch(tiles_hbm, tiles, tiles_sem, PIECES)
+    tiles_start, tiles_ready = fetch(tiles_hbm, tiles, tiles_sem, PARTS)
     per = blocks // PIECES
     for piece in range(PIECES):
         picked_start(piece)
-    for piece in range(PIECES):
-        tiles_start(piece)
+    tiles_start(0)
+    tiles[count:] = jnp.zeros((tiles.shape[0] - count, *tiles.shape[1:]), BF16)
 
     @pl.loop(0, PIECES)
     def _(piece):
@@ -286,16 +352,16 @@
 
     for piece in range(PIECES):
         picked_ready(piece)
-
-    @pl.loop(0, PIECES)
-    def _(piece):
-        tiles_ready(piece)
-
-        @pl.loop(0, count // PIECES // UNROLL)
-        def _(j):
-            base = piece * (count // PIECES) + j * UNROLL
-            for i in range(UNROLL):
-                acc[target_ref[base + i]] += dot(tiles[base + i], picked[slot_ref[base + i]])
+    for part in range(1, PARTS):
+        tiles_start(part)
+
+    @pl.loop(0, PARTS)
+    def _(part):
+        tiles_ready(part)
+
+        @pl.loop(0, table[3 * part + 2, 0])
+        def _(j):
+            products(table, 3 * part, j * GROUP, tiles, acc, target_ref, picked, slot_ref)
 
     def leave(k):
         at = pl.ds(k * per, per)
@@ -313,7 +379,7 @@
         leave(piece).wait()
 
 
-def decode(picked, grid_blocks, tiles, slot, target):
+def decode(picked, grid_blocks, tiles, table, slot, target):
     count, edge, _ = tiles.shape
     width = grid_blocks.shape[2]
     dma = pltpu.SemaphoreType.DMA
@@ -321,12 +387,12 @@
         decode_body,
         out_shape=jax.ShapeDtypeStruct(grid_blocks.shape, BF16),
         grid_spec=pltpu.PrefetchScalarGridSpec(
-            num_scalar_prefetch=2,
+            num_scalar_prefetch=3,
             in_specs=[hbm(), vmem(), hbm()],
             out_specs=hbm(),
             scratch_shapes=[
                 pltpu.VMEM(picked.shape, BF16),
-                pltpu.VMEM(tiles.shape, BF16),
+                pltpu.VMEM((count + 8, edge, edge), BF16),
                 pltpu.VMEM(grid_blocks.shape, F32),
                 pltpu.VMEM(grid_blocks.shape, BF16),
                 *[dma((PIECES,))] * 3,
@@ -337,7 +403,7 @@
             flops=2 * count * edge * edge * width, bytes_accessed=16 * MB, transcendentals=0
         ),
         name="decode",
-    )(slot, target, *stay(picked), grid_blocks, *stay(tiles))
+    )(table, slot, target, *stay(picked), grid_blocks, *stay(tiles))
 
 
 def swap(x):
@@ -375,9 +441,9 @@
     mesh_other = swap(mesh_send)
     self_other, pooled_other, out_other = swap(self_weight), swap(pooled_weight), swap(out_flat)
 
-    own, near_weight, near_tiles = load("load_encode", (grid_nodes, send_weight, encode_tiles))
+    own, near_weight, near_tiles, table = load(encode_slot, bands, grid_nodes, send_weight, encode_tiles)
     slot_sums = encode(
-        own, grid_other, near_weight, near_tiles, encode_source, encode_slot, slot_block[0], core_1, bands
+        own, grid_other, near_weight, near_tiles, table, encode_source, encode_slot, slot_block[0], core_1, bands
     )
     arrived = lax.all_to_all(slot_sums, ("band", "mp"), split_axis=0, concat_axis=0, tiled=True)
     keep, send, outgoing = mesh_update(
@@ -390,6 +456,7 @@
     )
     returned = lax.all_to_all(outgoing, ("band", "mp"), split_axis=0, concat_axis=0, tiled=True)
     came = swap(send)
+    decode_table = pairs(decode_target, grid_nodes.shape[0] // edge, PARTS, came)
     came = came.reshape(mesh_blocks, 1, rows, width)
     kept = keep.reshape(mesh_blocks, 1, rows, width)
     mesh_state = jnp.concatenate(
@@ -399,6 +466,7 @@
         returned.reshape(bands, edge, width),
         grid_nodes.reshape(-1, edge, width),
         decode_tiles,
+        decode_table,
         decode_slot,
         decode_target,
     )

time: 157 us -> 160 us (1.019)
  Pallas kernels: 27.7 us -> 32.9 us
  waiting for transfers between devices: 106 us -> 103 us
    pallas_call x1 -> x2, Pallas kernels: 3.54 us -> 7.9 us  [the longest x1 4.79 us: load(): pl.pallas_call(load_body, out_shape=(pltpu.VMEM(own.shape, BF16), pltpu.V...]
    all_to_all x1, waiting for transfers between devices: 50.3 us -> 47.2 us  [per_device(): lax.all_to_all(outgoing, ('band', 'mp'), split_axis=0, concat_axis=0, til...]
  transfers between devices with their start and end apart: 8 -> 8, of which waited for: 5 -> 4; matrix products, arithmetic and copies ran while one was open for 1% -> 1% of each run, Pallas kernels for 2% -> 5%
where the time goes in v5:
time: 160 us
  waiting for transfers between devices  103 us (64%)
  Pallas kernels  32.9 us (21%)
  starting transfers between devices  21 us (13%)
  local copies, waits for them, and re-layouts  2.23 us (1%)
    all_to_all x1, waiting for transfers between devices, per_device(): lax.all_to_all(slot_sums, ('band', 'mp'), split_axis=0, concat_axis=0, ti...  52.3 us
    all_to_all x1, waiting for transfers between devices, per_device(): lax.all_to_all(outgoing, ('band', 'mp'), split_axis=0, concat_axis=0, til...  47.2 us
    all_to_all x1, starting transfers between devices, per_device(): lax.all_to_all(slot_sums, ('band', 'mp'), split_axis=0, concat_axis=0, ti...  11.7 us
    pallas_call x1, Pallas kernels, decode(): pl.pallas_call(decode_body, out_shape=jax.ShapeDtypeStruct(grid_blocks.sh...  9.67 us
    pallas_call x1, Pallas kernels, encode(): pl.pallas_call(encode_body, out_shape=pltpu.HBM(sent, BF16), grid_spec=pl...  9.6 us
    all_to_all x1, starting transfers between devices, per_device(): lax.all_to_all(outgoing, ('band', 'mp'), split_axis=0, concat_axis=0, til...  7.92 us
    pallas_call x1, Pallas kernels, mesh_update(): pl.pallas_call(mesh_body, out_shape=(flat, flat, pltpu.HBM(leaving, BF16)...  5.69 us
    pallas_call x1, Pallas kernels, load(): pl.pallas_call(load_body, out_shape=(pltpu.VMEM(own.shape, BF16), pltpu.V...  4.79 us
  transfers between devices with their start and end apart: 8, of which 4 were waited for; matrix products, arithmetic and copies ran while one was open for 1% of the time, Pallas kernels for 5%

profile of v5, /device:TPU:0, one launch (start us, length us, event | category | flops | bytes accessed | tf_op | source)
XLA Modules:
  0.0 159.6 jit_solution(12650040780581683240)
XLA Ops:
  0.6 0.1 collective-permute-start
  0.7 0.7 copy-done.5
  1.4 4.8 %load_encode.1 = (bf16[4096,256]{1,0:T(8,128)(2,1)S(1)}, bf16[512,256]{1,0:T(8,128)(2,1)S(1)}, bf16[200,128,128]{2,1,0:T(8,128)(2,1)S(1)}, s32[8,256]{1,0:T(8,128)S(1)}) custom-call(s32[192]{0:T(256)S(1)} %copy-done.5, bf16[4096,256]{1,0:T(8,128)(2,1)} %own_hbm.1, bf16[512,256]{1,0:T(8,128)(2,1)} %weight_hbm.1, bf16[192,128,128]{2,1,0:T(8,128)(2,1)} %tiles_hbm.2), custom_call_target="tpu_custom_call" | custom-call | bytes 16777216 | tf_op jit(solution)/shard_map/load_encode/pallas_call | solution.py:128
  6.3 9.6 %encode.1 = bf16[128,136,128]{2,1,0:T(8,128)(2,1)} custom-call(s32[8,256]{1,0:T(8,128)S(1)} %get-tuple-element.9.table, s32[192]{0:T(256)S(1)} %copy-done.6, s32[192]{0:T(256)S(1)} %copy-done.8, s32[64]{0:T(128)S(1)} %bitcast.21, s32[1]{0:T(128)} %bitcast.core_ref, bf16[4096,256]{1,0:T(8,128)(2,1)S(1)} %get-tuple-element.10.own, ...), custom_call_target="tpu_custom_call" | custom-call | flops 1677721600 | bytes 16777216 | tf_op jit(solution)/shard_map/encode/pallas_call | solution.py:209
  15.9 0.0 copy-start.11
  15.9 0.0 copy-start.12
  15.9 11.7 %all-to-all-start = ((bf16[128,136,128]{2,1,0:T(8,128)(2,1)}), bf16[128,136,128]{2,1,0:T(8,128)(2,1)}, u32[]{:S(2)}, u32[]{:S(2)}) async-start(bf16[128,136,128]{2,1,0:T(8,128)(2,1)} %encode.1), calls=%async_computation | async-start | bytes 8912896 | tf_op jit(solution)/shard_map/all_to_all | solution.py:448
  27.7 0.1 copy.20
  27.7 0.1 collective-permute-start.4
  27.8 0.5 collective-permute-start.2
  28.3 0.1 collective-permute-start.3
  28.5 0.5 collective-permute-start.1
  29.0 1.7 %collective-permute-done.1.theirs_ref = bf16[256,256]{1,0:T(8,128)(2,1)S(1)} collective-permute-done((bf16[256,256]{1,0:T(8,128)(2,1)S(1)}, bf16[256,256]{1,0:T(8,128)(2,1)S(1)}, u32[]{:S(2)}, u32[]{:S(2)}) %collective-permute-start.1) | collective-permute-done | bytes 131104 | tf_op jit(solution)/shard_map/ppermute | solution.py:410
  30.7 52.3 %all-to-all-done.arrived_hbm = bf16[128,136,128]{2,1,0:T(8,128)(2,1)} async-done(((bf16[128,136,128]{2,1,0:T(8,128)(2,1)}), bf16[128,136,128]{2,1,0:T(8,128)(2,1)}, u32[]{:S(2)}, u32[]{:S(2)}) %all-to-all-start) | async-done | bytes 4456480 | tf_op jit(solution)/shard_map/all_to_all | solution.py:448
  83.0 5.7 %mesh_update.1 = (bf16[256,256]{1,0:T(8,128)(2,1)S(1)}, bf16[256,256]{1,0:T(8,128)(2,1)S(1)}, bf16[128,64,256]{2,1,0:T(8,128)(2,1)}) custom-call(s32[1]{0:T(128)} %bitcast.core_ref, bf16[128,136,128]{2,1,0:T(8,128)(2,1)} %all-to-all-done.arrived_hbm, bf16[256,256]{1,0:T(8,128)(2,1)S(1)} %bitcast.20, bf16[256,256]{1,0:T(8,128)(2,1)S(1)} %collective-permute-done.1.theirs_ref, ...), custom_call_target="tpu_custom_call" | custom-call | flops 1000000000 | bytes 12582912 | tf_op jit(solution)/shard_map/mesh_update/pallas_call | solution.py:309
  88.7 0.0 copy-start
  88.8 7.9 %all-to-all-start.1 = ((bf16[128,64,256]{2,1,0:T(8,128)(2,1)}), bf16[128,64,256]{2,1,0:T(8,128)(2,1)}, u32[]{:S(2)}, u32[]{:S(2)}) async-start(bf16[128,64,256]{2,1,0:T(8,128)(2,1)} %get-tuple-element.14), calls=%async_computation.1 | async-start | bytes 8388608 | tf_op jit(solution)/shard_map/all_to_all | solution.py:457
  96.7 0.1 collective-permute-start.5
  96.8 1.3 collective-permute-done.5.after
  98.2 0.7 copy.17
  98.9 3.1 %pair_decode.1.table = s32[8,256]{1,0:T(8,128)} custom-call(s32[192]{0:T(256)} %target_ref.1, bf16[256,256]{1,0:T(8,128)(2,1)} %copy-done.10), custom_call_target="tpu_custom_call" | custom-call | bytes 8388608 | tf_op jit(solution)/shard_map/pair_decode/pallas_call | solution.py:115
  102.0 47.2 %all-to-all-done.1 = bf16[128,64,256]{2,1,0:T(8,128)(2,1)} async-done(((bf16[128,64,256]{2,1,0:T(8,128)(2,1)}), bf16[128,64,256]{2,1,0:T(8,128)(2,1)}, u32[]{:S(2)}, u32[]{:S(2)}) %all-to-all-start.1) | async-done | bytes 4194336 | tf_op jit(solution)/shard_map/all_to_all | solution.py:457
  149.2 0.7 copy-done.3
  149.9 9.7 %decode.1 = bf16[32,128,256]{2,1,0:T(8,128)(2,1)} custom-call(s32[8,256]{1,0:T(8,128)S(1)} %copy-done.3, s32[192]{0:T(256)S(1)} %copy-done.7, s32[192]{0:T(256)S(1)} %copy-done.4, bf16[64,128,256]{2,1,0:T(8,128)(2,1)} %bitcast.5.picked_hbm, bf16[32,128,256]{2,1,0:T(8,128)(2,1)S(1)} %bitcast.17, bf16[192,128,128]{2,1,0:T(8,128)(2,1)} %tiles_hbm.3), custom_call_target="tpu_custom_call" | custom-call | flops 1610612736 | bytes 16777216 | tf_op jit(solution)/shard_map/decode/pallas_call | solution.py:386
  (28 shorter events, 0.1 us)
Async XLA Ops:
  0.6 5.6 %collective-permute-start = (bf16[4096,256]{1,0:T(8,128)(2,1)}, bf16[4096,256]{1,0:T(8,128)(2,1)S(1)}, u32[]{:S(2)}, u32[]{:S(2)}) collective-permute-start(bf16[4096,256]{1,0:T(8,128)(2,1)} %own_hbm.1), channel_id=1, source_target_pairs={{0,1},{1,0},{2,3},{3,2},{4,5},{5,4},{6,7},{7,6},{8,9},{9,8},{10,11... | collective-permute-start | bytes 6291464 | tf_op jit(solution)/shard_map/ppermute | solution.py:410
  0.7 0.7 copy-start.5
  1.4 4.8 %copy-start.6 = (s32[192]{0:T(256)S(1)}, s32[192]{0:T(256)}, u32[]{:S(2)}) copy-start(s32[192]{0:T(256)} %slot_ref.2) | copy-start | bytes 2308
  1.4 4.8 %copy-start.8 = (s32[192]{0:T(256)S(1)}, s32[192]{0:T(256)}, u32[]{:S(2)}) copy-start(s32[192]{0:T(256)} %source_ref.1) | copy-start | bytes 2308
  1.4 4.8 %copy-start.9 = (s32[1,64]{1,0:T(1,128)S(1)}, s32[1,64]{1,0:T(1,128)}, u32[]{:S(2)}) copy-start(s32[1,64]{1,0:T(1,128)} %param.22) | copy-start | bytes 772
  15.9 11.8 %copy-start.11 = (bf16[256,2,512]{2,1,0:T(2,128)(2,1)S(1)}, bf16[256,2,512]{2,1,0:T(2,128)(2,1)}, u32[]{:S(2)}) copy-start(bf16[256,2,512]{2,1,0:T(2,128)(2,1)} %param.18) | copy-start | bytes 1572868
  15.9 12.0 %copy-start.1 = (bf16[512,256]{1,0:T(8,128)(2,1)S(1)}, bf16[512,256]{1,0:T(8,128)(2,1)}, u32[]{:S(2)}) copy-start(bf16[512,256]{1,0:T(8,128)(2,1)} %self_w.1) | copy-start | bytes 786436
  15.9 12.4 %copy-start.2 = (bf16[512,256]{1,0:T(8,128)(2,1)S(1)}, bf16[512,256]{1,0:T(8,128)(2,1)}, u32[]{:S(2)}) copy-start(bf16[512,256]{1,0:T(8,128)(2,1)} %pool_w.1) | copy-start | bytes 786436
  15.9 12.5 %copy-start.12 = (bf16[512,256]{1,0:T(8,128)(2,1)S(1)}, bf16[512,256]{1,0:T(8,128)(2,1)}, u32[]{:S(2)}) copy-start(bf16[512,256]{1,0:T(8,128)(2,1)} %param.14) | copy-start | bytes 786436
  15.9 67.1 %all-to-all-start = ((bf16[128,136,128]{2,1,0:T(8,128)(2,1)}), bf16[128,136,128]{2,1,0:T(8,128)(2,1)}, u32[]{:S(2)}, u32[]{:S(2)}) async-start(bf16[128,136,128]{2,1,0:T(8,128)(2,1)} %encode.1), calls=%async_computation | async-start | bytes 8912896 | tf_op jit(solution)/shard_map/all_to_all | solution.py:448
  27.7 2.9 %collective-permute-start.4 = (bf16[256,1024]{1,0:T(8,128)(2,1)S(1)}, bf16[256,1024]{1,0:T(8,128)(2,1)S(1)}, u32[]{:S(2)}, u32[]{:S(2)}) collective-permute-start(bf16[256,1024]{1,0:T(8,128)(2,1)S(1)} %bitcast.18), channel_id=1, source_target_pairs={{0,1},{1,0},{2,3},{3,2},{4,5},{5,4},{6,7},{7,6},{8,9},{9,8},{10,11... | collective-permute-start | bytes 1572872 | tf_op jit(solution)/shard_map/ppermute | solution.py:410
  27.8 2.8 %collective-permute-start.2 = (bf16[512,256]{1,0:T(8,128)(2,1)S(1)}, bf16[512,256]{1,0:T(8,128)(2,1)S(1)}, u32[]{:S(2)}, u32[]{:S(2)}) collective-permute-start(bf16[512,256]{1,0:T(8,128)(2,1)S(1)} %copy-done.1), channel_id=1, source_target_pairs={{0,1},{1,0},{2,3},{3,2},{4,5},{5,4},{6,7},{7,6},{8,9},{9,8},{10,11... | collective-permute-start | bytes 786440 | tf_op jit(solution)/shard_map/ppermute | solution.py:410
  28.3 2.3 %collective-permute-start.3 = (bf16[512,256]{1,0:T(8,128)(2,1)S(1)}, bf16[512,256]{1,0:T(8,128)(2,1)S(1)}, u32[]{:S(2)}, u32[]{:S(2)}) collective-permute-start(bf16[512,256]{1,0:T(8,128)(2,1)S(1)} %copy-done.2), channel_id=1, source_target_pairs={{0,1},{1,0},{2,3},{3,2},{4,5},{5,4},{6,7},{7,6},{8,9},{9,8},{10,11... | collective-permute-start | bytes 786440 | tf_op jit(solution)/shard_map/ppermute | solution.py:410
  28.5 2.2 %collective-permute-start.1 = (bf16[256,256]{1,0:T(8,128)(2,1)S(1)}, bf16[256,256]{1,0:T(8,128)(2,1)S(1)}, u32[]{:S(2)}, u32[]{:S(2)}) collective-permute-start(bf16[256,256]{1,0:T(8,128)(2,1)S(1)} %bitcast.28), channel_id=1, source_target_pairs={{0,1},{1,0},{2,3},{3,2},{4,5},{5,4},{6,7},{7,6},{8,9},{9,8},{10,11... | collective-permute-start | bytes 393224 | tf_op jit(solution)/shard_map/ppermute | solution.py:410
  88.7 60.5 %copy-start = (bf16[4096,256]{1,0:T(8,128)(2,1)S(1)}, bf16[4096,256]{1,0:T(8,128)(2,1)}, u32[]{:S(2)}) copy-start(bf16[4096,256]{1,0:T(8,128)(2,1)} %own_hbm.1) | copy-start | bytes 6291460
  88.7 60.5 %copy-start.4 = (s32[192]{0:T(256)S(1)}, s32[192]{0:T(256)}, u32[]{:S(2)}) copy-start(s32[192]{0:T(256)} %target_ref.1) | copy-start | bytes 2308
  88.7 60.4 %copy-start.7 = (s32[192]{0:T(256)S(1)}, s32[192]{0:T(256)}, u32[]{:S(2)}) copy-start(s32[192]{0:T(256)} %slot_ref.3) | copy-start | bytes 2308
  88.8 60.4 %all-to-all-start.1 = ((bf16[128,64,256]{2,1,0:T(8,128)(2,1)}), bf16[128,64,256]{2,1,0:T(8,128)(2,1)}, u32[]{:S(2)}, u32[]{:S(2)}) async-start(bf16[128,64,256]{2,1,0:T(8,128)(2,1)} %get-tuple-element.14), calls=%async_computation.1 | async-start | bytes 8388608 | tf_op jit(solution)/shard_map/all_to_all | solution.py:457
  96.7 1.4 collective-permute-start.5
  98.1 0.8 copy-start.10
  149.2 0.7 copy-start.3

commit v6 on v4

--- a/solution.py
+++ b/solution.py
@@ -75,18 +75,16 @@
 
 PIECES = 4
 UNROLL = 48
-TAG = 8
 
 
 def encode_body(
-    slot_ref, source_ref, link_ref, core_ref, own, other, weight, tiles, out_hbm, message, acc, out, out_sem,
+    slot_ref, source_ref, core_ref, own, other, weight, tiles, out_hbm, message, acc, out, out_sem,
 ):
     core = core_ref[0]
     blocks, edge, width = message.shape
     slots = acc.shape[0]
     count = tiles.shape[0]
     rows = edge // 2
-    lanes = out.shape[2]
     inner = 8 * edge
     per = blocks * edge // inner // PIECES
     cleared = slots // (per * PIECES)
@@ -120,14 +118,8 @@
         @pl.loop(0, slots // PIECES, unroll=4)
         def _(j):
             slot = piece * (slots // PIECES) + j
-            tag = jnp.full((TAG, lanes), link_ref[slot].astype(F32), F32).astype(BF16)
             for part in range(2):
-                value = acc[slot, part * rows : (part + 1) * rows, :].astype(BF16)
-                for column in range(2):
-                    out[2 * slot + part, column * rows : (column + 1) * rows, :] = value[
-                        :, column * lanes : (column + 1) * lanes
-                    ]
-                out[2 * slot + part, 2 * rows :, :] = tag
+                out[2 * slot + part] = acc[slot, part * rows : (part + 1) * rows, :].astype(BF16)
 
         leave(piece).start()
 
@@ -135,16 +127,16 @@
         leave(piece).wait()
 
 
-def encode(own, other, weight, tiles, source, slot, link, core, slots):
+def encode(own, other, weight, tiles, source, slot, core, slots):
     count, edge, _ = tiles.shape
     width = weight.shape[1]
-    sent = (2 * slots, edge + TAG, width // 2)
+    sent = (2 * slots, edge // 2, width)
     dma = pltpu.SemaphoreType.DMA
     return pl.pallas_call(
         encode_body,
         out_shape=pltpu.HBM(sent, BF16),
         grid_spec=pltpu.PrefetchScalarGridSpec(
-            num_scalar_prefetch=4,
+            num_scalar_prefetch=3,
             in_specs=[vmem()] * 4,
             out_specs=hbm(),
             scratch_shapes=[
@@ -159,18 +151,16 @@
             flops=2 * count * edge * edge * width, bytes_accessed=16 * MB, transcendentals=own.shape[0] * width
         ),
         name="encode",
-    )(slot, source, link, core, own, other, weight, tiles)
+    )(slot, source, core, own, other, weight, tiles)
 
 
 def mesh_body(
-    core_ref, arrived_hbm, mine_ref, theirs_ref, self_w, self_o, pool_w, pool_o, out_w, out_o, keep, send,
-    outgoing_hbm, arrived, acc, state, source, outgoing, block_ref, arrived_sem, out_sem,
+    block_ref, core_ref, arrived_hbm, mine_ref, theirs_ref, self_w, self_o, pool_w, pool_o, out_w, out_o, keep, send,
+    outgoing_hbm, arrived, acc, state, source, outgoing, arrived_sem, out_sem,
 ):
     core = core_ref[0]
     bands = arrived.shape[0] // 2
-    lanes = arrived.shape[2]
-    rows = acc.shape[1]
-    width = 2 * lanes
+    width = arrived.shape[2]
     arrived_start, ready = fetch(arrived_hbm, arrived, arrived_sem, PIECES)
     for piece in range(PIECES):
         arrived_start(piece)
@@ -180,23 +170,12 @@
     def _(piece):
         ready(piece)
 
-        @pl.loop(0, bands // PIECES, unroll=16)
-        def _(j):
-            band = piece * (bands // PIECES) + j
-            tag = arrived[2 * band, 2 * rows :, :].astype(F32)
-            block = jnp.max(tag).astype(jnp.int32)
-            block_ref[band] = block
-
-        @pl.loop(0, bands // PIECES, unroll=2)
+        @pl.loop(0, bands // PIECES, unroll=4)
         def _(j):
             band = piece * (bands // PIECES) + j
             block = block_ref[band]
             for part in range(2):
-                for column in range(2):
-                    at = (2 * part + column) * lanes
-                    acc[block, :, at : at + lanes] += arrived[
-                        2 * band + part, column * rows : (column + 1) * rows, :
-                    ].astype(F32)
+                acc[block, :, part * width : (part + 1) * width] += arrived[2 * band + part].astype(F32)
 
     pooled = acc[...].reshape(-1, 2 * width).astype(BF16)
     mine, theirs = mine_ref[...], theirs_ref[...]
@@ -234,17 +213,16 @@
         leave(piece).wait()
 
 
-def mesh_update(arrived, core, mesh, mesh_other, weights, blocks):
-    pieces, height, lanes = arrived.shape
-    rows, width = (height - TAG) // 2, 2 * lanes
+def mesh_update(arrived, owner_block, core, mesh, mesh_other, weights, blocks):
+    pieces, rows, width = arrived.shape
     flat = jax.ShapeDtypeStruct(mesh.shape, BF16)
-    leaving = (pieces, rows, width)
+    leaving = arrived.shape
     dma = pltpu.SemaphoreType.DMA
     return pl.pallas_call(
         mesh_body,
         out_shape=(flat, flat, pltpu.HBM(leaving, BF16)),
         grid_spec=pltpu.PrefetchScalarGridSpec(
-            num_scalar_prefetch=1,
+            num_scalar_prefetch=2,
             in_specs=[hbm()] + [vmem()] * 8,
             out_specs=[vmem(), vmem(), hbm()],
             scratch_shapes=[
@@ -253,7 +231,6 @@
                 pltpu.VMEM((blocks * rows, 2 * width), F32),
                 pltpu.VMEM((blocks, rows, 2 * width), BF16),
                 pltpu.VMEM(leaving, BF16),
-                pltpu.SMEM((pieces // 2,), jnp.int32),
                 dma((PIECES,)),
                 dma((PIECES,)),
             ],
@@ -261,7 +238,7 @@
         compiler_params=NARROW,
         cost_estimate=pl.CostEstimate(flops=10**9, bytes_accessed=12 * MB, transcendentals=1 << 17),
         name="mesh_update",
-    )(core, *stay(arrived), mesh, mesh_other, *weights)
+    )(owner_block, core, *stay(arrived), mesh, mesh_other, *weights)
 
 
 def decode_body(
@@ -275,17 +252,18 @@
     per = blocks // PIECES
     for piece in range(PIECES):
         picked_start(piece)
-    for piece in range(PIECES):
+    tiles_start(0)
+
+    @pl.loop(0, PIECES)
+    def _(piece):
+        @pl.loop(0, per, unroll=4)
+        def _(j):
+            acc[piece * per + j] = start[piece * per + j].astype(F32)
+
+    for piece in range(PIECES):
+        picked_ready(piece)
+    for piece in range(1, PIECES):
         tiles_start(piece)
-
-    @pl.loop(0, PIECES)
-    def _(piece):
-        @pl.loop(0, per, unroll=4)
-        def _(j):
-            acc[piece * per + j] = start[piece * per + j].astype(F32)
-
-    for piece in range(PIECES):
-        picked_ready(piece)
 
     @pl.loop(0, PIECES)
     def _(piece):
@@ -342,6 +320,20 @@
 
 def swap(x):
     return lax.ppermute(x, "mp", SWAP)
+
+
+def owner_blocks(row):
+    bands = lax.axis_size("band")
+    me = lax.axis_index("band")
+    table = row
+    bit = 1
+    while bit < bands:
+        table = jnp.concatenate([table, lax.ppermute(table, "band", [(k, k ^ bit) for k in range(bands)])])
+        bit *= 2
+    number = jnp.arange(bands, dtype=jnp.int32)
+    column = jnp.sum(jnp.where(number[None, :] == me, table, 0), axis=1)
+    moved = (number[:, None] ^ me) == number[None, :]
+    return jnp.sum(jnp.where(moved, column[None, :], 0), axis=1).astype(jnp.int32)
 
 
 def per_device(
@@ -377,11 +369,12 @@
 
     own, near_weight, near_tiles = load("load_encode", (grid_nodes, send_weight, encode_tiles))
     slot_sums = encode(
-        own, grid_other, near_weight, near_tiles, encode_source, encode_slot, slot_block[0], core_1, bands
+        own, grid_other, near_weight, near_tiles, encode_source, encode_slot, core_1, bands
     )
     arrived = lax.all_to_all(slot_sums, ("band", "mp"), split_axis=0, concat_axis=0, tiled=True)
     keep, send, outgoing = mesh_update(
         arrived,
+        owner_blocks(slot_block),
         core_1,
         mesh_keep,
         mesh_other,

time: 157 us -> 171 us (1.089)
  starting transfers between devices: 20.9 us -> 67.3 us
  waiting for transfers between devices: 106 us -> 74.9 us
    all_to_all x1, waiting for transfers between devices: 52.3 us -> 0.01 us  [per_device(): lax.all_to_all(slot_sums, ('band', 'mp'), split_axis=0, concat_axis=0, ti...]
    ppermute x0 -> x6, starting transfers between devices: none -> 47.9 us  [owner_blocks(): lax.ppermute(table, 'band', [(k, k ^ bit) for k in range(bands)])]
    ppermute x0 -> x6, waiting for transfers between devices: none -> 22.5 us  [owner_blocks(): lax.ppermute(table, 'band', [(k, k ^ bit) for k in range(bands)])]
  transfers between devices with their start and end apart: 8 -> 14, of which waited for: 5 -> 9; matrix products, arithmetic and copies ran while one was open for 1% -> 1% of each run, Pallas kernels for 2% -> 2%
where the time goes in v6:
time: 171 us
  waiting for transfers between devices  74.9 us (44%)
  starting transfers between devices  67.3 us (39%)
  Pallas kernels  26.8 us (16%)
    all_to_all x1, waiting for transfers between devices, per_device(): lax.all_to_all(outgoing, ('band', 'mp'), split_axis=0, concat_axis=0, til...  50.3 us
    ppermute x6, starting transfers between devices, owner_blocks(): lax.ppermute(table, 'band', [(k, k ^ bit) for k in range(bands)])  47.9 us
    ppermute x6, waiting for transfers between devices, owner_blocks(): lax.ppermute(table, 'band', [(k, k ^ bit) for k in range(bands)])  22.5 us
    all_to_all x1, starting transfers between devices, per_device(): lax.all_to_all(slot_sums, ('band', 'mp'), split_axis=0, concat_axis=0, ti...  11.7 us
    pallas_call x1, Pallas kernels, encode(): pl.pallas_call(encode_body, out_shape=pltpu.HBM(sent, BF16), grid_spec=pl...  8.82 us
    pallas_call x1, Pallas kernels, decode(): pl.pallas_call(decode_body, out_shape=jax.ShapeDtypeStruct(grid_blocks.sh...  8.67 us
    all_to_all x1, starting transfers between devices, per_device(): lax.all_to_all(outgoing, ('band', 'mp'), split_axis=0, concat_axis=0, til...  6.78 us
    pallas_call x1, Pallas kernels, mesh_update(): pl.pallas_call(mesh_body, out_shape=(flat, flat, pltpu.HBM(leaving, BF16)...  5.79 us
  transfers between devices with their start and end apart: 14, of which 9 were waited for; matrix products, arithmetic and copies ran while one was open for 1% of the time, Pallas kernels for 2%

profile of v6, /device:TPU:0, one launch (start us, length us, event | category | flops | bytes accessed | tf_op | source)
XLA Modules:
  0.0 171.2 jit_solution(8107811436343319566)
XLA Ops:
  0.8 3.5 %load_encode.1 = (bf16[4096,256]{1,0:T(8,128)(2,1)S(1)}, bf16[512,256]{1,0:T(8,128)(2,1)S(1)}, bf16[192,128,128]{2,1,0:T(8,128)(2,1)S(1)}) custom-call(bf16[4096,256]{1,0:T(8,128)(2,1)} %refs_0_.1, bf16[512,256]{1,0:T(8,128)(2,1)} %refs_1_.1, bf16[192,128,128]{2,1,0:T(8,128)(2,1)} %refs_2_.1), custom_call_target="tpu_custom_call" | custom-call | bytes 16777216 | tf_op jit(solution)/shard_map/load_encode/pallas_call | solution.py:64
  4.3 0.8 collective-permute-done.6.other
  5.1 8.8 %encode.1 = bf16[128,64,256]{2,1,0:T(8,128)(2,1)} custom-call(s32[192]{0:T(256)S(1)} %copy-done.3, s32[192]{0:T(256)S(1)} %copy-done.4, s32[1]{0:T(128)} %bitcast.core_ref, bf16[4096,256]{1,0:T(8,128)(2,1)S(1)} %get-tuple-element.8.own, bf16[4096,256]{1,0:T(8,128)(2,1)S(1)} %collective-permute-done.6.other, bf16[512,256]{1,0:T(8,128)(2,1)S(1)} %get-tuple-element.9.weight, ...), custom_call_target="tpu_custom_call" | custom-call | flops 1610612736 | bytes 16777216 | tf_op jit(solution)/shard_map/encode/pallas_call | solution.py:135
  14.0 11.7 %all-to-all-start = ((bf16[128,64,256]{2,1,0:T(8,128)(2,1)}), bf16[128,64,256]{2,1,0:T(8,128)(2,1)}, u32[]{:S(2)}, u32[]{:S(2)}) async-start(bf16[128,64,256]{2,1,0:T(8,128)(2,1)} %encode.1), calls=%async_computation | async-start | bytes 8388608 | tf_op jit(solution)/shard_map/all_to_all | solution.py:374
  25.7 1.1 collective-permute-start
  26.8 9.8 %collective-permute-done = s32[1,64]{1,0:T(1,128)S(1)} collective-permute-done((s32[1,64]{1,0:T(1,128)S(1)}, s32[1,64]{1,0:T(1,128)S(1)}, u32[]{:S(2)}, u32[]{:S(2)}) %collective-permute-start) | collective-permute-done | bytes 288 | tf_op jit(solution)/shard_map/ppermute | solution.py:331
  36.6 18.1 %collective-permute-start.1 = (s32[2,64]{1,0:T(2,128)S(1)}, s32[2,64]{1,0:T(2,128)S(1)}, u32[]{:S(2)}, u32[]{:S(2)}) collective-permute-start(s32[2,64]{1,0:T(2,128)S(1)} %pad_add_fusion.2), channel_id=1, source_target_pairs={{0,4},{2,6},{4,0},{6,2},{8,12},{10,14},{12,8},{14,10},{16,20},{18,... | collective-permute-start | bytes 1544 | tf_op jit(solution)/shard_map/ppermute | solution.py:331
  54.7 3.6 %collective-permute-done.1 = s32[2,64]{1,0:T(2,128)S(1)} collective-permute-done((s32[2,64]{1,0:T(2,128)S(1)}, s32[2,64]{1,0:T(2,128)S(1)}, u32[]{:S(2)}, u32[]{:S(2)}) %collective-permute-start.1) | collective-permute-done | bytes 544 | tf_op jit(solution)/shard_map/ppermute | solution.py:331
  58.3 23.0 %collective-permute-start.2 = (s32[4,64]{1,0:T(4,128)S(1)}, s32[4,64]{1,0:T(4,128)S(1)}, u32[]{:S(2)}, u32[]{:S(2)}) collective-permute-start(s32[4,64]{1,0:T(4,128)S(1)} %pad_add_fusion.1), channel_id=1, source_target_pairs={{0,8},{2,10},{4,12},{6,14},{8,0},{10,2},{12,4},{14,6},{16,24},{18,... | collective-permute-start | bytes 3080 | tf_op jit(solution)/shard_map/ppermute | solution.py:331
  81.4 1.4 collective-permute-done.2
  82.8 3.2 %collective-permute-start.3 = (s32[8,64]{1,0:T(8,128)S(1)}, s32[8,64]{1,0:T(8,128)S(1)}, u32[]{:S(2)}, u32[]{:S(2)}) collective-permute-start(s32[8,64]{1,0:T(8,128)S(1)} %pad_add_fusion), channel_id=1, source_target_pairs={{0,16},{2,18},{4,20},{6,22},{8,24},{10,26},{12,28},{14,30},{16,0},... | collective-permute-start | bytes 6152 | tf_op jit(solution)/shard_map/ppermute | solution.py:331
  86.1 0.5 collective-permute-start.8
  86.7 1.3 collective-permute-done.3
  88.0 1.2 collective-permute-start.4
  89.2 2.5 %collective-permute-done.4 = s32[16,64]{1,0:T(8,128)S(1)} collective-permute-done((s32[16,64]{1,0:T(8,128)S(1)}, s32[16,64]{1,0:T(8,128)S(1)}, u32[]{:S(2)}, u32[]{:S(2)}) %collective-permute-start.4) | collective-permute-done | bytes 4128 | tf_op jit(solution)/shard_map/ppermute | solution.py:331
  91.8 1.3 collective-permute-start.5
  93.0 4.0 %collective-permute-done.5 = s32[32,64]{1,0:T(8,128)S(1)} collective-permute-done((s32[32,64]{1,0:T(8,128)S(1)}, s32[32,64]{1,0:T(8,128)S(1)}, u32[]{:S(2)}, u32[]{:S(2)}) %collective-permute-start.5) | collective-permute-done | bytes 8224 | tf_op jit(solution)/shard_map/ppermute | solution.py:331
  97.2 0.2 select_reduce_fusion.block_ref
  97.4 5.8 %mesh_update.1 = (bf16[256,256]{1,0:T(8,128)(2,1)S(1)}, bf16[256,256]{1,0:T(8,128)(2,1)S(1)}, bf16[128,64,256]{2,1,0:T(8,128)(2,1)}) custom-call(s32[64]{0:T(128)S(1)} %select_reduce_fusion.block_ref, s32[1]{0:T(128)} %bitcast.core_ref, bf16[128,64,256]{2,1,0:T(8,128)(2,1)} %all-to-all-done.arrived_hbm, bf16[256,256]{1,0:T(8,128)(2,1)S(1)} %bitcast.19, ...), custom_call_target="tpu_custom_call" | custom-call | flops 1000000000 | bytes 12582912 | tf_op jit(solution)/shard_map/mesh_update/pallas_call | solution.py:221
  103.3 6.8 %all-to-all-start.1 = ((bf16[128,64,256]{2,1,0:T(8,128)(2,1)}), bf16[128,64,256]{2,1,0:T(8,128)(2,1)}, u32[]{:S(2)}, u32[]{:S(2)}) async-start(bf16[128,64,256]{2,1,0:T(8,128)(2,1)} %get-tuple-element.11), calls=%async_computation.1 | async-start | bytes 8388608 | tf_op jit(solution)/shard_map/all_to_all | solution.py:384
  110.2 1.3 collective-permute-done.11
  111.5 0.7 copy.17
  112.3 50.3 %all-to-all-done.1 = bf16[128,64,256]{2,1,0:T(8,128)(2,1)} async-done(((bf16[128,64,256]{2,1,0:T(8,128)(2,1)}), bf16[128,64,256]{2,1,0:T(8,128)(2,1)}, u32[]{:S(2)}, u32[]{:S(2)}) %all-to-all-start.1) | async-done | bytes 4194336 | tf_op jit(solution)/shard_map/all_to_all | solution.py:384
  162.6 8.7 %decode.1 = bf16[32,128,256]{2,1,0:T(8,128)(2,1)} custom-call(s32[192]{0:T(256)S(1)} %copy-done.5, s32[192]{0:T(256)S(1)} %copy-done.6, bf16[64,128,256]{2,1,0:T(8,128)(2,1)} %bitcast.4.picked_hbm, bf16[32,128,256]{2,1,0:T(8,128)(2,1)S(1)} %bitcast.16, bf16[192,128,128]{2,1,0:T(8,128)(2,1)} %tiles_hbm.1), custom_call_target="tpu_custom_call" | custom-call | flops 1610612736 | bytes 16777216 | tf_op jit(solution)/shard_map/decode/pallas_call | solution.py:298
  (43 shorter events, 0.9 us)
Async XLA Ops:
  0.6 4.5 %collective-permute-start.6 = (bf16[4096,256]{1,0:T(8,128)(2,1)}, bf16[4096,256]{1,0:T(8,128)(2,1)S(1)}, u32[]{:S(2)}, u32[]{:S(2)}) collective-permute-start(bf16[4096,256]{1,0:T(8,128)(2,1)} %refs_0_.1), channel_id=1, source_target_pairs={{0,1},{1,0},{2,3},{3,2},{4,5},{5,4},{6,7},{7,6},{8,9},{9,8},{10,11... | collective-permute-start | bytes 6291464 | tf_op jit(solution)/shard_map/ppermute | solution.py:322
  0.7 4.4 %copy-start.3 = (s32[192]{0:T(256)S(1)}, s32[192]{0:T(256)}, u32[]{:S(2)}) copy-start(s32[192]{0:T(256)} %slot_ref.2) | copy-start | bytes 2308
  0.7 4.3 %copy-start.4 = (s32[192]{0:T(256)S(1)}, s32[192]{0:T(256)}, u32[]{:S(2)}) copy-start(s32[192]{0:T(256)} %source_ref.1) | copy-start | bytes 2308
  13.9 11.8 %copy-start.9 = (s32[1,64]{1,0:T(1,128)S(1)}, s32[1,64]{1,0:T(1,128)}, u32[]{:S(2)}) copy-start(s32[1,64]{1,0:T(1,128)} %param.22) | copy-start | bytes 772
  13.9 67.3 %copy-start.7 = (bf16[256,2,512]{2,1,0:T(2,128)(2,1)S(1)}, bf16[256,2,512]{2,1,0:T(2,128)(2,1)}, u32[]{:S(2)}) copy-start(bf16[256,2,512]{2,1,0:T(2,128)(2,1)} %param.18) | copy-start | bytes 1572868
  13.9 72.0 %copy-start.8 = (bf16[512,256]{1,0:T(8,128)(2,1)S(1)}, bf16[512,256]{1,0:T(8,128)(2,1)}, u32[]{:S(2)}) copy-start(bf16[512,256]{1,0:T(8,128)(2,1)} %param.14) | copy-start | bytes 786436
  14.0 72.2 %copy-start.1 = (bf16[512,256]{1,0:T(8,128)(2,1)S(1)}, bf16[512,256]{1,0:T(8,128)(2,1)}, u32[]{:S(2)}) copy-start(bf16[512,256]{1,0:T(8,128)(2,1)} %self_w.1) | copy-start | bytes 786436
  14.0 72.6 %copy-start.2 = (bf16[512,256]{1,0:T(8,128)(2,1)S(1)}, bf16[512,256]{1,0:T(8,128)(2,1)}, u32[]{:S(2)}) copy-start(bf16[512,256]{1,0:T(8,128)(2,1)} %pool_w.1) | copy-start | bytes 786436
  14.0 83.5 %all-to-all-start = ((bf16[128,64,256]{2,1,0:T(8,128)(2,1)}), bf16[128,64,256]{2,1,0:T(8,128)(2,1)}, u32[]{:S(2)}, u32[]{:S(2)}) async-start(bf16[128,64,256]{2,1,0:T(8,128)(2,1)} %encode.1), calls=%async_computation | async-start | bytes 8388608 | tf_op jit(solution)/shard_map/all_to_all | solution.py:374
  25.7 10.9 %collective-permute-start = (s32[1,64]{1,0:T(1,128)S(1)}, s32[1,64]{1,0:T(1,128)S(1)}, u32[]{:S(2)}, u32[]{:S(2)}) collective-permute-start(s32[1,64]{1,0:T(1,128)S(1)} %copy-done.9), channel_id=1, source_target_pairs={{0,2},{2,0},{4,6},{6,4},{8,10},{10,8},{12,14},{14,12},{16,18},{18,... | collective-permute-start | bytes 776 | tf_op jit(solution)/shard_map/ppermute | solution.py:331
  36.6 21.7 %collective-permute-start.1 = (s32[2,64]{1,0:T(2,128)S(1)}, s32[2,64]{1,0:T(2,128)S(1)}, u32[]{:S(2)}, u32[]{:S(2)}) collective-permute-start(s32[2,64]{1,0:T(2,128)S(1)} %pad_add_fusion.2), channel_id=1, source_target_pairs={{0,4},{2,6},{4,0},{6,2},{8,12},{10,14},{12,8},{14,10},{16,20},{18,... | collective-permute-start | bytes 1544 | tf_op jit(solution)/shard_map/ppermute | solution.py:331
  58.3 24.5 %collective-permute-start.2 = (s32[4,64]{1,0:T(4,128)S(1)}, s32[4,64]{1,0:T(4,128)S(1)}, u32[]{:S(2)}, u32[]{:S(2)}) collective-permute-start(s32[4,64]{1,0:T(4,128)S(1)} %pad_add_fusion.1), channel_id=1, source_target_pairs={{0,8},{2,10},{4,12},{6,14},{8,0},{10,2},{12,4},{14,6},{16,24},{18,... | collective-permute-start | bytes 3080 | tf_op jit(solution)/shard_map/ppermute | solution.py:331
  81.3 16.1 %collective-permute-start.10 = (bf16[256,1024]{1,0:T(8,128)(2,1)S(1)}, bf16[256,1024]{1,0:T(8,128)(2,1)S(1)}, u32[]{:S(2)}, u32[]{:S(2)}) collective-permute-start(bf16[256,1024]{1,0:T(8,128)(2,1)S(1)} %bitcast.17), channel_id=1, source_target_pairs={{0,1},{1,0},{2,3},{3,2},{4,5},{5,4},{6,7},{7,6},{8,9},{9,8},{10,11... | collective-permute-start | bytes 1572872 | tf_op jit(solution)/shard_map/ppermute | solution.py:322
  82.8 5.2 %collective-permute-start.3 = (s32[8,64]{1,0:T(8,128)S(1)}, s32[8,64]{1,0:T(8,128)S(1)}, u32[]{:S(2)}, u32[]{:S(2)}) collective-permute-start(s32[8,64]{1,0:T(8,128)S(1)} %pad_add_fusion), channel_id=1, source_target_pairs={{0,16},{2,18},{4,20},{6,22},{8,24},{10,26},{12,28},{14,30},{16,0},... | collective-permute-start | bytes 6152 | tf_op jit(solution)/shard_map/ppermute | solution.py:331
  86.0 11.4 %collective-permute-start.7 = (bf16[256,256]{1,0:T(8,128)(2,1)S(1)}, bf16[256,256]{1,0:T(8,128)(2,1)S(1)}, u32[]{:S(2)}, u32[]{:S(2)}) collective-permute-start(bf16[256,256]{1,0:T(8,128)(2,1)S(1)} %bitcast.26), channel_id=1, source_target_pairs={{0,1},{1,0},{2,3},{3,2},{4,5},{5,4},{6,7},{7,6},{8,9},{9,8},{10,11... | collective-permute-start | bytes 393224 | tf_op jit(solution)/shard_map/ppermute | solution.py:322
  86.1 11.3 %collective-permute-start.8 = (bf16[512,256]{1,0:T(8,128)(2,1)S(1)}, bf16[512,256]{1,0:T(8,128)(2,1)S(1)}, u32[]{:S(2)}, u32[]{:S(2)}) collective-permute-start(bf16[512,256]{1,0:T(8,128)(2,1)S(1)} %copy-done.1), channel_id=1, source_target_pairs={{0,1},{1,0},{2,3},{3,2},{4,5},{5,4},{6,7},{7,6},{8,9},{9,8},{10,11... | collective-permute-start | bytes 786440 | tf_op jit(solution)/shard_map/ppermute | solution.py:322
  86.6 10.8 %collective-permute-start.9 = (bf16[512,256]{1,0:T(8,128)(2,1)S(1)}, bf16[512,256]{1,0:T(8,128)(2,1)S(1)}, u32[]{:S(2)}, u32[]{:S(2)}) collective-permute-start(bf16[512,256]{1,0:T(8,128)(2,1)S(1)} %copy-done.2), channel_id=1, source_target_pairs={{0,1},{1,0},{2,3},{3,2},{4,5},{5,4},{6,7},{7,6},{8,9},{9,8},{10,11... | collective-permute-start | bytes 786440 | tf_op jit(solution)/shard_map/ppermute | solution.py:322
  88.0 3.7 %collective-permute-start.4 = (s32[16,64]{1,0:T(8,128)S(1)}, s32[16,64]{1,0:T(8,128)S(1)}, u32[]{:S(2)}, u32[]{:S(2)}) collective-permute-start(s32[16,64]{1,0:T(8,128)S(1)} %concatenate.29), channel_id=1, source_target_pairs={{0,32},{2,34},{4,36},{6,38},{8,40},{10,42},{12,44},{14,46},{16,48}... | collective-permute-start | bytes 12296 | tf_op jit(solution)/shard_map/ppermute | solution.py:331
  91.8 5.3 %collective-permute-start.5 = (s32[32,64]{1,0:T(8,128)S(1)}, s32[32,64]{1,0:T(8,128)S(1)}, u32[]{:S(2)}, u32[]{:S(2)}) collective-permute-start(s32[32,64]{1,0:T(8,128)S(1)} %concatenate.30), channel_id=1, source_target_pairs={{0,64},{2,66},{4,68},{6,70},{8,72},{10,74},{12,76},{14,78},{16,80}... | collective-permute-start | bytes 24584 | tf_op jit(solution)/shard_map/ppermute | solution.py:331
  103.2 59.3 %copy-start = (bf16[4096,256]{1,0:T(8,128)(2,1)S(1)}, bf16[4096,256]{1,0:T(8,128)(2,1)}, u32[]{:S(2)}) copy-start(bf16[4096,256]{1,0:T(8,128)(2,1)} %refs_0_.1) | copy-start | bytes 6291460
  103.2 59.3 %copy-start.5 = (s32[192]{0:T(256)S(1)}, s32[192]{0:T(256)}, u32[]{:S(2)}) copy-start(s32[192]{0:T(256)} %slot_ref.3) | copy-start | bytes 2308
  103.3 59.3 %copy-start.6 = (s32[192]{0:T(256)S(1)}, s32[192]{0:T(256)}, u32[]{:S(2)}) copy-start(s32[192]{0:T(256)} %target_ref.1) | copy-start | bytes 2308
  103.3 59.3 %all-to-all-start.1 = ((bf16[128,64,256]{2,1,0:T(8,128)(2,1)}), bf16[128,64,256]{2,1,0:T(8,128)(2,1)}, u32[]{:S(2)}, u32[]{:S(2)}) async-start(bf16[128,64,256]{2,1,0:T(8,128)(2,1)} %get-tuple-element.11), calls=%async_computation.1 | async-start | bytes 8388608 | tf_op jit(solution)/shard_map/all_to_all | solution.py:384
  110.1 1.4 collective-permute-start.11

commit v7 on v4

--- a/solution.py
+++ b/solution.py
@@ -50,36 +50,41 @@
 NARROW = pltpu.CompilerParams(vmem_limit_bytes=44 * MB)
 
 
-def load_body(count, *refs):
-    sources, targets, semaphores = refs[:count], refs[-count - 1 : -1], refs[-1]
+def load_body(*refs):
+    semaphores, sums, refs = refs[-1], refs[-2], refs[:-2]
+    sources, targets = refs[: len(refs) // 2], refs[len(refs) // 2 :]
     copies = [pltpu.make_async_copy(x, y, semaphores.at[k]) for k, (x, y) in enumerate(zip(sources, targets))]
     for copy in copies:
         copy.start()
+
+    @pl.loop(0, sums.shape[0], unroll=4)
+    def _(k):
+        sums[k] = jnp.zeros(sums.shape[1:], F32)
+
     for copy in copies:
         copy.wait()
 
 
-def load(name, arrays, after=()):
+def load(arrays, sums):
     count = len(arrays)
     return pl.pallas_call(
-        functools.partial(load_body, count),
-        out_shape=tuple(pltpu.VMEM(a.shape, a.dtype) for a in arrays),
-        in_specs=[hbm()] * (count + len(after)),
-        out_specs=tuple(vmem() for _ in arrays),
+        load_body,
+        out_shape=(*[pltpu.VMEM(a.shape, a.dtype) for a in arrays], pltpu.VMEM(sums, F32)),
+        in_specs=[hbm()] * count,
+        out_specs=tuple(vmem() for _ in range(count + 1)),
         scratch_shapes=[pltpu.SemaphoreType.DMA((count,))],
-        compiler_params=pltpu.CompilerParams(vmem_limit_bytes=24 * MB),
+        compiler_params=pltpu.CompilerParams(vmem_limit_bytes=32 * MB),
         cost_estimate=pl.CostEstimate(flops=0, bytes_accessed=16 * MB, transcendentals=0),
-        name=name,
-    )(*stay(*arrays), *stay(*after))
+        name="load_encode",
+    )(*stay(*arrays))
 
 
 PIECES = 4
-UNROLL = 48
 TAG = 8
 
 
 def encode_body(
-    slot_ref, source_ref, link_ref, core_ref, own, other, weight, tiles, out_hbm, message, acc, out, out_sem,
+    slot_ref, source_ref, link_ref, core_ref, own, other, weight, tiles, _, out_hbm, acc, message, out, out_sem,
 ):
     core = core_ref[0]
     blocks, edge, width = message.shape
@@ -87,27 +92,17 @@
     count = tiles.shape[0]
     rows = edge // 2
     lanes = out.shape[2]
-    inner = 8 * edge
-    per = blocks * edge // inner // PIECES
-    cleared = slots // (per * PIECES)
-
-    @pl.loop(0, PIECES)
-    def _(piece):
-        @pl.loop(0, per)
-        def _(j):
-            step = piece * per + j
-            at = pl.ds(pl.multiple_of(step * inner, inner), inner)
-            z = dot(own[at, :], weight[half(core, width), :]) + dot(other[at, :], weight[half(1 - core, width), :])
-            message[pl.ds(step * 8, 8)] = silu(z).astype(BF16).reshape(8, edge, width)
-            acc[pl.ds(step * cleared, cleared)] = jnp.zeros((cleared, edge, width), F32)
-
-    @pl.loop(0, PIECES)
-    def _(piece):
-        @pl.loop(0, count // PIECES // UNROLL)
-        def _(j):
-            base = piece * (count // PIECES) + j * UNROLL
-            for i in range(UNROLL):
-                acc[slot_ref[base + i]] += dot(tiles[base + i], message[source_ref[base + i]])
+    many = blocks // 2
+    inner = many * edge
+
+    @pl.loop(0, 2)
+    def _(step):
+        at = pl.ds(pl.multiple_of(step * inner, inner), inner)
+        z = dot(own[at, :], weight[half(core, width), :]) + dot(other[at, :], weight[half(1 - core, width), :])
+        message[pl.ds(step * many, many)] = silu(z).astype(BF16).reshape(many, edge, width)
+
+    for i in range(count):
+        acc[slot_ref[i]] += dot(tiles[i], message[source_ref[i]])
 
     size = 2 * slots // PIECES
 
@@ -135,21 +130,21 @@
         leave(piece).wait()
 
 
-def encode(own, other, weight, tiles, source, slot, link, core, slots):
+def encode(own, other, weight, tiles, sums, source, slot, link, core, slots):
     count, edge, _ = tiles.shape
     width = weight.shape[1]
     sent = (2 * slots, edge + TAG, width // 2)
     dma = pltpu.SemaphoreType.DMA
     return pl.pallas_call(
         encode_body,
-        out_shape=pltpu.HBM(sent, BF16),
+        out_shape=(pltpu.HBM(sent, BF16), pltpu.VMEM(sums.shape, F32)),
+        input_output_aliases={8: 1},
         grid_spec=pltpu.PrefetchScalarGridSpec(
             num_scalar_prefetch=4,
-            in_specs=[vmem()] * 4,
-            out_specs=hbm(),
+            in_specs=[vmem()] * 5,
+            out_specs=(hbm(), vmem()),
             scratch_shapes=[
                 pltpu.VMEM((own.shape[0] // edge, edge, width), BF16),
-                pltpu.VMEM((slots, edge, width), F32),
                 pltpu.VMEM(sent, BF16),
                 dma((PIECES,)),
             ],
@@ -159,7 +154,7 @@
             flops=2 * count * edge * edge * width, bytes_accessed=16 * MB, transcendentals=own.shape[0] * width
         ),
         name="encode",
-    )(slot, source, link, core, own, other, weight, tiles)
+    )(slot, source, link, core, own, other, weight, tiles, sums)[0]
 
 
 def mesh_body(
@@ -271,12 +266,16 @@
     count = tiles.shape[0]
     blocks = acc.shape[0]
     picked_start, picked_ready = fetch(picked_hbm, picked, picked_sem, PIECES)
-    tiles_start, tiles_ready = fetch(tiles_hbm, tiles, tiles_sem, PIECES)
+    ends = [0, count // 4, count * 5 // 8, count]
+
+    def bring(k):
+        at = pl.ds(ends[k], ends[k + 1] - ends[k])
+        return pltpu.make_async_copy(tiles_hbm.at[at], tiles.at[at], tiles_sem.at[k])
+
     per = blocks // PIECES
     for piece in range(PIECES):
         picked_start(piece)
-    for piece in range(PIECES):
-        tiles_start(piece)
+    bring(0).start()
 
     @pl.loop(0, PIECES)
     def _(piece):
@@ -286,16 +285,12 @@
 
     for piece in range(PIECES):
         picked_ready(piece)
-
-    @pl.loop(0, PIECES)
-    def _(piece):
-        tiles_ready(piece)
-
-        @pl.loop(0, count // PIECES // UNROLL)
-        def _(j):
-            base = piece * (count // PIECES) + j * UNROLL
-            for i in range(UNROLL):
-                acc[target_ref[base + i]] += dot(tiles[base + i], picked[slot_ref[base + i]])
+    for k in range(1, 3):
+        bring(k).start()
+    for k in range(3):
+        bring(k).wait()
+        for i in range(ends[k], ends[k + 1]):
+            acc[target_ref[i]] += dot(tiles[i], picked[slot_ref[i]])
 
     def leave(k):
         at = pl.ds(k * per, per)
@@ -375,9 +370,9 @@
     mesh_other = swap(mesh_send)
     self_other, pooled_other, out_other = swap(self_weight), swap(pooled_weight), swap(out_flat)
 
-    own, near_weight, near_tiles = load("load_encode", (grid_nodes, send_weight, encode_tiles))
+    own, near_weight, near_tiles, sums = load((grid_nodes, send_weight, encode_tiles), (bands, edge, width))
     slot_sums = encode(
-        own, grid_other, near_weight, near_tiles, encode_source, encode_slot, slot_block[0], core_1, bands
+        own, grid_other, near_weight, near_tiles, sums, encode_source, encode_slot, slot_block[0], core_1, bands
     )
     arrived = lax.all_to_all(slot_sums, ("band", "mp"), split_axis=0, concat_axis=0, tiled=True)
     keep, send, outgoing = mesh_update(

time: 157 us -> 155 us (0.987)
  Pallas kernels: 27.7 us -> 25.7 us
where the time goes in v7:
time: 155 us
  waiting for transfers between devices  106 us (68%)
  Pallas kernels  25.7 us (17%)
  starting transfers between devices  21.1 us (14%)
    all_to_all x1, waiting for transfers between devices, per_device(): lax.all_to_all(slot_sums, ('band', 'mp'), split_axis=0, concat_axis=0, ti...  52.3 us
    all_to_all x1, waiting for transfers between devices, per_device(): lax.all_to_all(outgoing, ('band', 'mp'), split_axis=0, concat_axis=0, til...  50.1 us
    all_to_all x1, starting transfers between devices, per_device(): lax.all_to_all(slot_sums, ('band', 'mp'), split_axis=0, concat_axis=0, ti...  11.6 us
    pallas_call x1, Pallas kernels, decode(): pl.pallas_call(decode_body, out_shape=jax.ShapeDtypeStruct(grid_blocks.sh...  8.77 us
    all_to_all x1, starting transfers between devices, per_device(): lax.all_to_all(outgoing, ('band', 'mp'), split_axis=0, concat_axis=0, til...  7.92 us
    pallas_call x1, Pallas kernels, encode(): pl.pallas_call(encode_body, out_shape=(pltpu.HBM(sent, BF16), pltpu.VMEM(...  7.72 us
    pallas_call x1, Pallas kernels, mesh_update(): pl.pallas_call(mesh_body, out_shape=(flat, flat, pltpu.HBM(leaving, BF16)...  5.68 us
    ppermute x6, waiting for transfers between devices, swap(): return lax.ppermute(x, 'mp', SWAP)  3.87 us
  transfers between devices with their start and end apart: 8, of which 5 were waited for; matrix products, arithmetic and copies ran while one was open for 1% of the time, Pallas kernels for 2%

profile of v7, /device:TPU:0, one launch (start us, length us, event | category | flops | bytes accessed | tf_op | source)
XLA Modules:
  0.0 155.0 jit_solution(13715477502441751219)
XLA Ops:
  0.7 0.1 collective-permute-start
  0.8 3.5 %load_encode.1 = (bf16[4096,256]{1,0:T(8,128)(2,1)S(1)}, bf16[512,256]{1,0:T(8,128)(2,1)S(1)}, bf16[192,128,128]{2,1,0:T(8,128)(2,1)S(1)}, f32[64,128,256]{2,1,0:T(8,128)S(1)}) custom-call(bf16[4096,256]{1,0:T(8,128)(2,1)} %refs_0_.1, bf16[512,256]{1,0:T(8,128)(2,1)} %refs_1_.1, bf16[192,128,128]{2,1,0:T(8,128)(2,1)} %refs_2_.1), custom_call_target="tpu_custom_call" | custom-call | bytes 16777216 | tf_op jit(solution)/shard_map/load_encode/pallas_call | solution.py:70
  4.3 0.8 collective-permute-done.other
  5.1 7.7 %encode.1 = (bf16[128,136,128]{2,1,0:T(8,128)(2,1)}, f32[64,128,256]{2,1,0:T(8,128)S(1)}) custom-call(s32[192]{0:T(256)S(1)} %copy-done.3, s32[192]{0:T(256)S(1)} %copy-done.4, s32[64]{0:T(128)S(1)} %bitcast.21, s32[1]{0:T(128)} %bitcast.core_ref, bf16[4096,256]{1,0:T(8,128)(2,1)S(1)} %get-tuple-element.10.own, ...), custom_call_target="tpu_custom_call", output_to_operand_aliasing={{1}: (8, {})} | custom-call | flops 1610612736 | bytes 16777216 | tf_op jit(solution)/shard_map/encode/pallas_call | solution.py:138
  12.8 0.0 copy-start.8
  12.9 0.0 copy-start.2
  12.9 0.0 copy-start.9
  12.9 11.6 %all-to-all-start = ((bf16[128,136,128]{2,1,0:T(8,128)(2,1)}), bf16[128,136,128]{2,1,0:T(8,128)(2,1)}, u32[]{:S(2)}, u32[]{:S(2)}) async-start(bf16[128,136,128]{2,1,0:T(8,128)(2,1)} %get-tuple-element.14), calls=%async_computation | async-start | bytes 8912896 | tf_op jit(solution)/shard_map/all_to_all | solution.py:377
  24.6 0.1 copy.21
  24.6 0.1 collective-permute-start.4
  24.7 0.5 collective-permute-start.2
  25.2 0.1 collective-permute-start.3
  25.3 0.5 collective-permute-start.1
  25.8 1.7 %collective-permute-done.1.theirs_ref = bf16[256,256]{1,0:T(8,128)(2,1)S(1)} collective-permute-done((bf16[256,256]{1,0:T(8,128)(2,1)S(1)}, bf16[256,256]{1,0:T(8,128)(2,1)S(1)}, u32[]{:S(2)}, u32[]{:S(2)}) %collective-permute-start.1) | collective-permute-done | bytes 131104 | tf_op jit(solution)/shard_map/ppermute | solution.py:339
  27.6 52.3 %all-to-all-done.arrived_hbm = bf16[128,136,128]{2,1,0:T(8,128)(2,1)} async-done(((bf16[128,136,128]{2,1,0:T(8,128)(2,1)}), bf16[128,136,128]{2,1,0:T(8,128)(2,1)}, u32[]{:S(2)}, u32[]{:S(2)}) %all-to-all-start) | async-done | bytes 4456480 | tf_op jit(solution)/shard_map/all_to_all | solution.py:377
  79.9 5.7 %mesh_update.1 = (bf16[256,256]{1,0:T(8,128)(2,1)S(1)}, bf16[256,256]{1,0:T(8,128)(2,1)S(1)}, bf16[128,64,256]{2,1,0:T(8,128)(2,1)}) custom-call(s32[1]{0:T(128)} %bitcast.core_ref, bf16[128,136,128]{2,1,0:T(8,128)(2,1)} %all-to-all-done.arrived_hbm, bf16[256,256]{1,0:T(8,128)(2,1)S(1)} %bitcast.20, bf16[256,256]{1,0:T(8,128)(2,1)S(1)} %collective-permute-done.1.theirs_ref, ...), custom_call_target="tpu_custom_call" | custom-call | flops 1000000000 | bytes 12582912 | tf_op jit(solution)/shard_map/mesh_update/pallas_call | solution.py:238
  85.6 0.0 copy-start.5
  85.6 0.0 copy-start.6
  85.6 7.9 %all-to-all-start.1 = ((bf16[128,64,256]{2,1,0:T(8,128)(2,1)}), bf16[128,64,256]{2,1,0:T(8,128)(2,1)}, u32[]{:S(2)}, u32[]{:S(2)}) async-start(bf16[128,64,256]{2,1,0:T(8,128)(2,1)} %get-tuple-element.15), calls=%async_computation.1 | async-start | bytes 8388608 | tf_op jit(solution)/shard_map/all_to_all | solution.py:386
  93.6 0.3 collective-permute-start.5
  93.8 1.3 collective-permute-done.5
  95.2 0.7 copy.18
  96.0 50.1 %all-to-all-done.1 = bf16[128,64,256]{2,1,0:T(8,128)(2,1)} async-done(((bf16[128,64,256]{2,1,0:T(8,128)(2,1)}), bf16[128,64,256]{2,1,0:T(8,128)(2,1)}, u32[]{:S(2)}, u32[]{:S(2)}) %all-to-all-start.1) | async-done | bytes 4194336 | tf_op jit(solution)/shard_map/all_to_all | solution.py:386
  146.1 8.8 %decode.1 = bf16[32,128,256]{2,1,0:T(8,128)(2,1)} custom-call(s32[192]{0:T(256)S(1)} %copy-done.5, s32[192]{0:T(256)S(1)} %copy-done.6, bf16[64,128,256]{2,1,0:T(8,128)(2,1)} %bitcast.5.picked_hbm, bf16[32,128,256]{2,1,0:T(8,128)(2,1)S(1)} %bitcast.17, bf16[192,128,128]{2,1,0:T(8,128)(2,1)} %tiles_hbm.1), custom_call_target="tpu_custom_call" | custom-call | flops 1610612736 | bytes 16777216 | tf_op jit(solution)/shard_map/decode/pallas_call | solution.py:315
  (21 shorter events, 0.1 us)
Async XLA Ops:
  0.6 4.5 %copy-start.3 = (s32[192]{0:T(256)S(1)}, s32[192]{0:T(256)}, u32[]{:S(2)}) copy-start(s32[192]{0:T(256)} %slot_ref.2) | copy-start | bytes 2308
  0.6 4.5 %copy-start.4 = (s32[192]{0:T(256)S(1)}, s32[192]{0:T(256)}, u32[]{:S(2)}) copy-start(s32[192]{0:T(256)} %source_ref.1) | copy-start | bytes 2308
  0.7 4.5 %copy-start.7 = (s32[1,64]{1,0:T(1,128)S(1)}, s32[1,64]{1,0:T(1,128)}, u32[]{:S(2)}) copy-start(s32[1,64]{1,0:T(1,128)} %param.22) | copy-start | bytes 772
  0.7 4.5 %collective-permute-start = (bf16[4096,256]{1,0:T(8,128)(2,1)}, bf16[4096,256]{1,0:T(8,128)(2,1)S(1)}, u32[]{:S(2)}, u32[]{:S(2)}) collective-permute-start(bf16[4096,256]{1,0:T(8,128)(2,1)} %refs_0_.1), channel_id=1, source_target_pairs={{0,1},{1,0},{2,3},{3,2},{4,5},{5,4},{6,7},{7,6},{8,9},{9,8},{10,11... | collective-permute-start | bytes 6291464 | tf_op jit(solution)/shard_map/ppermute | solution.py:339
  12.8 11.7 %copy-start.8 = (bf16[256,2,512]{2,1,0:T(2,128)(2,1)S(1)}, bf16[256,2,512]{2,1,0:T(2,128)(2,1)}, u32[]{:S(2)}) copy-start(bf16[256,2,512]{2,1,0:T(2,128)(2,1)} %param.18) | copy-start | bytes 1572868
  12.9 11.9 %copy-start.1 = (bf16[512,256]{1,0:T(8,128)(2,1)S(1)}, bf16[512,256]{1,0:T(8,128)(2,1)}, u32[]{:S(2)}) copy-start(bf16[512,256]{1,0:T(8,128)(2,1)} %self_w.1) | copy-start | bytes 786436
  12.9 12.4 %copy-start.2 = (bf16[512,256]{1,0:T(8,128)(2,1)S(1)}, bf16[512,256]{1,0:T(8,128)(2,1)}, u32[]{:S(2)}) copy-start(bf16[512,256]{1,0:T(8,128)(2,1)} %pool_w.1) | copy-start | bytes 786436
  12.9 12.4 %copy-start.9 = (bf16[512,256]{1,0:T(8,128)(2,1)S(1)}, bf16[512,256]{1,0:T(8,128)(2,1)}, u32[]{:S(2)}) copy-start(bf16[512,256]{1,0:T(8,128)(2,1)} %param.14) | copy-start | bytes 786436
  12.9 67.0 %all-to-all-start = ((bf16[128,136,128]{2,1,0:T(8,128)(2,1)}), bf16[128,136,128]{2,1,0:T(8,128)(2,1)}, u32[]{:S(2)}, u32[]{:S(2)}) async-start(bf16[128,136,128]{2,1,0:T(8,128)(2,1)} %get-tuple-element.14), calls=%async_computation | async-start | bytes 8912896 | tf_op jit(solution)/shard_map/all_to_all | solution.py:377
  24.6 2.9 %collective-permute-start.4 = (bf16[256,1024]{1,0:T(8,128)(2,1)S(1)}, bf16[256,1024]{1,0:T(8,128)(2,1)S(1)}, u32[]{:S(2)}, u32[]{:S(2)}) collective-permute-start(bf16[256,1024]{1,0:T(8,128)(2,1)S(1)} %bitcast.18), channel_id=1, source_target_pairs={{0,1},{1,0},{2,3},{3,2},{4,5},{5,4},{6,7},{7,6},{8,9},{9,8},{10,11... | collective-permute-start | bytes 1572872 | tf_op jit(solution)/shard_map/ppermute | solution.py:339
  24.7 2.8 %collective-permute-start.2 = (bf16[512,256]{1,0:T(8,128)(2,1)S(1)}, bf16[512,256]{1,0:T(8,128)(2,1)S(1)}, u32[]{:S(2)}, u32[]{:S(2)}) collective-permute-start(bf16[512,256]{1,0:T(8,128)(2,1)S(1)} %copy-done.1), channel_id=1, source_target_pairs={{0,1},{1,0},{2,3},{3,2},{4,5},{5,4},{6,7},{7,6},{8,9},{9,8},{10,11... | collective-permute-start | bytes 786440 | tf_op jit(solution)/shard_map/ppermute | solution.py:339
  25.2 2.3 %collective-permute-start.3 = (bf16[512,256]{1,0:T(8,128)(2,1)S(1)}, bf16[512,256]{1,0:T(8,128)(2,1)S(1)}, u32[]{:S(2)}, u32[]{:S(2)}) collective-permute-start(bf16[512,256]{1,0:T(8,128)(2,1)S(1)} %copy-done.2), channel_id=1, source_target_pairs={{0,1},{1,0},{2,3},{3,2},{4,5},{5,4},{6,7},{7,6},{8,9},{9,8},{10,11... | collective-permute-start | bytes 786440 | tf_op jit(solution)/shard_map/ppermute | solution.py:339
  25.3 2.2 %collective-permute-start.1 = (bf16[256,256]{1,0:T(8,128)(2,1)S(1)}, bf16[256,256]{1,0:T(8,128)(2,1)S(1)}, u32[]{:S(2)}, u32[]{:S(2)}) collective-permute-start(bf16[256,256]{1,0:T(8,128)(2,1)S(1)} %bitcast.28), channel_id=1, source_target_pairs={{0,1},{1,0},{2,3},{3,2},{4,5},{5,4},{6,7},{7,6},{8,9},{9,8},{10,11... | collective-permute-start | bytes 393224 | tf_op jit(solution)/shard_map/ppermute | solution.py:339
  85.6 60.5 %copy-start = (bf16[4096,256]{1,0:T(8,128)(2,1)S(1)}, bf16[4096,256]{1,0:T(8,128)(2,1)}, u32[]{:S(2)}) copy-start(bf16[4096,256]{1,0:T(8,128)(2,1)} %refs_0_.1) | copy-start | bytes 6291460
  85.6 60.5 %copy-start.5 = (s32[192]{0:T(256)S(1)}, s32[192]{0:T(256)}, u32[]{:S(2)}) copy-start(s32[192]{0:T(256)} %slot_ref.3) | copy-start | bytes 2308
  85.6 60.4 %copy-start.6 = (s32[192]{0:T(256)S(1)}, s32[192]{0:T(256)}, u32[]{:S(2)}) copy-start(s32[192]{0:T(256)} %target_ref.1) | copy-start | bytes 2308
  85.6 60.4 %all-to-all-start.1 = ((bf16[128,64,256]{2,1,0:T(8,128)(2,1)}), bf16[128,64,256]{2,1,0:T(8,128)(2,1)}, u32[]{:S(2)}, u32[]{:S(2)}) async-start(bf16[128,64,256]{2,1,0:T(8,128)(2,1)} %get-tuple-element.15), calls=%async_computation.1 | async-start | bytes 8388608 | tf_op jit(solution)/shard_map/all_to_all | solution.py:386
  93.6 1.6 %collective-permute-start.5 = (bf16[256,256]{1,0:T(8,128)(2,1)S(1)}, bf16[256,256]{1,0:T(8,128)(2,1)S(1)}, u32[]{:S(2)}, u32[]{:S(2)}) collective-permute-start(bf16[256,256]{1,0:T(8,128)(2,1)S(1)} %get-tuple-element.17), channel_id=1, source_target_pairs={{0,1},{1,0},{2,3},{3,2},{4,5},{5,4},{6,7},{7,6},{8,9},{9,8},{10,11... | collective-permute-start | bytes 393224 | tf_op jit(solution)/shard_map/ppermute | solution.py:339

commit v8 on v7

--- a/solution.py
+++ b/solution.py
@@ -92,14 +92,8 @@
     count = tiles.shape[0]
     rows = edge // 2
     lanes = out.shape[2]
-    many = blocks // 2
-    inner = many * edge
-
-    @pl.loop(0, 2)
-    def _(step):
-        at = pl.ds(pl.multiple_of(step * inner, inner), inner)
-        z = dot(own[at, :], weight[half(core, width), :]) + dot(other[at, :], weight[half(1 - core, width), :])
-        message[pl.ds(step * many, many)] = silu(z).astype(BF16).reshape(many, edge, width)
+    z = dot(own[...], weight[half(core, width), :]) + dot(other[...], weight[half(1 - core, width), :])
+    message[...] = silu(z).astype(BF16).reshape(blocks, edge, width)
 
     for i in range(count):
         acc[slot_ref[i]] += dot(tiles[i], message[source_ref[i]])

time: 155 us -> 157 us (1.013)
  Pallas kernels: 25.7 us -> 27.7 us
    pallas_call x1, Pallas kernels: 7.72 us -> 9.74 us  [encode(): pl.pallas_call(encode_body, out_shape=(pltpu.HBM(sent, BF16), pltpu.VMEM(...]
where the time goes in v8:
time: 157 us
  waiting for transfers between devices  106 us (68%)
  Pallas kernels  27.7 us (18%)
  starting transfers between devices  21.1 us (13%)
    all_to_all x1, waiting for transfers between devices, per_device(): lax.all_to_all(slot_sums, ('band', 'mp'), split_axis=0, concat_axis=0, ti...  52.3 us
    all_to_all x1, waiting for transfers between devices, per_device(): lax.all_to_all(outgoing, ('band', 'mp'), split_axis=0, concat_axis=0, til...  50.1 us
    all_to_all x1, starting transfers between devices, per_device(): lax.all_to_all(slot_sums, ('band', 'mp'), split_axis=0, concat_axis=0, ti...  11.6 us
    pallas_call x1, Pallas kernels, encode(): pl.pallas_call(encode_body, out_shape=(pltpu.HBM(sent, BF16), pltpu.VMEM(...  9.74 us
    pallas_call x1, Pallas kernels, decode(): pl.pallas_call(decode_body, out_shape=jax.ShapeDtypeStruct(grid_blocks.sh...  8.77 us
    all_to_all x1, starting transfers between devices, per_device(): lax.all_to_all(outgoing, ('band', 'mp'), split_axis=0, concat_axis=0, til...  7.93 us
    pallas_call x1, Pallas kernels, mesh_update(): pl.pallas_call(mesh_body, out_shape=(flat, flat, pltpu.HBM(leaving, BF16)...  5.68 us
    ppermute x6, waiting for transfers between devices, swap(): return lax.ppermute(x, 'mp', SWAP)  3.87 us
  transfers between devices with their start and end apart: 8, of which 5 were waited for; matrix products, arithmetic and copies ran while one was open for 1% of the time, Pallas kernels for 2%

profile of v8, /device:TPU:0, one launch (start us, length us, event | category | flops | bytes accessed | tf_op | source)
XLA Modules:
  0.0 157.0 jit_solution(14760692525567945422)
XLA Ops:
  0.7 0.1 collective-permute-start
  0.8 3.5 %load_encode.1 = (bf16[4096,256]{1,0:T(8,128)(2,1)S(1)}, bf16[512,256]{1,0:T(8,128)(2,1)S(1)}, bf16[192,128,128]{2,1,0:T(8,128)(2,1)S(1)}, f32[64,128,256]{2,1,0:T(8,128)S(1)}) custom-call(bf16[4096,256]{1,0:T(8,128)(2,1)} %refs_0_.1, bf16[512,256]{1,0:T(8,128)(2,1)} %refs_1_.1, bf16[192,128,128]{2,1,0:T(8,128)(2,1)} %refs_2_.1), custom_call_target="tpu_custom_call" | custom-call | bytes 16777216 | tf_op jit(solution)/shard_map/load_encode/pallas_call | solution.py:70
  4.3 0.8 collective-permute-done.other
  5.1 9.7 %encode.1 = (bf16[128,136,128]{2,1,0:T(8,128)(2,1)}, f32[64,128,256]{2,1,0:T(8,128)S(1)}) custom-call(s32[192]{0:T(256)S(1)} %copy-done.3, s32[192]{0:T(256)S(1)} %copy-done.4, s32[64]{0:T(128)S(1)} %bitcast.21, s32[1]{0:T(128)} %bitcast.core_ref, bf16[4096,256]{1,0:T(8,128)(2,1)S(1)} %get-tuple-element.10.own, ...), custom_call_target="tpu_custom_call", output_to_operand_aliasing={{1}: (8, {})} | custom-call | flops 1610612736 | bytes 16777216 | tf_op jit(solution)/shard_map/encode/pallas_call | solution.py:132
  14.9 0.0 copy-start.8
  14.9 0.0 copy-start.1
  14.9 0.0 copy-start.2
  14.9 11.6 %all-to-all-start = ((bf16[128,136,128]{2,1,0:T(8,128)(2,1)}), bf16[128,136,128]{2,1,0:T(8,128)(2,1)}, u32[]{:S(2)}, u32[]{:S(2)}) async-start(bf16[128,136,128]{2,1,0:T(8,128)(2,1)} %get-tuple-element.14), calls=%async_computation | async-start | bytes 8912896 | tf_op jit(solution)/shard_map/all_to_all | solution.py:371
  26.6 0.1 copy.21
  26.7 0.1 collective-permute-start.4
  26.8 0.5 collective-permute-start.2
  27.2 0.1 collective-permute-start.3
  27.4 0.5 collective-permute-start.1
  27.9 1.7 %collective-permute-done.1.theirs_ref = bf16[256,256]{1,0:T(8,128)(2,1)S(1)} collective-permute-done((bf16[256,256]{1,0:T(8,128)(2,1)S(1)}, bf16[256,256]{1,0:T(8,128)(2,1)S(1)}, u32[]{:S(2)}, u32[]{:S(2)}) %collective-permute-start.1) | collective-permute-done | bytes 131104 | tf_op jit(solution)/shard_map/ppermute | solution.py:333
  29.6 52.3 %all-to-all-done.arrived_hbm = bf16[128,136,128]{2,1,0:T(8,128)(2,1)} async-done(((bf16[128,136,128]{2,1,0:T(8,128)(2,1)}), bf16[128,136,128]{2,1,0:T(8,128)(2,1)}, u32[]{:S(2)}, u32[]{:S(2)}) %all-to-all-start) | async-done | bytes 4456480 | tf_op jit(solution)/shard_map/all_to_all | solution.py:371
  81.9 5.7 %mesh_update.1 = (bf16[256,256]{1,0:T(8,128)(2,1)S(1)}, bf16[256,256]{1,0:T(8,128)(2,1)S(1)}, bf16[128,64,256]{2,1,0:T(8,128)(2,1)}) custom-call(s32[1]{0:T(128)} %bitcast.core_ref, bf16[128,136,128]{2,1,0:T(8,128)(2,1)} %all-to-all-done.arrived_hbm, bf16[256,256]{1,0:T(8,128)(2,1)S(1)} %bitcast.20, bf16[256,256]{1,0:T(8,128)(2,1)S(1)} %collective-permute-done.1.theirs_ref, ...), custom_call_target="tpu_custom_call" | custom-call | flops 1000000000 | bytes 12582912 | tf_op jit(solution)/shard_map/mesh_update/pallas_call | solution.py:232
  87.6 0.0 copy-start.5
  87.6 0.0 copy-start.6
  87.7 7.9 %all-to-all-start.1 = ((bf16[128,64,256]{2,1,0:T(8,128)(2,1)}), bf16[128,64,256]{2,1,0:T(8,128)(2,1)}, u32[]{:S(2)}, u32[]{:S(2)}) async-start(bf16[128,64,256]{2,1,0:T(8,128)(2,1)} %get-tuple-element.15), calls=%async_computation.1 | async-start | bytes 8388608 | tf_op jit(solution)/shard_map/all_to_all | solution.py:380
  95.6 0.3 collective-permute-start.5
  95.9 1.3 collective-permute-done.5
  97.3 0.7 copy.18
  98.0 50.1 %all-to-all-done.1 = bf16[128,64,256]{2,1,0:T(8,128)(2,1)} async-done(((bf16[128,64,256]{2,1,0:T(8,128)(2,1)}), bf16[128,64,256]{2,1,0:T(8,128)(2,1)}, u32[]{:S(2)}, u32[]{:S(2)}) %all-to-all-start.1) | async-done | bytes 4194336 | tf_op jit(solution)/shard_map/all_to_all | solution.py:380
  148.1 8.8 %decode.1 = bf16[32,128,256]{2,1,0:T(8,128)(2,1)} custom-call(s32[192]{0:T(256)S(1)} %copy-done.5, s32[192]{0:T(256)S(1)} %copy-done.6, bf16[64,128,256]{2,1,0:T(8,128)(2,1)} %bitcast.5.picked_hbm, bf16[32,128,256]{2,1,0:T(8,128)(2,1)S(1)} %bitcast.17, bf16[192,128,128]{2,1,0:T(8,128)(2,1)} %tiles_hbm.1), custom_call_target="tpu_custom_call" | custom-call | flops 1610612736 | bytes 16777216 | tf_op jit(solution)/shard_map/decode/pallas_call | solution.py:309
  (21 shorter events, 0.1 us)
Async XLA Ops:
  0.6 4.5 %copy-start.3 = (s32[192]{0:T(256)S(1)}, s32[192]{0:T(256)}, u32[]{:S(2)}) copy-start(s32[192]{0:T(256)} %slot_ref.2) | copy-start | bytes 2308
  0.6 4.5 %copy-start.4 = (s32[192]{0:T(256)S(1)}, s32[192]{0:T(256)}, u32[]{:S(2)}) copy-start(s32[192]{0:T(256)} %source_ref.1) | copy-start | bytes 2308
  0.7 4.5 %copy-start.7 = (s32[1,64]{1,0:T(1,128)S(1)}, s32[1,64]{1,0:T(1,128)}, u32[]{:S(2)}) copy-start(s32[1,64]{1,0:T(1,128)} %param.22) | copy-start | bytes 772
  0.7 4.5 %collective-permute-start = (bf16[4096,256]{1,0:T(8,128)(2,1)}, bf16[4096,256]{1,0:T(8,128)(2,1)S(1)}, u32[]{:S(2)}, u32[]{:S(2)}) collective-permute-start(bf16[4096,256]{1,0:T(8,128)(2,1)} %refs_0_.1), channel_id=1, source_target_pairs={{0,1},{1,0},{2,3},{3,2},{4,5},{5,4},{6,7},{7,6},{8,9},{9,8},{10,11... | collective-permute-start | bytes 6291464 | tf_op jit(solution)/shard_map/ppermute | solution.py:333
  14.9 11.7 %copy-start.8 = (bf16[256,2,512]{2,1,0:T(2,128)(2,1)S(1)}, bf16[256,2,512]{2,1,0:T(2,128)(2,1)}, u32[]{:S(2)}) copy-start(bf16[256,2,512]{2,1,0:T(2,128)(2,1)} %param.18) | copy-start | bytes 1572868
  14.9 11.9 %copy-start.1 = (bf16[512,256]{1,0:T(8,128)(2,1)S(1)}, bf16[512,256]{1,0:T(8,128)(2,1)}, u32[]{:S(2)}) copy-start(bf16[512,256]{1,0:T(8,128)(2,1)} %self_w.1) | copy-start | bytes 786436
  14.9 12.4 %copy-start.2 = (bf16[512,256]{1,0:T(8,128)(2,1)S(1)}, bf16[512,256]{1,0:T(8,128)(2,1)}, u32[]{:S(2)}) copy-start(bf16[512,256]{1,0:T(8,128)(2,1)} %pool_w.1) | copy-start | bytes 786436
  14.9 12.4 %copy-start.9 = (bf16[512,256]{1,0:T(8,128)(2,1)S(1)}, bf16[512,256]{1,0:T(8,128)(2,1)}, u32[]{:S(2)}) copy-start(bf16[512,256]{1,0:T(8,128)(2,1)} %param.14) | copy-start | bytes 786436
  14.9 67.0 %all-to-all-start = ((bf16[128,136,128]{2,1,0:T(8,128)(2,1)}), bf16[128,136,128]{2,1,0:T(8,128)(2,1)}, u32[]{:S(2)}, u32[]{:S(2)}) async-start(bf16[128,136,128]{2,1,0:T(8,128)(2,1)} %get-tuple-element.14), calls=%async_computation | async-start | bytes 8912896 | tf_op jit(solution)/shard_map/all_to_all | solution.py:371
  26.7 2.9 %collective-permute-start.4 = (bf16[256,1024]{1,0:T(8,128)(2,1)S(1)}, bf16[256,1024]{1,0:T(8,128)(2,1)S(1)}, u32[]{:S(2)}, u32[]{:S(2)}) collective-permute-start(bf16[256,1024]{1,0:T(8,128)(2,1)S(1)} %bitcast.18), channel_id=1, source_target_pairs={{0,1},{1,0},{2,3},{3,2},{4,5},{5,4},{6,7},{7,6},{8,9},{9,8},{10,11... | collective-permute-start | bytes 1572872 | tf_op jit(solution)/shard_map/ppermute | solution.py:333
  26.8 2.8 %collective-permute-start.2 = (bf16[512,256]{1,0:T(8,128)(2,1)S(1)}, bf16[512,256]{1,0:T(8,128)(2,1)S(1)}, u32[]{:S(2)}, u32[]{:S(2)}) collective-permute-start(bf16[512,256]{1,0:T(8,128)(2,1)S(1)} %copy-done.1), channel_id=1, source_target_pairs={{0,1},{1,0},{2,3},{3,2},{4,5},{5,4},{6,7},{7,6},{8,9},{9,8},{10,11... | collective-permute-start | bytes 786440 | tf_op jit(solution)/shard_map/ppermute | solution.py:333
  27.2 2.3 %collective-permute-start.3 = (bf16[512,256]{1,0:T(8,128)(2,1)S(1)}, bf16[512,256]{1,0:T(8,128)(2,1)S(1)}, u32[]{:S(2)}, u32[]{:S(2)}) collective-permute-start(bf16[512,256]{1,0:T(8,128)(2,1)S(1)} %copy-done.2), channel_id=1, source_target_pairs={{0,1},{1,0},{2,3},{3,2},{4,5},{5,4},{6,7},{7,6},{8,9},{9,8},{10,11... | collective-permute-start | bytes 786440 | tf_op jit(solution)/shard_map/ppermute | solution.py:333
  27.4 2.2 %collective-permute-start.1 = (bf16[256,256]{1,0:T(8,128)(2,1)S(1)}, bf16[256,256]{1,0:T(8,128)(2,1)S(1)}, u32[]{:S(2)}, u32[]{:S(2)}) collective-permute-start(bf16[256,256]{1,0:T(8,128)(2,1)S(1)} %bitcast.28), channel_id=1, source_target_pairs={{0,1},{1,0},{2,3},{3,2},{4,5},{5,4},{6,7},{7,6},{8,9},{9,8},{10,11... | collective-permute-start | bytes 393224 | tf_op jit(solution)/shard_map/ppermute | solution.py:333
  87.6 60.5 %copy-start = (bf16[4096,256]{1,0:T(8,128)(2,1)S(1)}, bf16[4096,256]{1,0:T(8,128)(2,1)}, u32[]{:S(2)}) copy-start(bf16[4096,256]{1,0:T(8,128)(2,1)} %refs_0_.1) | copy-start | bytes 6291460
  87.6 60.5 %copy-start.5 = (s32[192]{0:T(256)S(1)}, s32[192]{0:T(256)}, u32[]{:S(2)}) copy-start(s32[192]{0:T(256)} %slot_ref.3) | copy-start | bytes 2308
  87.6 60.5 %copy-start.6 = (s32[192]{0:T(256)S(1)}, s32[192]{0:T(256)}, u32[]{:S(2)}) copy-start(s32[192]{0:T(256)} %target_ref.1) | copy-start | bytes 2308
  87.7 60.4 %all-to-all-start.1 = ((bf16[128,64,256]{2,1,0:T(8,128)(2,1)}), bf16[128,64,256]{2,1,0:T(8,128)(2,1)}, u32[]{:S(2)}, u32[]{:S(2)}) async-start(bf16[128,64,256]{2,1,0:T(8,128)(2,1)} %get-tuple-element.15), calls=%async_computation.1 | async-start | bytes 8388608 | tf_op jit(solution)/shard_map/all_to_all | solution.py:380
  95.6 1.6 %collective-permute-start.5 = (bf16[256,256]{1,0:T(8,128)(2,1)S(1)}, bf16[256,256]{1,0:T(8,128)(2,1)S(1)}, u32[]{:S(2)}, u32[]{:S(2)}) collective-permute-start(bf16[256,256]{1,0:T(8,128)(2,1)S(1)} %get-tuple-element.17), channel_id=1, source_target_pairs={{0,1},{1,0},{2,3},{3,2},{4,5},{5,4},{6,7},{7,6},{8,9},{9,8},{10,11... | collective-permute-start | bytes 393224 | tf_op jit(solution)/shard_map/ppermute | solution.py:333
